TPU v7x, 32 devices: a whole 2x2x4 slice. The times are simulated.
32 devices in a mesh: grp: 4 (over y, core), dev: 8 (over z, x).
Axes of the slice: x: 2, y: 2, z: 4, core: 2. Of those that a mesh axis runs over, the one named last changes fastest.
Arguments:
- samples: int32 [128, 515, 1024], P(('grp', 'dev')), may hold values from -128 to 127
- taps: int32 [4, 1024], replicated, may hold values from -1024 to 1024
Outputs:
- gram: float32 [2, 512, 128, 128], P(None, ('grp', 'dev'))
All inputs are finite; a program needn't handle non-finite values.
Results may differ from a plain program's by a relative error of at most 0.0029.
Values may be sent and summed in bfloat16 or wider, within the bound.
No kernel may reach another device: no remote copies, remote signals or barrier semaphores. Data moves between devices by JAX's collectives and lax.ppermute only.
A program may use at most 128 MiB of HBM per device.

v0:
```python
import math

import jax
import jax.numpy as jnp
from jax import lax
from jax.sharding import PartitionSpec as P

P_SIZE = 32
Q = 32
CHAN = 512
TAPS = 4
SPECTRA = 512


gain_shift = 2.0 ** (-21)


def filter_bank(samples, taps):
    voltages = samples.astype(jnp.float32)
    weights = taps.astype(jnp.float32)
    filtered = weights[0][None, None, :] * voltages[:, 0:SPECTRA, :]
    for tap_index in range(1, TAPS):
        filtered = (
            filtered
            + weights[tap_index][None, None, :] * voltages[:, tap_index : tap_index + SPECTRA, :]
        )
    return filtered * gain_shift


def cross_terms(left_real, left_imag, right_real, right_imag):
    part_real = jnp.einsum(
        "cis,cjs->cij", left_real, right_real, preferred_element_type=jnp.float32
    ) + jnp.einsum("cis,cjs->cij", left_imag, right_imag, preferred_element_type=jnp.float32)
    part_imag = jnp.einsum(
        "cis,cjs->cij", left_imag, right_real, preferred_element_type=jnp.float32
    ) - jnp.einsum("cis,cjs->cij", left_real, right_imag, preferred_element_type=jnp.float32)
    return (part_real, part_imag)


def correlate_block(block):
    real_part = block[0, 0]
    imag_part = block[1, 0]
    gram_real, gram_imag = cross_terms(real_part, imag_part, real_part, imag_part)
    return jnp.stack([gram_real, gram_imag]) * (1.0 / SPECTRA)


def channelise(filtered):
    in_rows = filtered.shape[0]
    folded = filtered.reshape(in_rows, SPECTRA, P_SIZE, Q)
    first_index = jnp.arange(P_SIZE, dtype=jnp.float32)
    angle_one = 2.0 * math.pi / P_SIZE * first_index[:, None] * first_index[None, :]
    table_one = jnp.stack([jnp.cos(angle_one), -jnp.sin(angle_one)])
    section_one = jnp.einsum("ispq,rkp->rikqs", folded, table_one, precision=lax.Precision.HIGHEST)
    second_index = jnp.arange(Q, dtype=jnp.float32)
    phase = 2.0 * math.pi / (P_SIZE * Q) * first_index[:, None] * second_index[None, :]
    cos_twiddle = jnp.cos(phase)[None, :, :, None]
    sin_twiddle = jnp.sin(phase)[None, :, :, None]
    turned_real = section_one[0] * cos_twiddle + section_one[1] * sin_twiddle
    turned_imag = section_one[1] * cos_twiddle - section_one[0] * sin_twiddle
    turned = jnp.stack([turned_real, turned_imag])
    out_index = jnp.arange(Q // 2, dtype=jnp.float32)
    angle_three = 2.0 * math.pi / Q * out_index[:, None] * second_index[None, :]
    cos_three = jnp.cos(angle_three)
    sin_three = jnp.sin(angle_three)
    table_three = jnp.stack([jnp.stack([cos_three, sin_three]), jnp.stack([-sin_three, cos_three])])
    channels = jnp.einsum("uikqs,oumq->omkis", turned, table_three, precision=lax.Precision.HIGHEST)
    return channels.reshape(2, CHAN, in_rows, SPECTRA).astype(jnp.bfloat16)


def local(samples, taps):
    in_rows = samples.shape[0]
    channelised = channelise(filter_bank(samples, taps))
    groups = lax.axis_size("grp")
    members = lax.axis_size("dev")
    ch_dev = CHAN // (groups * members)
    parcel = channelised.reshape(2, groups * members, ch_dev, in_rows, SPECTRA)
    return correlate_block(
        lax.all_to_all(parcel, ("grp", "dev"), split_axis=1, concat_axis=3, tiled=True)
    )


def solution(mesh):
    in_specs = (P(("grp", "dev"), None, None), P())
    out_specs = P(None, ("grp", "dev"), None, None)
    return jax.shard_map(local, mesh=mesh, in_specs=in_specs, out_specs=out_specs, check_vma=False)
```

profile of v0, /device:TPU:0, one launch (start us, length us, event | category | flops | bytes accessed | tf_op | source)
XLA Modules:
  0.0 200.7 jit_solution(6811028159604737583)
XLA Ops:
  0.0 0.7 convert_element_type.16
  0.8 11.3 %copy.11 = s32[4,515,1024]{1,2,0:T(8,128)} copy(s32[4,515,1024]{2,0,1:T(4,128)} %param.2) | data formatting | bytes 16875520 | tf_op args[0]
  12.0 4.7 %convert_element_type.17 = f32[4,515,1024]{1,2,0:T(8,128)S(1)} convert(s32[4,515,1024]{1,2,0:T(8,128)} %copy.11) | non-fusion elementwise | flops 2109440 | bytes 16875520 | tf_op jit(solution)/shard_map/convert_element_type | solution.py:19
  16.7 0.1 fusion.48
  16.8 0.1 fusion.47
  16.9 0.1 fusion.49
  17.1 8.9 %fusion.4 = f32[4,512,1024]{1,2,0:T(8,128)} fusion(f32[4,515,1024]{1,2,0:T(8,128)S(1)} %convert_element_type.17, f32[1024]{0:T(1024)S(1)} %bitcast.58, f32[1024]{0:T(1024)S(1)} %bitcast.59, f32[1024]{0:T(1024)S(1)} %bitcast.60, f32[1024]{0:T(1024)S(1)} %bitcast.57), kind=kLoop, calls=%fused_computation.6 | loop fusion | flops 16777216 | bytes 41959424 | tf_op jit(solution)/shard_map/mul | solution.py:27
  26.0 25.3 %fusion.10 = f32[2,4,32,32,512]{4,2,3,1,0:T(8,128)S(1)} fusion(f32[4,512,32,32]{1,3,2,0:T(8,128)} %bitcast.48, f32[1,32,32]{2,1,0:T(8,128)S(1)} %get-tuple-element.21, f32[1,32,32]{2,1,0:T(8,128)S(1)} %get-tuple-element.20), kind=kOutput, calls=%fused_computation.18 | convolution fusion | flops 1610614784 | bytes 25174016 | tf_op jit(solution)/shard_map/ispq,rkp->rikqs/dot_general | solution.py:53
  51.3 7.3 %multiply_add_fusion = (f32[1,4,32,32,512]{4,2,3,1,0:T(8,128)}, f32[1,4,32,32,512]{4,2,3,1,0:T(8,128)}) fusion(f32[2,4,32,32,512]{4,2,3,1,0:T(8,128)S(1)} %fusion.10, f32[32,32]{0,1:T(8,128)S(1)} %get-tuple-element.19, f32[32,32]{0,1:T(8,128)S(1)} %get-tuple-element.18), kind=kLoop, calls=%fused_computation.17 | loop fusion | flops 12582912 | bytes 33562624 | tf_op jit(solution)/shard_map/add | solution.py:58
  58.6 7.0 %pad_maximum_fusion = f32[2,4,32,32,512]{4,2,3,1,0:T(8,128)S(1)} fusion(f32[1,4,32,32,512]{4,2,3,1,0:T(8,128)} %get-tuple-element.6, f32[1,4,32,32,512]{4,2,3,1,0:T(8,128)} %get-tuple-element.5), kind=kLoop, calls=%fused_computation | loop fusion | flops 4194304 | bytes 33554432 | tf_op jit(solution)/shard_map/stack | solution.py:60
  65.6 16.2 %fusion.13 = bf16[2,16,32,4,512]{4,1,2,3,0:T(8,128)(2,1)S(1)} fusion(f32[2,4,32,32,512]{4,2,3,1,0:T(8,128)S(1)} %pad_maximum_fusion, f32[1,2,16,32]{3,2,1,0:T(8,128)S(1)} %get-tuple-element.14, f32[1,2,16,32]{3,2,1,0:T(8,128)S(1)} %get-tuple-element.13), kind=kOutput, calls=%fused_computation.19 | convolution fusion | flops 1612711936 | bytes 20979712 | tf_op jit(solution)/shard_map/uikqs,oumq->omkis/dot_general | solution.py:66
  81.8 2.5 %copy.14 = bf16[2,16,32,4,512]{4,2,1,3,0:T(8,128)(2,1)S(1)} copy(bf16[2,16,32,4,512]{4,1,2,3,0:T(8,128)(2,1)S(1)} %fusion.13) | data formatting | bytes 8388608 | tf_op jit(solution)/shard_map/convert_element_type | solution.py:67
  84.4 0.6 copy.15
  85.0 102.3 %all_to_all.15 = bf16[2,32,16,4,512]{4,2,3,0,1:T(8,128)(2,1)S(1)} all-to-all(bf16[2,32,16,4,512]{4,2,3,0,1:T(8,128)(2,1)S(1)} %copy.15), channel_id=1, replica_groups=mesh['grp'=4,'dev'=8] {'grp','dev'}, dimensions={1} | all-to-all | bytes 8388608 | tf_op jit(solution)/shard_map/all_to_all | solution.py:78
  187.3 0.8 fusion.54
  188.2 2.3 %fusion.20 = f32[16,128,128]{2,1,0:T(8,128)S(1)} fusion(bf16[16,128,512]{2,0,1:T(8,128)(2,1)S(1)} %bitcast.54), kind=kOutput, calls=%fused_computation.25 | convolution fusion | flops 268435456 | bytes 3145728 | tf_op jit(solution)/shard_map/cis,cjs->cij/dot_general | solution.py:33
  190.5 2.3 %fusion.16 = f32[16,128,128]{2,1,0:T(8,128)S(1)} fusion(bf16[16,128,512]{2,0,1:T(8,128)(2,1)S(1)} %bitcast.55, bf16[16,128,512]{2,0,1:T(8,128)(2,1)S(1)} %bitcast.51), kind=kOutput, calls=%fused_computation.21 | convolution fusion | flops 268435456 | bytes 5242880 | tf_op jit(solution)/shard_map/cis,cjs->cij/dot_general | solution.py:36
  192.8 3.5 %fusion.29 = f32[1,16,128,128]{3,2,1,0:T(8,128)S(1)} fusion(f32[16,128,128]{2,1,0:T(8,128)S(1)} %fusion.20, bf16[16,128,512]{2,0,1:T(8,128)(2,1)S(1)} %bitcast.52), kind=kOutput, calls=%fused_computation.32 | convolution fusion | flops 268697600 | bytes 4194304 | tf_op jit(solution)/shard_map/cis,cjs->cij/dot_general | solution.py:31
  196.3 2.4 %fusion.37 = f32[1,16,128,128]{3,2,1,0:T(8,128)S(1)} fusion(f32[16,128,128]{2,1,0:T(8,128)S(1)} %fusion.16, bf16[16,128,512]{2,0,1:T(8,128)(2,1)S(1)} %bitcast.53, bf16[16,128,512]{2,0,1:T(8,128)(2,1)S(1)} %bitcast.56), kind=kOutput, calls=%fused_computation.34 | convolution fusion | flops 268697600 | bytes 6291456 | tf_op jit(solution)/shard_map/cis,cjs->cij/dot_general | solution.py:34
  198.7 1.5 maximum_multiply_fusion
  (5 shorter events, 0.0 us)
where the time goes:
time: 204 us; the launch traced here: 201 us
  blocking collectives  102 us (50%)
  matrix products  52.1 us (26%)
  other arithmetic  30.5 us (15%)
  local copies, waits for them, and re-layouts  15.3 us (8%)
    all_to_all x1, blocking collectives, local(): lax.all_to_all(parcel, ('grp', 'dev'), split_axis=1, concat_axis=3, tiled...  102 us
    dot_general x1, matrix products, channelise(): jnp.einsum('ispq,rkp->rikqs', folded, table_one, precision=lax.Precision....  25.3 us
    dot_general x1, matrix products, channelise(): jnp.einsum('uikqs,oumq->omkis', turned, table_three, precision=lax.Precis...  16.2 us
    unnamed x1, local copies, waits for them, and re-layouts  11.3 us
    mul x1, other arithmetic, filter_bank(): return filtered * gain_shift  8.92 us
    add x1, other arithmetic, channelise(): turned_real = section_one[0] * cos_twiddle + section_one[1] * sin_twiddle  7.29 us
    another operation x1, other arithmetic, channelise(): turned = jnp.stack([turned_real, turned_imag])  7 us
    convert_element_type x1, other arithmetic, filter_bank(): voltages = samples.astype(jnp.float32)  4.65 us

commit v1 on v0

v1 whole, which is shorter than its diff:
```python
import functools
import math

import jax
import jax.numpy as jnp
import numpy as np
from jax import lax
from jax.experimental import pallas as pl
from jax.experimental.pallas import tpu as pltpu
from jax.sharding import PartitionSpec as P

BRANCH = 1024
CHAN = 512
TAPS = 4
SPECTRA = 512
GAIN = 2.0**-21
ROWS = 8
BLOCK = 128


def radix_of(ch_dev):
    return 4 if 2 * ch_dev == 4 * ROWS else 1


def tables(devices, ch_dev):
    radix = radix_of(ch_dev)
    depth = BRANCH // radix
    n = np.arange(depth)
    per = ch_dev // radix
    mats = []
    for residue in range(radix):
        chan = radix * np.arange(CHAN // radix).reshape(devices, per) + residue
        angle = 2.0 * math.pi / BRANCH * ((chan[:, :, None] * n) % BRANCH)
        c, s = np.cos(angle), np.sin(angle)
        if residue == 1:
            re, im = np.concatenate([c, -s], -1), np.concatenate([-s, -c], -1)
        elif residue == 3:
            re, im = np.concatenate([c, s], -1), np.concatenate([-s, c], -1)
        else:
            re, im = c, -s
        mats.append(np.stack([re, im], 1).reshape(devices * 2 * per, -1) * GAIN)
    return mats


def split(x):
    hi = x.astype(jnp.bfloat16)
    return hi, (x - hi.astype(jnp.float32)).astype(jnp.bfloat16)


def split_np(m):
    hi = m.astype(np.float32).astype(jnp.bfloat16)
    return hi, (m - hi.astype(np.float64)).astype(np.float32).astype(jnp.bfloat16)


def product(w, f):
    return lax.dot_general(w, f, (((1,), (1,)), ((), ())), preferred_element_type=jnp.float32)


def filter_kernel(radix, x_ref, taps_ref, *refs):
    w_refs, o_ref, f_ref = refs[:-2], refs[-2], refs[-1]
    rows = o_ref.shape[1]
    taps = taps_ref[...].astype(jnp.float32)
    x = x_ref[...].astype(jnp.float32)
    f = taps[0] * x[0:BLOCK]
    for t in range(1, TAPS):
        f = f + taps[t] * x[t : t + BLOCK]
    f_ref[...] = f
    dests = o_ref.shape[0]
    q = BRANCH // radix
    for i in range(rows):
        fi = f_ref[:, i, :]
        if radix == 4:
            f0, f1, f2, f3 = (fi[:, a * q : (a + 1) * q] for a in range(4))
            even, odd = f0 + f2, f1 + f3
            delta = split(jnp.concatenate([f0 - f2, f1 - f3], 1))
            ops = [split(even + odd), delta, split(even - odd), delta]
        else:
            ops = [split(fi)]
        outs = []
        for r, (hi, lo) in enumerate(ops):
            w_hi, w_lo = w_refs[2 * r][...], w_refs[2 * r + 1][...]
            y = product(w_hi, hi) + (product(w_hi, lo) + product(w_lo, hi))
            outs.append(y.reshape(dests, ROWS, BLOCK))
        o_ref[:, i] = jnp.concatenate(outs, 1).astype(jnp.bfloat16)


def channelise(frames, taps, first, spectra, devices, ch_dev):
    rows = frames.shape[1]
    radix = radix_of(ch_dev)
    mats = [m for w in tables(devices, ch_dev) for m in split_np(w)]
    start = first
    return pl.pallas_call(
        functools.partial(filter_kernel, radix),
        out_shape=jax.ShapeDtypeStruct((devices, rows, 2 * ch_dev, spectra), jnp.bfloat16),
        grid=(spectra // BLOCK,),
        in_specs=[
            pl.BlockSpec(
                (pl.Element(BLOCK + TAPS - 1), pl.Element(rows), pl.Element(BRANCH)),
                lambda j: (start + j * BLOCK, 0, 0),
            ),
            pl.BlockSpec((TAPS, BRANCH), lambda j: (0, 0)),
        ]
        + [pl.BlockSpec(m.shape, lambda j: (0, 0)) for m in mats],
        out_specs=pl.BlockSpec((devices, rows, 2 * ch_dev, BLOCK), lambda j: (0, 0, 0, j)),
        scratch_shapes=[pltpu.VMEM((BLOCK, rows, BRANCH), jnp.float32)],
        compiler_params=pltpu.CompilerParams(vmem_limit_bytes=48 << 20),
        cost_estimate=pl.CostEstimate(flops=6 * spectra * rows * 393216, bytes_accessed=8 << 20, transcendentals=0),
    )(frames, taps, *[jnp.asarray(m) for m in mats])


def gram_kernel(ch_dev, radix, d_ref, p_ref, o_ref, z_ref):
    sources, rows = d_ref.shape[0], d_ref.shape[1]
    span = d_ref.shape[3]
    parts = 2 * ch_dev
    order = p_ref[...]
    for pair in range(sources // 2):
        block = d_ref[2 * pair : 2 * pair + 2].reshape(2 * rows * parts, span)
        turned = jnp.dot(order, block, preferred_element_type=jnp.float32)
        z_ref[:, 2 * rows * pair : 2 * rows * (pair + 1), :] = turned.reshape(parts, 2 * rows, span)
    inputs = sources * rows
    per = ch_dev // radix
    first = pl.program_id(0) == 0
    for c in range(ch_dev):
        at = (c % radix) * 2 * per + c // radix
        z = jnp.concatenate([z_ref[at], z_ref[at + per]], 0).astype(jnp.bfloat16)
        g = product(z, z)
        real = (g[:inputs, :inputs] + g[inputs:, inputs:]) * (1.0 / SPECTRA)
        imag = (g[inputs:, :inputs] - g[:inputs, inputs:]) * (1.0 / SPECTRA)

        @pl.when(first)
        def _():
            o_ref[0, c] = real
            o_ref[1, c] = imag

        @pl.when(jnp.logical_not(first))
        def _():
            o_ref[0, c] += real
            o_ref[1, c] += imag


def correlate(block, ch_dev):
    sources, rows, parts, spectra = block.shape
    radix = radix_of(ch_dev)
    inputs = sources * rows
    span = 256
    wide = 2 * rows * parts
    order = np.zeros((wide, wide), np.float32)
    for a in range(2 * rows):
        for b in range(parts):
            order[b * 2 * rows + a, a * parts + b] = 1.0
    return pl.pallas_call(
        functools.partial(gram_kernel, ch_dev, radix),
        out_shape=jax.ShapeDtypeStruct((2, ch_dev, inputs, inputs), jnp.float32),
        grid=(spectra // span,),
        in_specs=[
            pl.BlockSpec((sources, rows, parts, span), lambda j: (0, 0, 0, j)),
            pl.BlockSpec((wide, wide), lambda j: (0, 0)),
        ],
        out_specs=pl.BlockSpec((2, ch_dev, inputs, inputs), lambda j: (0, 0, 0, 0)),
        scratch_shapes=[pltpu.VMEM((parts, inputs, span), jnp.float32)],
        compiler_params=pltpu.CompilerParams(vmem_limit_bytes=48 << 20),
    )(block, jnp.asarray(order, jnp.bfloat16))


def local(samples, taps):
    groups = lax.axis_size("grp")
    members = lax.axis_size("dev")
    devices = groups * members
    ch_dev = CHAN // devices
    frames = jnp.transpose(samples, (1, 0, 2))
    parcel = channelise(frames, taps, 0, SPECTRA, devices, ch_dev)
    got = lax.all_to_all(parcel, ("grp", "dev"), split_axis=0, concat_axis=0, tiled=True)
    return correlate(got, ch_dev)


def solution(mesh):
    in_specs = (P(("grp", "dev"), None, None), P())
    out_specs = P(None, ("grp", "dev"), None, None)
    return jax.shard_map(local, mesh=mesh, in_specs=in_specs, out_specs=out_specs, check_vma=False)
```

time: 204 us -> 160 us (0.78); the launches traced: 201 us -> 160 us
  matrix products: 52.1 us -> 0 us
  Pallas kernels: 0 us -> 49.8 us
  other arithmetic: 30.5 us -> 0 us
  local copies, waits for them, and re-layouts: 15.3 us -> 8.14 us
    dot_general x6 -> x0, matrix products: 52.1 us -> none  [the longest x1 25.3 us: channelise(): jnp.einsum('ispq,rkp->rikqs', folded, table_one, precision=lax.Precision....]
    pallas_call x0 -> x2, Pallas kernels: none -> 49.8 us  [the longest x1 38.8 us: channelise(): pl.pallas_call(functools.partial(filter_kernel, radix), out_shape=jax.Sha...]
    mul x5 -> x0, other arithmetic: 10.5 us -> none  [the longest x1 8.92 us: filter_bank(): return filtered * gain_shift]
    add x1 -> x0, other arithmetic: 7.29 us -> none  [channelise(): turned_real = section_one[0] * cos_twiddle + section_one[1] * sin_twiddle]
    another operation x2 -> x0, other arithmetic: 7.01 us -> none  [the longest x1 7 us: channelise(): turned = jnp.stack([turned_real, turned_imag])]
    convert_element_type x2 -> x0, other arithmetic: 5.38 us -> none  [the longest x1 4.65 us: filter_bank(): voltages = samples.astype(jnp.float32)]
    convert_element_type x2 -> x0, local copies, waits for them, and re-layouts: 3.18 us -> none  [channelise(): return channels.reshape(2, CHAN, in_rows, SPECTRA).astype(jnp.bfloat16)]
    unnamed x1 -> x20, local copies, waits for them, and re-layouts: 11.3 us -> 8.14 us
where the time goes in v1:
time: 160 us
  blocking collectives  102 us (64%)
  Pallas kernels  49.8 us (31%)
  local copies, waits for them, and re-layouts  8.14 us (5%)
    all_to_all x1, blocking collectives, local(): lax.all_to_all(parcel, ('grp', 'dev'), split_axis=0, concat_axis=0, tiled...  102 us
    pallas_call x1, Pallas kernels, channelise(): pl.pallas_call(functools.partial(filter_kernel, radix), out_shape=jax.Sha...  38.8 us
    pallas_call x1, Pallas kernels, correlate(): pl.pallas_call(functools.partial(gram_kernel, ch_dev, radix), out_shape=j...  11.1 us
    unnamed x20, local copies, waits for them, and re-layouts  8.14 us

profile of v1, /device:TPU:0, one launch (start us, length us, event | category | flops | bytes accessed | tf_op | source)
XLA Modules:
  0.0 160.1 jit_solution(13258776438711339792)
XLA Ops:
  0.0 0.0 copy-start.1
  0.0 0.7 copy-done.1
  0.7 0.0 copy-start.2
  0.7 0.9 copy-done.2
  1.7 0.0 copy-start.3
  1.7 0.9 copy-done.3
  2.6 0.0 copy-start.4
  2.6 0.9 copy-done.4
  3.6 0.0 copy-start.5
  3.6 0.9 copy-done.5
  4.5 0.0 copy-start.6
  4.5 0.9 copy-done.6
  5.4 0.0 copy-start.7
  5.4 0.9 copy-done.7
  6.3 0.0 copy-start.8
  6.3 0.9 copy-done.8
  7.2 0.0 copy-start.9
  7.2 0.9 copy-done.9
  8.1 38.8 %shard_map.109 = bf16[32,4,32,512]{3,2,1,0:T(8,128)(2,1)S(1)} custom-call(s32[515,4,1024]{2,1,0:T(4,128)} %bitcast.1, s32[4,1024]{1,0:T(4,128)S(1)} %copy-done.1, bf16[256,256]{1,0:T(8,128)(2,1)S(1)} %copy-done.9, bf16[256,256]{1,0:T(8,128)(2,1)S(1)} %copy-done.8, bf16[256,512]{1,0:T(8,128)(2,1)S(1)} %copy-done.5, bf16[256,512]{1,0:T(8,128)(2,1)S(1)} %copy-done.4, ...), custom_call_target="tpu_custom_call" | custom-call | flops 4831838208 | bytes 8388608 | tf_op jit(solution)/shard_map/pallas_call | solution.py:92
  46.9 0.0 copy-start
  46.9 102.1 %all_to_all.5.d_ref = bf16[32,4,32,512]{3,2,1,0:T(8,128)(2,1)S(1)} all-to-all(bf16[32,4,32,512]{3,2,1,0:T(8,128)(2,1)S(1)} %shard_map.109), channel_id=1, replica_groups=mesh['grp'=4,'dev'=8] {'grp','dev'}, dimensions={0} | all-to-all | bytes 8388608 | tf_op jit(solution)/shard_map/all_to_all | solution.py:172
  149.0 0.0 copy-done
  149.1 11.1 %shard_map.110 = f32[2,16,128,128]{3,2,1,0:T(8,128)} custom-call(bf16[32,4,32,512]{3,2,1,0:T(8,128)(2,1)S(1)} %all_to_all.5.d_ref, bf16[256,256]{1,0:T(8,128)(2,1)S(1)} %copy-done), custom_call_target="tpu_custom_call" | custom-call | tf_op jit(solution)/shard_map/pallas_call | solution.py:151
Async XLA Ops:
  0.0 0.7 copy-start.1
  0.7 0.9 copy-start.2
  1.7 0.9 copy-start.3
  2.6 0.9 copy-start.4
  3.6 0.9 copy-start.5
  4.5 0.9 copy-start.6
  5.4 0.9 copy-start.7
  6.3 0.9 copy-start.8
  7.2 0.9 copy-start.9
  46.9 102.1 %copy-start = (bf16[256,256]{1,0:T(8,128)(2,1)S(1)}, bf16[256,256]{1,0:T(8,128)(2,1)}, u32[]{:S(2)}) copy-start(bf16[256,256]{1,0:T(8,128)(2,1)} %constant.26.clone.p_ref) | copy-start | bytes 393220

commit v2 on v0

v2 whole, which is shorter than its diff:
```python
import functools
import math

import jax
import jax.numpy as jnp
import numpy as np
from jax import lax
from jax.experimental import pallas as pl
from jax.experimental.pallas import tpu as pltpu
from jax.sharding import Mesh
from jax.sharding import PartitionSpec as P

BRANCH = 1024
CHAN = 512
TAPS = 4
SPECTRA = 512
GAIN = 2.0**-21
LANES = 128
TILES = BRANCH // LANES
ROWS = 8
BLOCK = 128
AHEAD = 2
STEP = 8
VMEM = 48 << 20

TERMS = {4: (((0, 0),), ((2, 1), (3, 2)), ((1, 3),), ((4, 1), (5, 2))), 1: (((0, 0),),)}


def radix_of(ch_dev):
    return 4 if 2 * ch_dev == 4 * ROWS else 1


def tables(groups, far, near, ch_dev):
    radix = radix_of(ch_dev)
    per = ch_dev // radix
    n = np.arange(BRANCH // radix)
    pieces = []
    for residue in (0, 2, 1, 3) if radix == 4 else (0,):
        chan = radix * np.arange(CHAN // radix).reshape(groups, far, near, per) + residue
        chan = chan.transpose(1, 0, 2, 3)[..., None]
        angle = 2.0 * math.pi / BRANCH * ((chan * n) % BRANCH)
        c, s = np.cos(angle), np.sin(angle)
        if residue == 1:
            pairs = [(c, -s), (-s, -c)]
        elif residue == 3:
            pairs = [(c, -s), (s, c)]
        else:
            pairs = [(c, -s)]
        for re, im in pairs:
            pieces.append(np.stack([re, im], 3).reshape(far, groups * near * 2 * per, -1))
    full = np.stack(pieces) * GAIN
    hi = full.astype(np.float32).astype(jnp.bfloat16)
    lo = (full - hi.astype(np.float64)).astype(np.float32).astype(jnp.bfloat16)
    return np.stack([hi, lo])


def split(x):
    hi = x.astype(jnp.bfloat16)
    return hi, (x - hi.astype(jnp.float32)).astype(jnp.bfloat16)


def product(w, f):
    return lax.dot_general(w, f, (((1,), (1,)), ((), ())), preferred_element_type=jnp.float32)


def filter_kernel(radix, rows, far, me_ref, x_ref, taps_ref, w_ref, *refs):
    outs, f_ref = refs[:-1], refs[-1]
    wide = TILES * rows

    def body(n, carry):
        at = pl.multiple_of(n * STEP, STEP)
        for h in range(0, wide, 8):
            x = x_ref[pl.ds(at, STEP + TAPS - 1), h : h + 8, :].astype(jnp.float32)
            w = taps_ref[:, h : h + 8, :]
            f = w[0] * x[0:STEP]
            for t in range(1, TAPS):
                f = f + w[t] * x[t : t + STEP]
            f_ref[pl.ds(at, STEP), h : h + 8, :] = f
        return carry

    lax.fori_loop(0, BLOCK // STEP, body, 0)
    stride = f_ref.shape[1]
    flat = f_ref.reshape(BLOCK * stride, LANES)
    tiles = TILES // radix
    me = me_ref[0]

    def weights(half, piece):
        return jnp.concatenate([w_ref[half, piece, jnp.bitwise_xor(me, k)] for k in range(far)], 0)

    for first in range(0, rows, 2):
        pair = (first, first + 1)

        def voltage(a):
            return jnp.concatenate(
                [
                    jnp.concatenate(
                        [flat[pl.ds((tiles * a + h) * rows + i, BLOCK, stride=stride), :] for h in range(tiles)], 1
                    )
                    for i in pair
                ],
                0,
            )

        if radix == 4:
            f0, f1, f2, f3 = (voltage(a) for a in range(4))
            even, odd = f0 + f2, f1 + f3
            ops = [split(even + odd), split(f0 - f2), split(f1 - f3), split(even - odd)]
        else:
            ops = [split(voltage(0))]
        sums = []
        for terms in TERMS[radix]:
            y = 0.0
            for piece, at in terms:
                hi, lo = ops[at]
                w_hi, w_lo = weights(0, piece), weights(1, piece)
                y = y + (product(w_hi, hi) + (product(w_hi, lo) + product(w_lo, hi)))
            sums.append(y)
        span = sums[0].shape[0] // far
        for k in range(far):
            for n, i in enumerate(pair):
                part = [
                    y[k * span : (k + 1) * span, n * BLOCK : (n + 1) * BLOCK].reshape(span // ROWS, ROWS, BLOCK)
                    for y in sums
                ]
                block = jnp.concatenate(part, 1).astype(jnp.bfloat16)
                if len(outs) > 1:
                    outs[k][:, i] = block
                else:
                    outs[0][:, 0, k, i] = block


def channelise(me, frames, taps, table, first, blocks, rows, near, ch_dev, apart):
    radix = radix_of(ch_dev)
    far = table.shape[2]
    parts = 2 * ch_dev
    wide = TILES * rows
    if apart:
        out_shape = [jax.ShapeDtypeStruct((near, rows, parts, BLOCK), jnp.bfloat16)] * far
        out_specs = [pl.BlockSpec((near, rows, parts, BLOCK), lambda j, me: (0, 0, 0, 0))] * far
    else:
        out_shape = jax.ShapeDtypeStruct((near, blocks, far, rows, parts, BLOCK), jnp.bfloat16)
        out_specs = pl.BlockSpec((near, 1, far, rows, parts, BLOCK), lambda j, me: (0, j, 0, 0, 0, 0))
    return pl.pallas_call(
        functools.partial(filter_kernel, radix, rows, far),
        out_shape=out_shape,
        grid_spec=pltpu.PrefetchScalarGridSpec(
            num_scalar_prefetch=1,
            grid=(blocks,),
            in_specs=[
                pl.BlockSpec(
                    (pl.Element(BLOCK + TAPS - 1), pl.Element(wide), pl.Element(LANES)),
                    lambda j, me: ((first + j) * BLOCK, 0, 0),
                ),
                pl.BlockSpec(taps.shape, lambda j, me: (0, 0, 0)),
                pl.BlockSpec(table.shape, lambda j, me: (0, 0, 0, 0, 0)),
            ],
            out_specs=out_specs,
            scratch_shapes=[pltpu.VMEM((BLOCK, wide + 8, LANES), jnp.float32)],
        ),
        compiler_params=pltpu.CompilerParams(vmem_limit_bytes=VMEM),
        cost_estimate=pl.CostEstimate(flops=blocks * 3 << 30, bytes_accessed=blocks * 4 << 20, transcendentals=0),
    )(me, frames, taps, table)


def gram_kernel(radix, ch_dev, rows, far, near_size, picks, more, me_ref, order_ref, *refs):
    z_ref, o_ref = refs[-1], refs[-2]
    arrays = refs[:-2]
    if more:
        before, arrays = arrays[0], arrays[1:]
    order = order_ref[...]
    parts = 2 * ch_dev
    both = near_size * rows
    me = me_ref[0]
    for n, pick in enumerate(picks):
        for k in range(far):
            low = pl.multiple_of(jnp.bitwise_xor(me, k) * both, both)
            view = pick(arrays, k)
            for g in range(view.shape[0] // near_size):
                block = view[g * near_size : (g + 1) * near_size].reshape(both * parts, BLOCK)
                turned = jnp.dot(order, block, preferred_element_type=jnp.float32)
                z_ref[:, pl.ds(g * far * both + low, both), n * BLOCK : (n + 1) * BLOCK] = turned.reshape(
                    parts, both, BLOCK
                )
    inputs = z_ref.shape[1]
    per = ch_dev // radix
    for c in range(ch_dev):
        at = (c % radix) * 2 * per + c // radix
        z = jnp.concatenate([z_ref[at], z_ref[at + per]], 0).astype(jnp.bfloat16)
        g = product(z, z)
        real = (g[:inputs, :inputs] + g[inputs:, inputs:]) * (1.0 / SPECTRA)
        imag = (g[inputs:, :inputs] - g[:inputs, inputs:]) * (1.0 / SPECTRA)
        if more:
            real, imag = before[0, c] + real, before[1, c] + imag
        o_ref[0, c] = real
        o_ref[1, c] = imag


def correlate(me, arrays, picks, before, rows, groups, far, near_size, ch_dev):
    parts = 2 * ch_dev
    both = near_size * rows
    wide = both * parts
    order = np.zeros((wide, wide), np.float32)
    for a in range(both):
        for b in range(parts):
            order[b * both + a, a * parts + b] = 1.0
    inputs = groups * far * both
    shape = (2, ch_dev, inputs, inputs)
    args = ([] if before is None else [before]) + list(arrays)
    vmem = pl.BlockSpec(memory_space=pltpu.VMEM)
    return pl.pallas_call(
        functools.partial(gram_kernel, radix_of(ch_dev), ch_dev, rows, far, near_size, picks, before is not None),
        out_shape=jax.ShapeDtypeStruct(shape, jnp.float32),
        in_specs=[pl.BlockSpec(memory_space=pltpu.SMEM)] + [vmem] * (1 + len(args)),
        out_specs=vmem,
        scratch_shapes=[pltpu.VMEM((parts, inputs, len(picks) * BLOCK), jnp.float32)],
        compiler_params=pltpu.CompilerParams(vmem_limit_bytes=VMEM),
        cost_estimate=pl.CostEstimate(flops=3 << 30, bytes_accessed=4 << 20, transcendentals=0),
    )(me, jnp.asarray(order, jnp.bfloat16), *args)


def local(samples, taps):
    rows = samples.shape[0]
    groups, far, near_size = lax.axis_size("grp"), lax.axis_size("far"), lax.axis_size("near")
    near = groups * near_size
    ch_dev = CHAN // (near * far)
    me = lax.axis_index("far").reshape(1)
    count = samples.shape[1]
    frames = samples.reshape(rows, count, TILES, LANES).transpose(1, 2, 0, 3).reshape(count, TILES * rows, LANES)
    weights = taps.astype(jnp.float32).reshape(TAPS, TILES, 1, LANES)
    weights = jnp.broadcast_to(weights, (TAPS, TILES, rows, LANES)).reshape(TAPS, TILES * rows, LANES)
    table = jnp.asarray(tables(groups, far, near_size, ch_dev))
    make = lambda first, blocks, apart: channelise(
        me, frames, weights, table, first, blocks, rows, near, ch_dev, apart
    )
    hops = [k for k in range(far - 1, 0, -1)]
    main = [k for k in hops if k >= far // 2]
    side = [k for k in hops if k < far // 2]
    pairs = lambda k: [(a, a ^ k) for a in range(far)]
    sent = []

    def send(x, k):
        if k in main:
            if len(sent) >= AHEAD:
                x, sent[-AHEAD] = lax.optimization_barrier((x, sent[-AHEAD]))
            sent.append(lax.ppermute(x, "far", pairs(k)))
            return len(sent) - 1
        return lax.ppermute(x, "far", pairs(k))

    def swap(x):
        return lax.all_to_all(x, ("grp", "near"), split_axis=0, concat_axis=0, tiled=True)

    early = [make(0, 1, True), make(1, 1, True)]
    got = []
    for parcel in early:
        got.append({k: send(parcel[k], k) for k in main + side})
    late = swap(make(2, 2, False))
    tail = []
    for n in range(2):
        tail.append({k: send(late[:, n, k], k) for k in main + side})
    arrived = lambda of, k: sent[of[k]] if k in main else of[k]
    first = jnp.stack(
        [
            jnp.stack([early[n][0] if k == 0 else arrived(got[n], k) for k in range(far)], 1)
            for n in range(2)
        ],
        1,
    )
    first = swap(first)
    head = correlate(
        me,
        [first],
        [lambda a, k, n=n: a[0].at[:, n, k] for n in range(2)],
        None,
        rows,
        groups,
        far,
        near_size,
        ch_dev,
    )
    last = [late[:, n, 0] if k == 0 else arrived(tail[n], k) for n in range(2) for k in range(far)]
    return correlate(
        me,
        last,
        [lambda a, k, n=n: a[n * far + k] for n in range(2)],
        head,
        rows,
        groups,
        far,
        near_size,
        ch_dev,
    )


def solution(mesh):
    groups, members = mesh.shape["grp"], mesh.shape["dev"]
    finer = Mesh(mesh.devices.reshape(groups, members // 2, 2), ("grp", "far", "near"))
    whole = ("grp", "far", "near")
    return jax.shard_map(
        local,
        mesh=finer,
        in_specs=(P(whole, None, None), P()),
        out_specs=P(None, whole, None, None),
        check_vma=False,
    )
```

time: 204 us -> 126 us (0.62)
  the two profiles are of different devices: /device:TPU:0 before, /device:TPU:10 now
where the time goes in v2:
time: 126 us
  waiting for transfers between devices  69.8 us (55%)
  starting transfers between devices  27 us (21%)
  Pallas kernels  22.3 us (18%)
  local copies, waits for them, and re-layouts  4.42 us (4%)
  other arithmetic  2.49 us (2%)
    ppermute x8, waiting for transfers between devices, send(): sent.append(lax.ppermute(x, 'far', pairs(k)))  69.7 us
    pallas_call x3, Pallas kernels, channelise(): pl.pallas_call(functools.partial(filter_kernel, radix, rows, far), out_sh...  15.3 us
    ppermute x8, starting transfers between devices, send(): sent.append(lax.ppermute(x, 'far', pairs(k)))  13.6 us
    all_to_all x2, starting transfers between devices, swap(): lax.all_to_all(x, ('grp', 'near'), split_axis=0, concat_axis=0, tiled=True)  9.24 us
    pallas_call x2, Pallas kernels, correlate(): pl.pallas_call(functools.partial(gram_kernel, radix_of(ch_dev), ch_dev, r...  7.04 us
    ppermute x4, starting transfers between devices, send(): return lax.ppermute(x, 'far', pairs(k))  4.11 us
    squeeze x1, local copies, waits for them, and re-layouts, local(): tail.append({k: send(late[:, n, k], k) for k in main + side})  2.99 us
  transfers between devices with their start and end apart: 14, of which 7 were waited for; matrix products, arithmetic and copies ran while one was open for 2% of the time, Pallas kernels for 8%

profile of v2, /device:TPU:10, one launch (start us, length us, event | category | flops | bytes accessed | tf_op | source)
XLA Modules:
  0.0 126.0 jit_solution(13350843780015507479)
XLA Ops:
  0.0 0.7 convert_bitcast_fusion
  0.7 0.0 copy-start
  0.8 1.4 %copy-done = bf16[2,6,4,64,256]{4,3,2,1,0:T(8,128)(2,1)S(1)} copy-done((bf16[2,6,4,64,256]{4,3,2,1,0:T(8,128)(2,1)S(1)}, bf16[2,6,4,64,256]{4,3,2,1,0:T(8,128)(2,1)}, u32[]{:S(2)}) %copy-start) | copy-done | bytes 1572888
  2.2 7.4 %shard_map.57 = bf16[8,2,4,4,32,128]{5,4,3,2,1,0:T(8,128)(2,1)} custom-call(s32[1]{0:T(128)} %bitcast.me_ref, s32[515,32,128]{2,1,0:T(8,128)} %bitcast.68, f32[4,32,128]{2,1,0:T(8,128)S(1)} %bitcast.58, bf16[2,6,4,64,256]{4,3,2,1,0:T(8,128)(2,1)S(1)} %copy-done), custom_call_target="tpu_custom_call" | custom-call | flops 6442450944 | bytes 8388608 | tf_op jit(solution)/shard_map/pallas_call | solution.py:143
  9.5 0.0 copy-start.1
  9.5 4.9 %all-to-all-start = ((bf16[8,2,4,4,32,128]{5,4,3,2,1,0:T(8,128)(2,1)}), bf16[8,2,4,4,32,128]{5,4,3,2,1,0:T(8,128)(2,1)}, u32[]{:S(2)}, u32[]{:S(2)}) async-start(bf16[8,2,4,4,32,128]{5,4,3,2,1,0:T(8,128)(2,1)} %shard_map.57), calls=%async_computation | async-start | bytes 4194304 | tf_op jit(solution)/shard_map/all_to_all | solution.py:250
  14.4 0.0 copy-done.1
  14.4 4.0 %shard_map.55 = (bf16[8,4,32,128]{3,2,1,0:T(8,128)(2,1)S(1)}, bf16[8,4,32,128]{3,2,1,0:T(8,128)(2,1)S(1)}, bf16[8,4,32,128]{3,2,1,0:T(8,128)(2,1)S(1)}, bf16[8,4,32,128]{3,2,1,0:T(8,128)(2,1)S(1)}) custom-call(s32[1]{0:T(128)} %bitcast.me_ref, s32[515,32,128]{2,1,0:T(8,128)} %bitcast.69, f32[4,32,128]{2,1,0:T(8,128)S(1)} %bitcast.59, ...), custom_call_target="tpu_custom_call" | custom-call | flops 3221225472 | bytes 4194304 | tf_op jit(solution)/shard_map/pallas_call | solution.py:143
  18.4 0.1 collective-permute-start
  18.5 3.0 %collective-permute-start.1 = (bf16[8,4,32,128]{3,2,1,0:T(8,128)(2,1)S(1)}, bf16[8,4,32,128]{3,2,1,0:T(8,128)(2,1)S(1)}, u32[]{:S(2)}, u32[]{:S(2)}) collective-permute-start(bf16[8,4,32,128]{3,2,1,0:T(8,128)(2,1)S(1)} %get-tuple-element.28), channel_id=1, source_target_pairs={{0,4},{2,6},{4,0},{6,2},{1,5},{3,7},{5,1},{7,3},{8,12},{10,14},{12... | collective-permute-start | bytes 786440 | tf_op jit(solution)/shard_map/ppermute | solution.py:245
  21.5 0.4 collective-permute-start.2
  21.9 4.0 %shard_map.56 = (bf16[8,4,32,128]{3,2,1,0:T(8,128)(2,1)S(1)}, bf16[8,4,32,128]{3,2,1,0:T(8,128)(2,1)S(1)}, bf16[8,4,32,128]{3,2,1,0:T(8,128)(2,1)S(1)}, bf16[8,4,32,128]{3,2,1,0:T(8,128)(2,1)S(1)}) custom-call(s32[1]{0:T(128)} %bitcast.me_ref, s32[515,32,128]{2,1,0:T(8,128)} %bitcast.70, f32[4,32,128]{2,1,0:T(8,128)S(1)} %bitcast.60, ...), custom_call_target="tpu_custom_call" | custom-call | flops 3221225472 | bytes 4194304 | tf_op jit(solution)/shard_map/pallas_call | solution.py:143
  25.9 1.2 collective-permute-start.3
  27.1 12.4 %collective-permute-done.1 = bf16[8,4,32,128]{3,2,1,0:T(8,128)(2,1)S(1)} collective-permute-done((bf16[8,4,32,128]{3,2,1,0:T(8,128)(2,1)S(1)}, bf16[8,4,32,128]{3,2,1,0:T(8,128)(2,1)S(1)}, u32[]{:S(2)}, u32[]{:S(2)}) %collective-permute-start.1) | collective-permute-done | bytes 262176 | tf_op jit(solution)/shard_map/ppermute | solution.py:245
  39.5 3.4 %collective-permute-start.4 = (bf16[8,4,32,128]{3,2,1,0:T(8,128)(2,1)S(1)}, bf16[8,4,32,128]{3,2,1,0:T(8,128)(2,1)S(1)}, u32[]{:S(2)}, u32[]{:S(2)}) collective-permute-start(bf16[8,4,32,128]{3,2,1,0:T(8,128)(2,1)S(1)} %get-tuple-element.35), channel_id=1, source_target_pairs={{0,4},{2,6},{4,0},{6,2},{1,5},{3,7},{5,1},{7,3},{8,12},{10,14},{12... | collective-permute-start | bytes 786440 | tf_op jit(solution)/shard_map/ppermute | solution.py:245
  42.9 14.4 %collective-permute-done.2 = bf16[8,4,32,128]{3,2,1,0:T(8,128)(2,1)S(1)} collective-permute-done((bf16[8,4,32,128]{3,2,1,0:T(8,128)(2,1)S(1)}, bf16[8,4,32,128]{3,2,1,0:T(8,128)(2,1)S(1)}, u32[]{:S(2)}, u32[]{:S(2)}) %collective-permute-start.2) | collective-permute-done | bytes 262176 | tf_op jit(solution)/shard_map/ppermute | solution.py:245
  57.2 1.6 %collective-permute-start.5 = (bf16[8,4,32,128]{3,2,1,0:T(8,128)(2,1)S(1)}, bf16[8,4,32,128]{3,2,1,0:T(8,128)(2,1)S(1)}, u32[]{:S(2)}, u32[]{:S(2)}) collective-permute-start(bf16[8,4,32,128]{3,2,1,0:T(8,128)(2,1)S(1)} %get-tuple-element.37), channel_id=1, source_target_pairs={{0,6},{2,4},{4,2},{6,0},{1,7},{3,5},{5,3},{7,1},{8,14},{10,12},{12... | collective-permute-start | bytes 786440 | tf_op jit(solution)/shard_map/ppermute | solution.py:245
  58.8 0.0 collective-permute-done
  58.8 0.1 maximum_bitcast_fusion
  59.0 0.0 all-to-all-done
  59.0 3.0 %slice_bitcast_fusion = (bf16[8,4,32,128]{3,2,1,0:T(8,128)(2,1)}, bf16[8,4,32,128]{3,2,1,0:T(8,128)(2,1)S(1)}, bf16[8,4,32,128]{3,2,1,0:T(8,128)(2,1)}, bf16[8,4...) fusion(bf16[8,2,4,4,32,128]{5,4,3,2,1,0:T(8,128)(2,1)} %all-to-, ...), kind=kLoop, calls=%fused_computation.3 | loop fusion | bytes 4194304 | tf_op jit(solution)/shard_map/squeeze | solution.py:259
  62.0 5.4 %collective-permute-done.5 = bf16[8,4,32,128]{3,2,1,0:T(8,128)(2,1)S(1)} collective-permute-done((bf16[8,4,32,128]{3,2,1,0:T(8,128)(2,1)S(1)}, bf16[8,4,32,128]{3,2,1,0:T(8,128)(2,1)S(1)}, u32[]{:S(2)}, u32[]{:S(2)}) %collective-permute-start.5) | collective-permute-done | bytes 262176 | tf_op jit(solution)/shard_map/ppermute | solution.py:245
  67.4 0.0 collective-permute-done.4
  67.4 0.0 collective-permute-done.3
  67.4 0.1 maximum_bitcast_fusion.1
  67.5 1.5 %pad_maximum_fusion = bf16[8,2,4,4,32,128]{5,4,3,2,1,0:T(8,128)(2,1)} fusion(bf16[8,1,4,4,32,128]{5,4,3,2,1,0:T(8,128)(2,1)S(1)} %maximum_bitcast_fusion.1, bf16[8,1,4,4,32,128]{5,4,3,2,1,0:T(8,128)(2,1)S(1)} %maximum_bitcast_fusion), kind=kLoop, calls=%fused_computation | loop fusion | flops 1048576 | bytes 4194304 | tf_op jit(solution)/shard_map/stack | solution.py:261
  69.0 0.0 copy-start.2
  69.0 4.4 %all-to-all-start.1 = ((bf16[8,2,4,4,32,128]{5,4,3,2,1,0:T(8,128)(2,1)}), bf16[8,2,4,4,32,128]{5,4,3,2,1,0:T(8,128)(2,1)S(1)}, u32[]{:S(2)}, u32[]{:S(2)}) async-start(bf16[8,2,4,4,32,128]{5,4,3,2,1,0:T(8,128)(2,1)} %pad_maximum_fusion), calls=%async_computation.1 | async-start | bytes 4194304 | tf_op jit(solution)/shard_map/all_to_all | solution.py:250
  73.4 0.0 collective-permute-start.7
  73.4 1.6 %collective-permute-start.8 = (bf16[8,4,32,128]{3,2,1,0:T(8,128)(2,1)}, bf16[8,4,32,128]{3,2,1,0:T(8,128)(2,1)S(1)}, u32[]{:S(2)}, u32[]{:S(2)}) collective-permute-start(bf16[8,4,32,128]{3,2,1,0:T(8,128)(2,1)} %get-tuple-element.41), channel_id=1, source_target_pairs={{0,6},{2,4},{4,2},{6,0},{1,7},{3,5},{5,3},{7,1},{8,14},{10,12},{12... | collective-permute-start | bytes 786440 | tf_op jit(solution)/shard_map/ppermute | solution.py:245
  75.0 2.8 %collective-permute-start.9 = (bf16[8,4,32,128]{3,2,1,0:T(8,128)(2,1)}, bf16[8,4,32,128]{3,2,1,0:T(8,128)(2,1)S(1)}, u32[]{:S(2)}, u32[]{:S(2)}) collective-permute-start(bf16[8,4,32,128]{3,2,1,0:T(8,128)(2,1)} %get-tuple-element.45), channel_id=1, source_target_pairs={{0,2},{2,0},{4,6},{6,4},{1,3},{3,1},{5,7},{7,5},{8,10},{10,8},{12,... | collective-permute-start | bytes 786440 | tf_op jit(solution)/shard_map/ppermute | solution.py:247
  77.8 0.0 collective-permute-start.6
  77.8 13.8 %collective-permute-done.7.refs_3_ = bf16[8,4,32,128]{3,2,1,0:T(8,128)(2,1)S(1)} collective-permute-done((bf16[8,4,32,128]{3,2,1,0:T(8,128)(2,1)}, bf16[8,4,32,128]{3,2,1,0:T(8,128)(2,1)S(1)}, u32[]{:S(2)}, u32[]{:S(2)}) %collective-permute-start.7) | collective-permute-done | bytes 262176 | tf_op jit(solution)/shard_map/ppermute | solution.py:245
  91.6 3.3 %collective-permute-start.10 = (bf16[8,4,32,128]{3,2,1,0:T(8,128)(2,1)}, bf16[8,4,32,128]{3,2,1,0:T(8,128)(2,1)}, u32[]{:S(2)}, u32[]{:S(2)}) collective-permute-start(bf16[8,4,32,128]{3,2,1,0:T(8,128)(2,1)} %get-tuple-element.43), channel_id=1, source_target_pairs={{0,4},{2,6},{4,0},{6,2},{1,5},{3,7},{5,1},{7,3},{8,12},{10,14},{12... | collective-permute-start | bytes 786440 | tf_op jit(solution)/shard_map/ppermute | solution.py:245
  94.9 4.4 %collective-permute-done.8.refs_4_ = bf16[8,4,32,128]{3,2,1,0:T(8,128)(2,1)S(1)} collective-permute-done((bf16[8,4,32,128]{3,2,1,0:T(8,128)(2,1)}, bf16[8,4,32,128]{3,2,1,0:T(8,128)(2,1)S(1)}, u32[]{:S(2)}, u32[]{:S(2)}) %collective-permute-start.8) | collective-permute-done | bytes 262176 | tf_op jit(solution)/shard_map/ppermute | solution.py:245
  99.3 0.3 collective-permute-start.11
  99.6 0.0 all-to-all-done.1.refs_0_
  99.6 0.0 copy-done.2
  99.6 2.3 %shard_map.58.refs_0_ = f32[2,16,128,128]{3,2,1,0:T(8,128)S(1)} custom-call(s32[1]{0:T(128)} %bitcast.me_ref, bf16[256,256]{1,0:T(8,128)(2,1)S(1)} %copy-done.2, bf16[8,2,4,4,32,128]{5,4,3,2,1,0:T(8,128)(2,1)S(1)} %all-to-all-done.1.refs_0_), custom_call_target="tpu_custom_call" | custom-call | flops 3221225472 | bytes 4194304 | tf_op jit(solution)/shard_map/pallas_call | solution.py:210
  101.9 0.0 collective-permute-done.9.refs_6_
  102.0 0.0 collective-permute-done.6.refs_2_
  102.0 12.2 %collective-permute-done.10.refs_7_ = bf16[8,4,32,128]{3,2,1,0:T(8,128)(2,1)} collective-permute-done((bf16[8,4,32,128]{3,2,1,0:T(8,128)(2,1)}, bf16[8,4,32,128]{3,2,1,0:T(8,128)(2,1)}, u32[]{:S(2)}, u32[]{:S(2)}) %collective-permute-start.10) | collective-permute-done | bytes 262176 | tf_op jit(solution)/shard_map/ppermute | solution.py:245
  114.1 7.2 %collective-permute-done.11.refs_8_ = bf16[8,4,32,128]{3,2,1,0:T(8,128)(2,1)} collective-permute-done((bf16[8,4,32,128]{3,2,1,0:T(8,128)(2,1)}, bf16[8,4,32,128]{3,2,1,0:T(8,128)(2,1)}, u32[]{:S(2)}, u32[]{:S(2)}) %collective-permute-start.11) | collective-permute-done | bytes 262176 | tf_op jit(solution)/shard_map/ppermute | solution.py:245
  121.3 4.7 %shard_map.59 = f32[2,16,128,128]{3,2,1,0:T(8,128)} custom-call(s32[1]{0:T(128)} %bitcast.me_ref, bf16[256,256]{1,0:T(8,128)(2,1)S(1)} %copy-done.2, f32[2,16,128,128]{3,2,1,0:T(8,128)S(1)} %shard_map.58.refs_0_, bf16[8,4,32,128]{3,2,1,0:T(8,128)(2,1)S(1)} %get-tuple-element.50.refs_1_, bf16[8,4,32,128]{3,2,1,0:T(8,128)(2,1)} %collective-permute-done.6.refs_2_, ...), custom_call_target="tpu_custom_call" | custom-call | flops 3221225472 | bytes 4194304 | tf_op jit(solution)/shard_map/pallas_call | solution.py:210
  (2 shorter events, 0.0 us)
Async XLA Ops:
  0.7 1.4 %copy-start = (bf16[2,6,4,64,256]{4,3,2,1,0:T(8,128)(2,1)S(1)}, bf16[2,6,4,64,256]{4,3,2,1,0:T(8,128)(2,1)}, u32[]{:S(2)}) copy-start(bf16[2,6,4,64,256]{4,3,2,1,0:T(8,128)(2,1)} %constant.10.clone.w_ref) | copy-start | bytes 4718596
  9.5 4.9 %copy-start.1 = (bf16[2,6,4,64,256]{4,3,2,1,0:T(8,128)(2,1)S(1)}, bf16[2,6,4,64,256]{4,3,2,1,0:T(8,128)(2,1)}, u32[]{:S(2)}) copy-start(bf16[2,6,4,64,256]{4,3,2,1,0:T(8,128)(2,1)} %constant.10.clone.w_ref) | copy-start | bytes 4718596
  9.5 49.4 %all-to-all-start = ((bf16[8,2,4,4,32,128]{5,4,3,2,1,0:T(8,128)(2,1)}), bf16[8,2,4,4,32,128]{5,4,3,2,1,0:T(8,128)(2,1)}, u32[]{:S(2)}, u32[]{:S(2)}) async-start(bf16[8,2,4,4,32,128]{5,4,3,2,1,0:T(8,128)(2,1)} %shard_map.57), calls=%async_computation | async-start | bytes 4194304 | tf_op jit(solution)/shard_map/all_to_all | solution.py:250
  18.4 40.4 %collective-permute-start = (bf16[8,4,32,128]{3,2,1,0:T(8,128)(2,1)S(1)}, bf16[8,4,32,128]{3,2,1,0:T(8,128)(2,1)S(1)}, u32[]{:S(2)}, u32[]{:S(2)}) collective-permute-start(bf16[8,4,32,128]{3,2,1,0:T(8,128)(2,1)S(1)} %get-tuple-element.26), channel_id=1, source_target_pairs={{0,2},{2,0},{4,6},{6,4},{1,3},{3,1},{5,7},{7,5},{8,10},{10,8},{12,... | collective-permute-start | bytes 786440 | tf_op jit(solution)/shard_map/ppermute | solution.py:247
  18.5 21.0 %collective-permute-start.1 = (bf16[8,4,32,128]{3,2,1,0:T(8,128)(2,1)S(1)}, bf16[8,4,32,128]{3,2,1,0:T(8,128)(2,1)S(1)}, u32[]{:S(2)}, u32[]{:S(2)}) collective-permute-start(bf16[8,4,32,128]{3,2,1,0:T(8,128)(2,1)S(1)} %get-tuple-element.28), channel_id=1, source_target_pairs={{0,4},{2,6},{4,0},{6,2},{1,5},{3,7},{5,1},{7,3},{8,12},{10,14},{12... | collective-permute-start | bytes 786440 | tf_op jit(solution)/shard_map/ppermute | solution.py:245
  21.5 35.7 %collective-permute-start.2 = (bf16[8,4,32,128]{3,2,1,0:T(8,128)(2,1)S(1)}, bf16[8,4,32,128]{3,2,1,0:T(8,128)(2,1)S(1)}, u32[]{:S(2)}, u32[]{:S(2)}) collective-permute-start(bf16[8,4,32,128]{3,2,1,0:T(8,128)(2,1)S(1)} %get-tuple-element.31), channel_id=1, source_target_pairs={{0,6},{2,4},{4,2},{6,0},{1,7},{3,5},{5,3},{7,1},{8,14},{10,12},{12... | collective-permute-start | bytes 786440 | tf_op jit(solution)/shard_map/ppermute | solution.py:245
  25.9 41.5 %collective-permute-start.3 = (bf16[8,4,32,128]{3,2,1,0:T(8,128)(2,1)S(1)}, bf16[8,4,32,128]{3,2,1,0:T(8,128)(2,1)S(1)}, u32[]{:S(2)}, u32[]{:S(2)}) collective-permute-start(bf16[8,4,32,128]{3,2,1,0:T(8,128)(2,1)S(1)} %get-tuple-element.34), channel_id=1, source_target_pairs={{0,2},{2,0},{4,6},{6,4},{1,3},{3,1},{5,7},{7,5},{8,10},{10,8},{12,... | collective-permute-start | bytes 786440 | tf_op jit(solution)/shard_map/ppermute | solution.py:247
  39.5 27.9 %collective-permute-start.4 = (bf16[8,4,32,128]{3,2,1,0:T(8,128)(2,1)S(1)}, bf16[8,4,32,128]{3,2,1,0:T(8,128)(2,1)S(1)}, u32[]{:S(2)}, u32[]{:S(2)}) collective-permute-start(bf16[8,4,32,128]{3,2,1,0:T(8,128)(2,1)S(1)} %get-tuple-element.35), channel_id=1, source_target_pairs={{0,4},{2,6},{4,0},{6,2},{1,5},{3,7},{5,1},{7,3},{8,12},{10,14},{12... | collective-permute-start | bytes 786440 | tf_op jit(solution)/shard_map/ppermute | solution.py:245
  57.2 10.2 %collective-permute-start.5 = (bf16[8,4,32,128]{3,2,1,0:T(8,128)(2,1)S(1)}, bf16[8,4,32,128]{3,2,1,0:T(8,128)(2,1)S(1)}, u32[]{:S(2)}, u32[]{:S(2)}) collective-permute-start(bf16[8,4,32,128]{3,2,1,0:T(8,128)(2,1)S(1)} %get-tuple-element.37), channel_id=1, source_target_pairs={{0,6},{2,4},{4,2},{6,0},{1,7},{3,5},{5,3},{7,1},{8,14},{10,12},{12... | collective-permute-start | bytes 786440 | tf_op jit(solution)/shard_map/ppermute | solution.py:245
  69.0 30.6 %copy-start.2 = (bf16[256,256]{1,0:T(8,128)(2,1)S(1)}, bf16[256,256]{1,0:T(8,128)(2,1)}, u32[]{:S(2)}) copy-start(bf16[256,256]{1,0:T(8,128)(2,1)} %constant.11.clone.order_ref) | copy-start | bytes 393220
  69.0 30.6 %all-to-all-start.1 = ((bf16[8,2,4,4,32,128]{5,4,3,2,1,0:T(8,128)(2,1)}), bf16[8,2,4,4,32,128]{5,4,3,2,1,0:T(8,128)(2,1)S(1)}, u32[]{:S(2)}, u32[]{:S(2)}) async-start(bf16[8,2,4,4,32,128]{5,4,3,2,1,0:T(8,128)(2,1)} %pad_maximum_fusion), calls=%async_computation.1 | async-start | bytes 4194304 | tf_op jit(solution)/shard_map/all_to_all | solution.py:250
  73.4 18.2 %collective-permute-start.7 = (bf16[8,4,32,128]{3,2,1,0:T(8,128)(2,1)}, bf16[8,4,32,128]{3,2,1,0:T(8,128)(2,1)S(1)}, u32[]{:S(2)}, u32[]{:S(2)}) collective-permute-start(bf16[8,4,32,128]{3,2,1,0:T(8,128)(2,1)} %get-tuple-element.39), channel_id=1, source_target_pairs={{0,4},{2,6},{4,0},{6,2},{1,5},{3,7},{5,1},{7,3},{8,12},{10,14},{12... | collective-permute-start | bytes 786440 | tf_op jit(solution)/shard_map/ppermute | solution.py:245
  73.4 25.9 %collective-permute-start.8 = (bf16[8,4,32,128]{3,2,1,0:T(8,128)(2,1)}, bf16[8,4,32,128]{3,2,1,0:T(8,128)(2,1)S(1)}, u32[]{:S(2)}, u32[]{:S(2)}) collective-permute-start(bf16[8,4,32,128]{3,2,1,0:T(8,128)(2,1)} %get-tuple-element.41), channel_id=1, source_target_pairs={{0,6},{2,4},{4,2},{6,0},{1,7},{3,5},{5,3},{7,1},{8,14},{10,12},{12... | collective-permute-start | bytes 786440 | tf_op jit(solution)/shard_map/ppermute | solution.py:245
  75.0 26.9 %collective-permute-start.9 = (bf16[8,4,32,128]{3,2,1,0:T(8,128)(2,1)}, bf16[8,4,32,128]{3,2,1,0:T(8,128)(2,1)S(1)}, u32[]{:S(2)}, u32[]{:S(2)}) collective-permute-start(bf16[8,4,32,128]{3,2,1,0:T(8,128)(2,1)} %get-tuple-element.45), channel_id=1, source_target_pairs={{0,2},{2,0},{4,6},{6,4},{1,3},{3,1},{5,7},{7,5},{8,10},{10,8},{12,... | collective-permute-start | bytes 786440 | tf_op jit(solution)/shard_map/ppermute | solution.py:247
  77.8 24.2 %collective-permute-start.6 = (bf16[8,4,32,128]{3,2,1,0:T(8,128)(2,1)}, bf16[8,4,32,128]{3,2,1,0:T(8,128)(2,1)}, u32[]{:S(2)}, u32[]{:S(2)}) collective-permute-start(bf16[8,4,32,128]{3,2,1,0:T(8,128)(2,1)} %get-tuple-element.49), channel_id=1, source_target_pairs={{0,2},{2,0},{4,6},{6,4},{1,3},{3,1},{5,7},{7,5},{8,10},{10,8},{12,... | collective-permute-start | bytes 786440 | tf_op jit(solution)/shard_map/ppermute | solution.py:247
  91.6 22.5 %collective-permute-start.10 = (bf16[8,4,32,128]{3,2,1,0:T(8,128)(2,1)}, bf16[8,4,32,128]{3,2,1,0:T(8,128)(2,1)}, u32[]{:S(2)}, u32[]{:S(2)}) collective-permute-start(bf16[8,4,32,128]{3,2,1,0:T(8,128)(2,1)} %get-tuple-element.43), channel_id=1, source_target_pairs={{0,4},{2,6},{4,0},{6,2},{1,5},{3,7},{5,1},{7,3},{8,12},{10,14},{12... | collective-permute-start | bytes 786440 | tf_op jit(solution)/shard_map/ppermute | solution.py:245
  99.3 22.0 %collective-permute-start.11 = (bf16[8,4,32,128]{3,2,1,0:T(8,128)(2,1)}, bf16[8,4,32,128]{3,2,1,0:T(8,128)(2,1)}, u32[]{:S(2)}, u32[]{:S(2)}) collective-permute-start(bf16[8,4,32,128]{3,2,1,0:T(8,128)(2,1)} %get-tuple-element.44), channel_id=1, source_target_pairs={{0,6},{2,4},{4,2},{6,0},{1,7},{3,5},{5,3},{7,1},{8,14},{10,12},{12... | collective-permute-start | bytes 786440 | tf_op jit(solution)/shard_map/ppermute | solution.py:245

commit v3 on v2

v3 whole, which is shorter than its diff:
```python
import functools
import math

import jax
import jax.numpy as jnp
import numpy as np
from jax import lax
from jax.experimental import pallas as pl
from jax.experimental.pallas import tpu as pltpu
from jax.sharding import Mesh
from jax.sharding import PartitionSpec as P

BRANCH = 1024
CHAN = 512
TAPS = 4
SPECTRA = 512
GAIN = 2.0**-21
LANES = 128
TILES = BRANCH // LANES
ROWS = 8
BLOCK = 128
EARLY = 1
HEAD_FLOPS = 5 * 10**10
STEP = 8
VMEM = 32 << 20
FILTER_VMEM = 56 << 20

TERMS = {4: (((0, 0),), ((2, 1), (3, 2)), ((1, 3),), ((4, 1), (5, 2))), 1: (((0, 0),),)}


def radix_of(ch_dev):
    return 4 if 2 * ch_dev == 4 * ROWS else 1


def tables(groups, far, near, ch_dev):
    radix = radix_of(ch_dev)
    per = ch_dev // radix
    n = np.arange(BRANCH // radix)
    pieces = []
    for residue in (0, 2, 1, 3) if radix == 4 else (0,):
        chan = radix * np.arange(CHAN // radix).reshape(groups, far, near, per) + residue
        chan = chan.transpose(1, 0, 2, 3)[..., None]
        angle = 2.0 * math.pi / BRANCH * ((chan * n) % BRANCH)
        c, s = np.cos(angle), np.sin(angle)
        if residue == 1:
            pairs = [(c, -s), (-s, -c)]
        elif residue == 3:
            pairs = [(c, -s), (s, c)]
        else:
            pairs = [(c, -s)]
        for re, im in pairs:
            pieces.append(np.stack([re, im], 3).reshape(far, groups * near * 2 * per, -1))
    full = np.stack(pieces) * GAIN
    hi = full.astype(np.float32).astype(jnp.bfloat16)
    lo = (full - hi.astype(np.float64)).astype(np.float32).astype(jnp.bfloat16)
    return np.stack([hi, lo])


def split(x):
    hi = x.astype(jnp.bfloat16)
    return hi, (x - hi.astype(jnp.float32)).astype(jnp.bfloat16)


def product(w, f):
    return lax.dot_general(w, f, (((1,), (1,)), ((), ())), preferred_element_type=jnp.float32)


def filter_kernel(radix, rows, far, apart, me_ref, x_ref, taps_ref, table_ref, *refs):
    outs, (f_ref, turn_ref, taps_f_ref, w_ref, sem) = refs[:-5], refs[-5:]
    wide = TILES * rows
    fetch = pltpu.make_async_copy(table_ref, w_ref, sem)

    @pl.when(pl.program_id(0) == 0)
    def _():
        fetch.start()
        for t in range(TAPS):
            for h in range(TILES):
                tap = taps_ref[t : t + 1, h * LANES : (h + 1) * LANES].astype(jnp.float32)
                taps_f_ref[t, h * rows : (h + 1) * rows, :] = jnp.broadcast_to(tap, (rows, LANES))

    def body(n, carry):
        at = pl.multiple_of(n * STEP, STEP)
        for h in range(0, wide, 8):
            x = x_ref[pl.ds(at, STEP + TAPS - 1), h : h + 8, :].astype(jnp.float32)
            w = taps_f_ref[:, h : h + 8, :]
            f = w[0] * x[0:STEP]
            for t in range(1, TAPS):
                f = f + w[t] * x[t : t + STEP]
            f_ref[pl.ds(at, STEP), h : h + 8, :] = f
        return carry

    lax.fori_loop(0, BLOCK // STEP, body, 0)

    @pl.when(pl.program_id(0) == 0)
    def _():
        fetch.wait()

    stride = f_ref.shape[1]
    flat = f_ref.reshape(BLOCK * stride, LANES)
    tiles = TILES // radix

    def weights(half, piece):
        return jnp.concatenate([w_ref[half, piece, jnp.bitwise_xor(me_ref[0], k)] for k in range(far)], 0)

    for first in range(0, rows, 2):
        pair = (first, first + 1)

        def voltage(a):
            return jnp.concatenate(
                [
                    jnp.concatenate(
                        [flat[pl.ds((tiles * a + h) * rows + i, BLOCK, stride=stride), :] for h in range(tiles)], 1
                    )
                    for i in pair
                ],
                0,
            )

        if radix == 4:
            f0, f1, f2, f3 = (voltage(a) for a in range(4))
            even, odd = f0 + f2, f1 + f3
            ops = [split(even + odd), split(f0 - f2), split(f1 - f3), split(even - odd)]
        else:
            ops = [split(voltage(0))]
        sums = []
        for terms in TERMS[radix]:
            y = 0.0
            for piece, at in terms:
                hi, lo = ops[at]
                w_hi, w_lo = weights(0, piece), weights(1, piece)
                y = y + (product(w_hi, hi) + (product(w_hi, lo) + product(w_lo, hi)))
            sums.append(y)
        span = sums[0].shape[0] // far
        for k in range(far):
            for n, i in enumerate(pair):
                part = [
                    y[k * span : (k + 1) * span, n * BLOCK : (n + 1) * BLOCK].reshape(span // ROWS, ROWS, BLOCK)
                    for y in sums
                ]
                block = jnp.concatenate(part, 1).astype(jnp.bfloat16)
                if apart:
                    turn_ref[k, i] = block
                    for r in range(block.shape[0]):
                        outs[k][r, i] = turn_ref[k, i, jnp.bitwise_xor(me_ref[1], r)]
                else:
                    groups, _, near_size = outs[0].shape[:3]
                    outs[0][:, k, :, 0, i] = block.reshape(groups, near_size, *block.shape[1:])


def channelise(me, frames, taps, table, first, blocks, rows, groups, near_size, ch_dev, apart):
    radix = radix_of(ch_dev)
    far = table.shape[2]
    near = groups * near_size
    parts = 2 * ch_dev
    wide = TILES * rows
    if apart:
        shape = (near, rows, parts, BLOCK)
        out_shape = [jax.ShapeDtypeStruct(shape, jnp.bfloat16)] * far
        out_specs = [pl.BlockSpec(shape, lambda j, me: (0, 0, 0, 0))] * far
    else:
        shape = (groups, far, near_size, blocks, rows, parts, BLOCK)
        out_shape = [jax.ShapeDtypeStruct(shape, jnp.bfloat16)]
        out_specs = [pl.BlockSpec(shape[:3] + (1,) + shape[4:], lambda j, me: (0, 0, 0, j, 0, 0, 0))]
    return pl.pallas_call(
        functools.partial(filter_kernel, radix, rows, far, apart),
        out_shape=out_shape,
        grid_spec=pltpu.PrefetchScalarGridSpec(
            num_scalar_prefetch=1,
            grid=(blocks,),
            in_specs=[
                pl.BlockSpec(
                    (pl.Element(BLOCK + TAPS - 1), pl.Element(wide), pl.Element(LANES)),
                    lambda j, me: ((first + j) * BLOCK, 0, 0),
                ),
                pl.BlockSpec(taps.shape, lambda j, me: (0, 0)),
                pl.BlockSpec(memory_space=pltpu.HBM),
            ],
            out_specs=out_specs,
            scratch_shapes=[
                pltpu.VMEM((BLOCK, wide + 8, LANES), jnp.float32),
                pltpu.VMEM((far, rows, near, parts, BLOCK), jnp.bfloat16),
                pltpu.VMEM((TAPS, wide, LANES), jnp.float32),
                pltpu.VMEM(table.shape, table.dtype),
                pltpu.SemaphoreType.DMA,
            ],
        ),
        compiler_params=pltpu.CompilerParams(vmem_limit_bytes=FILTER_VMEM),
        cost_estimate=pl.CostEstimate(flops=1, bytes_accessed=1, transcendentals=0),
    )(me, frames, taps, table)


def gram_kernel(radix, ch_dev, rows, groups, far, near_size, pick, blocks, more, me_ref, order_ref, *refs):
    z_ref, o_ref = refs[-1], refs[-2]
    arrays = refs[:-2]
    if more:
        before, arrays = arrays[0], arrays[1:]
    parts = 2 * ch_dev
    both = near_size * rows
    me_far, me_near = me_ref[0], me_ref[1]
    me_group = me_near // near_size
    order = order_ref[me_near % near_size]
    for n in range(blocks):
        for k in range(far):
            for g in range(groups):
                at = jnp.bitwise_xor(me_group, g) * far + jnp.bitwise_xor(me_far, k)
                block = jnp.concatenate(
                    [
                        pick(arrays, n, k, g * near_size + x)[...].reshape(rows * parts, BLOCK)
                        for x in range(near_size)
                    ],
                    0,
                )
                turned = jnp.dot(order, block, preferred_element_type=jnp.float32)
                z_ref[:, pl.ds(pl.multiple_of(at * both, both), both), n * BLOCK : (n + 1) * BLOCK] = turned.reshape(
                    parts, both, BLOCK
                )
    inputs = z_ref.shape[1]
    per = ch_dev // radix
    for c in range(ch_dev):
        at = (c % radix) * 2 * per + c // radix
        z = jnp.concatenate([z_ref[at], z_ref[at + per]], 0).astype(jnp.bfloat16)
        g = product(z, z)
        real = (g[:inputs, :inputs] + g[inputs:, inputs:]) * (1.0 / SPECTRA)
        imag = (g[inputs:, :inputs] - g[:inputs, inputs:]) * (1.0 / SPECTRA)
        if more:
            real, imag = before[0, c] + real, before[1, c] + imag
        o_ref[0, c] = real
        o_ref[1, c] = imag


def correlate(me, arrays, pick, blocks, before, flops, rows, groups, far, near_size, ch_dev):
    parts = 2 * ch_dev
    both = near_size * rows
    wide = both * parts
    order = np.zeros((near_size, wide, wide), np.float32)
    for flip in range(near_size):
        for x in range(near_size):
            for i in range(rows):
                for b in range(parts):
                    order[flip, b * both + x * rows + i, ((x ^ flip) * rows + i) * parts + b] = 1.0
    inputs = groups * far * both
    shape = (2, ch_dev, inputs, inputs)
    args = ([] if before is None else [before]) + list(arrays)
    vmem = pl.BlockSpec(memory_space=pltpu.VMEM)
    return pl.pallas_call(
        functools.partial(
            gram_kernel,
            radix_of(ch_dev),
            ch_dev,
            rows,
            groups,
            far,
            near_size,
            pick,
            blocks,
            before is not None,
        ),
        out_shape=jax.ShapeDtypeStruct(shape, jnp.float32),
        in_specs=[pl.BlockSpec(memory_space=pltpu.SMEM)] + [vmem] * (1 + len(args)),
        out_specs=vmem,
        scratch_shapes=[pltpu.VMEM((parts, inputs, blocks * BLOCK), jnp.float32)],
        compiler_params=pltpu.CompilerParams(vmem_limit_bytes=VMEM),
        cost_estimate=pl.CostEstimate(flops=flops, bytes_accessed=1, transcendentals=0),
    )(me, jnp.asarray(order, jnp.bfloat16), *args)


def local(samples, taps):
    rows, count = samples.shape[:2]
    groups, far, near_size = lax.axis_size("grp"), lax.axis_size("far"), lax.axis_size("near")
    near = groups * near_size
    ch_dev = CHAN // (near * far)
    me = jnp.stack([lax.axis_index("far"), lax.axis_index(("grp", "near"))]).astype(jnp.int32)
    origin = jnp.zeros((2,), jnp.int32)
    frames = samples.reshape(rows, count, TILES, LANES).transpose(1, 2, 0, 3).reshape(count, TILES * rows, LANES)
    table = jnp.asarray(tables(groups, far, near_size, ch_dev))
    sizes = (rows, groups, far, near_size, ch_dev)
    rest = SPECTRA // BLOCK - EARLY

    def cross(x, k):
        return lax.ppermute(x, "far", [(a, a ^ k) for a in range(far)])

    def swap(x, r):
        return lax.ppermute(x, ("grp", "near"), [(a, a ^ r) for a in range(near)])

    early = list(channelise(me, frames, taps, table, 0, 1, rows, groups, near_size, ch_dev, True))
    frames, early[0] = lax.optimization_barrier((frames, early[0]))
    (late,) = channelise(origin, frames, taps, table, EARLY, rest, rows, groups, near_size, ch_dev, False)
    late = late.reshape(groups * far * near_size, *late.shape[3:])
    late = lax.all_to_all(late, ("grp", "far", "near"), split_axis=0, concat_axis=0, tiled=True)
    crossed = {k: cross(early[k], k) for k in range(far - 1, 0, -1)}
    crossed[0] = early[0]
    parcel = [jnp.stack([crossed[k][r] for k in range(far)], 0) for r in range(near)]
    first = parcel[:1] + [swap(parcel[r], r) for r in range(1, near)]
    head = correlate(me, first, lambda a, n, k, r: a[r].at[k], 1, None, HEAD_FLOPS, *sizes)
    where = lambda k, r: ((r // near_size) * far + k) * near_size + r % near_size
    return correlate(origin, [late], lambda a, n, k, r: a[0].at[where(k, r), n], rest, head, 1, *sizes)


def solution(mesh):
    groups, members = mesh.shape["grp"], mesh.shape["dev"]
    finer = Mesh(mesh.devices.reshape(groups, members // 2, 2), ("grp", "far", "near"))
    whole = ("grp", "far", "near")
    return jax.shard_map(
        local,
        mesh=finer,
        in_specs=(P(whole, None, None), P()),
        out_specs=P(None, whole, None, None),
        check_vma=False,
    )
```

time: 126 us -> 111 us (0.88)
  the two profiles are of different devices: /device:TPU:10 before, /device:TPU:0 now
where the time goes in v3:
time: 111 us
  waiting for transfers between devices  59.7 us (54%)
  Pallas kernels  25.2 us (23%)
  starting transfers between devices  18 us (16%)
  local copies, waits for them, and re-layouts  7.08 us (6%)
    ppermute x7, waiting for transfers between devices, swap(): return lax.ppermute(x, ('grp', 'near'), [(a, a ^ r) for a in range(near)])  41.1 us
    all_to_all x1, waiting for transfers between devices, local(): lax.all_to_all(late, ('grp', 'far', 'near'), split_axis=0, concat_axis=0,...  18.6 us
    pallas_call x2, Pallas kernels, channelise(): pl.pallas_call(functools.partial(filter_kernel, radix, rows, far, apart),...  17.7 us
    pallas_call x2, Pallas kernels, correlate(): pl.pallas_call(functools.partial(gram_kernel, radix_of(ch_dev), ch_dev, r...  7.51 us
    ppermute x7, starting transfers between devices, swap(): return lax.ppermute(x, ('grp', 'near'), [(a, a ^ r) for a in range(near)])  6.27 us
    all_to_all x1, starting transfers between devices, local(): lax.all_to_all(late, ('grp', 'far', 'near'), split_axis=0, concat_axis=0,...  6.08 us
    ppermute x3, starting transfers between devices, cross(): return lax.ppermute(x, 'far', [(a, a ^ k) for a in range(far)])  5.68 us
    slice x4, local copies, waits for them, and re-layouts, local(): crossed[k][r]  3.62 us
  transfers between devices with their start and end apart: 11, of which 5 were waited for; matrix products, arithmetic and copies ran while one was open for 4% of the time, Pallas kernels for 12%

profile of v3, /device:TPU:0, one launch (start us, length us, event | category | flops | bytes accessed | tf_op | source)
XLA Modules:
  0.0 110.9 jit_solution(16679359855740603642)
XLA Ops:
  0.0 0.6 pad_add_fusion.me_ref
  0.6 6.4 %shard_map.55 = (bf16[8,4,32,128]{3,2,1,0:T(8,128)(2,1)}, bf16[8,4,32,128]{3,2,1,0:T(8,128)(2,1)}, bf16[8,4,32,128]{3,2,1,0:T(8,128)(2,1)}, bf16[8,4,32,128]{3,2,1,0:T(8,128)(2,1)}) custom-call(s32[2]{0:T(128)} %pad_add_fusion.me_ref, s32[515,32,128]{2,1,0:T(8,128)} %bitcast.8, s32[4,1024]{1,0:T(4,128)} %taps_ref.3, ...), custom_call_target="tpu_custom_call" | custom-call | flops 1 | bytes 1 | tf_op jit(solution)/shard_map/pallas_call | solution.py:164
  7.0 3.1 %collective-permute-start = (bf16[8,4,32,128]{3,2,1,0:T(8,128)(2,1)}, bf16[8,4,32,128]{3,2,1,0:T(8,128)(2,1)}, u32[]{:S(2)}, u32[]{:S(2)}) collective-permute-start(bf16[8,4,32,128]{3,2,1,0:T(8,128)(2,1)} %get-tuple-element.13), channel_id=1, source_target_pairs={{0,2},{2,0},{4,6},{6,4},{1,3},{3,1},{5,7},{7,5},{8,10},{10,8},{12,... | collective-permute-start | bytes 786440 | tf_op jit(solution)/shard_map/ppermute | solution.py:280
  10.1 2.6 %collective-permute-start.1 = (bf16[8,4,32,128]{3,2,1,0:T(8,128)(2,1)}, bf16[8,4,32,128]{3,2,1,0:T(8,128)(2,1)}, u32[]{:S(2)}, u32[]{:S(2)}) collective-permute-start(bf16[8,4,32,128]{3,2,1,0:T(8,128)(2,1)} %get-tuple-element.14), channel_id=1, source_target_pairs={{0,4},{2,6},{4,0},{6,2},{1,5},{3,7},{5,1},{7,3},{8,12},{10,14},{12... | collective-permute-start | bytes 786440 | tf_op jit(solution)/shard_map/ppermute | solution.py:280
  12.7 0.0 collective-permute-start.2
  12.7 0.5 broadcast_1_me_ref.2.me_ref
  13.2 11.3 %shard_map.57 = bf16[4,4,2,3,4,32,128]{6,5,4,3,2,1,0:T(8,128)(2,1)} custom-call(s32[2]{0:T(128)} %broadcast_1_me_ref.2.me_ref, s32[515,32,128]{2,1,0:T(8,128)} %bitcast.9, s32[4,1024]{1,0:T(4,128)} %taps_ref.3, bf16[2,6,4,64,256]{4,3,2,1,0:T(8,128)(2,1)} %constant.19.clone.table_ref), custom_call_target="tpu_custom_call" | custom-call | flops 1 | bytes 1 | tf_op jit(solution)/shard_map/pallas_call | solution.py:164
  24.6 6.1 %all-to-all-start = ((bf16[32,3,4,32,128]{4,3,2,1,0:T(8,128)(2,1)}), bf16[32,3,4,32,128]{4,3,2,1,0:T(8,128)(2,1)S(1)}, u32[]{:S(2)}, u32[]{:S(2)}) async-start(bf16[32,3,4,32,128]{4,3,2,1,0:T(8,128)(2,1)} %bitcast.10), calls=%async_computation | async-start | bytes 6291456 | tf_op jit(solution)/shard_map/all_to_all | solution.py:289
  30.7 0.0 copy-start.2
  30.7 0.0 copy-start.4
  30.7 0.9 fusion
  31.6 0.0 collective-permute-done
  31.6 0.9 fusion.1
  32.5 0.0 collective-permute-done.1
  32.5 0.9 fusion.2
  33.4 0.0 collective-permute-done.2
  33.5 0.9 fusion.3
  34.4 1.8 %collective-permute-start.3 = (bf16[4,4,32,128]{3,2,1,0:T(8,128)(2,1)S(1)}, bf16[4,4,32,128]{3,2,1,0:T(8,128)(2,1)S(1)}, u32[]{:S(2)}, u32[]{:S(2)}) collective-permute-start(bf16[4,4,32,128]{3,2,1,0:T(8,128)(2,1)S(1)} %pad_maximum_fusion.1), channel_id=1, source_target_pairs={{0,1},{1,0},{8,9},{9,8},{16,17},{17,16},{24,25},{25,24},{2,3},{3,2... | collective-permute-start | bytes 393224 | tf_op jit(solution)/shard_map/ppermute | solution.py:283
  36.2 0.1 collective-permute-start.4
  36.3 0.4 collective-permute-start.5
  36.8 1.8 %collective-permute-start.6 = (bf16[4,4,32,128]{3,2,1,0:T(8,128)(2,1)S(1)}, bf16[4,4,32,128]{3,2,1,0:T(8,128)(2,1)S(1)}, u32[]{:S(2)}, u32[]{:S(2)}) collective-permute-start(bf16[4,4,32,128]{3,2,1,0:T(8,128)(2,1)S(1)} %pad_maximum_fusion.4), channel_id=1, source_target_pairs={{0,16},{1,17},{8,24},{9,25},{16,0},{17,1},{24,8},{25,9},{2,18},{3,... | collective-permute-start | bytes 393224 | tf_op jit(solution)/shard_map/ppermute | solution.py:283
  38.6 1.5 %collective-permute-start.7 = (bf16[4,4,32,128]{3,2,1,0:T(8,128)(2,1)S(1)}, bf16[4,4,32,128]{3,2,1,0:T(8,128)(2,1)S(1)}, u32[]{:S(2)}, u32[]{:S(2)}) collective-permute-start(bf16[4,4,32,128]{3,2,1,0:T(8,128)(2,1)S(1)} %pad_maximum_fusion.5), channel_id=1, source_target_pairs={{0,17},{1,16},{8,25},{9,24},{16,1},{17,0},{24,9},{25,8},{2,19},{3,... | collective-permute-start | bytes 393224 | tf_op jit(solution)/shard_map/ppermute | solution.py:283
  40.2 27.1 %collective-permute-done.3.refs_1_ = bf16[4,4,32,128]{3,2,1,0:T(8,128)(2,1)S(1)} collective-permute-done((bf16[4,4,32,128]{3,2,1,0:T(8,128)(2,1)S(1)}, bf16[4,4,32,128]{3,2,1,0:T(8,128)(2,1)S(1)}, u32[]{:S(2)}, u32[]{:S(2)}) %collective-permute-start.3) | collective-permute-done | bytes 131104 | tf_op jit(solution)/shard_map/ppermute | solution.py:283
  67.3 0.0 collective-permute-start.8
  67.3 0.0 collective-permute-done.4.refs_2_
  67.3 0.6 collective-permute-start.9
  67.9 0.0 copy-start.3
  67.9 1.2 %collective-permute-done.5.refs_3_ = bf16[4,4,32,128]{3,2,1,0:T(8,128)(2,1)S(1)} collective-permute-done((bf16[4,4,32,128]{3,2,1,0:T(8,128)(2,1)S(1)}, bf16[4,4,32,128]{3,2,1,0:T(8,128)(2,1)S(1)}, u32[]{:S(2)}, u32[]{:S(2)}) %collective-permute-start.5) | collective-permute-done | bytes 131104 | tf_op jit(solution)/shard_map/ppermute | solution.py:283
  69.2 0.0 collective-permute-done.6.refs_4_
  69.2 6.4 %collective-permute-done.7.refs_5_ = bf16[4,4,32,128]{3,2,1,0:T(8,128)(2,1)S(1)} collective-permute-done((bf16[4,4,32,128]{3,2,1,0:T(8,128)(2,1)S(1)}, bf16[4,4,32,128]{3,2,1,0:T(8,128)(2,1)S(1)}, u32[]{:S(2)}, u32[]{:S(2)}) %collective-permute-start.7) | collective-permute-done | bytes 131104 | tf_op jit(solution)/shard_map/ppermute | solution.py:283
  75.6 6.4 %collective-permute-done.8.refs_6_ = bf16[4,4,32,128]{3,2,1,0:T(8,128)(2,1)S(1)} collective-permute-done((bf16[4,4,32,128]{3,2,1,0:T(8,128)(2,1)S(1)}, bf16[4,4,32,128]{3,2,1,0:T(8,128)(2,1)S(1)}, u32[]{:S(2)}, u32[]{:S(2)}) %collective-permute-start.8) | collective-permute-done | bytes 131104 | tf_op jit(solution)/shard_map/ppermute | solution.py:283
  81.9 0.0 collective-permute-done.9.refs_7_
  81.9 0.0 copy-done.2
  81.9 0.0 copy-done.4
  81.9 2.1 %shard_map.56.refs_0_ = f32[2,16,128,128]{3,2,1,0:T(8,128)S(1)} custom-call(s32[2]{0:T(128)S(1)} %copy-done.4, bf16[2,256,256]{2,1,0:T(8,128)(2,1)S(1)} %copy-done.2, bf16[4,4,32,128]{3,2,1,0:T(8,128)(2,1)S(1)} %pad_maximum_fusion.refs_0_, bf16[4,4,32,128]{3,2,1,0:T(8,128)(2,1)S(1)} %collective-permute-done.3.refs_1_, ...), custom_call_target="tpu_custom_call" | custom-call | flops 49999998976 | bytes 1 | tf_op jit(solution)/shard_map/pallas_call | solution.py:245
  84.0 0.0 copy-start
  84.0 1.3 %copy-done = f32[2,16,128,128]{3,2,1,0:T(8,128)} copy-done((f32[2,16,128,128]{3,2,1,0:T(8,128)}, f32[2,16,128,128]{3,2,1,0:T(8,128)S(1)}, u32[]{:S(2)}) %copy-start) | copy-done | bytes 2097176
  85.3 18.6 %all-to-all-done.refs_1_ = bf16[32,3,4,32,128]{4,3,2,1,0:T(8,128)(2,1)S(1)} async-done(((bf16[32,3,4,32,128]{4,3,2,1,0:T(8,128)(2,1)}), bf16[32,3,4,32,128]{4,3,2,1,0:T(8,128)(2,1)S(1)}, u32[]{:S(2)}, u32[]{:S(2)}) %all-to-all-start) | async-done | bytes 3145760 | tf_op jit(solution)/shard_map/all_to_all | solution.py:289
  103.9 0.0 copy-done.3
  103.9 0.0 copy-start.1
  103.9 1.6 %copy-done.1 = f32[2,16,128,128]{3,2,1,0:T(8,128)S(1)} copy-done((f32[2,16,128,128]{3,2,1,0:T(8,128)S(1)}, f32[2,16,128,128]{3,2,1,0:T(8,128)}, u32[]{:S(2)}) %copy-start.1) | copy-done | bytes 2097176
  105.5 5.4 %shard_map.58 = f32[2,16,128,128]{3,2,1,0:T(8,128)} custom-call(s32[2]{0:T(128)S(1)} %copy-done.3, bf16[2,256,256]{2,1,0:T(8,128)(2,1)S(1)} %copy-done.2, f32[2,16,128,128]{3,2,1,0:T(8,128)S(1)} %copy-done.1, bf16[32,3,4,32,128]{4,3,2,1,0:T(8,128)(2,1)S(1)} %all-to-all-done.refs_1_), custom_call_target="tpu_custom_call" | custom-call | flops 1 | bytes 1 | tf_op jit(solution)/shard_map/pallas_call | solution.py:245
  (8 shorter events, 0.2 us)
Async XLA Ops:
  7.0 24.6 %collective-permute-start = (bf16[8,4,32,128]{3,2,1,0:T(8,128)(2,1)}, bf16[8,4,32,128]{3,2,1,0:T(8,128)(2,1)}, u32[]{:S(2)}, u32[]{:S(2)}) collective-permute-start(bf16[8,4,32,128]{3,2,1,0:T(8,128)(2,1)} %get-tuple-element.13), channel_id=1, source_target_pairs={{0,2},{2,0},{4,6},{6,4},{1,3},{3,1},{5,7},{7,5},{8,10},{10,8},{12,... | collective-permute-start | bytes 786440 | tf_op jit(solution)/shard_map/ppermute | solution.py:280
  10.1 22.4 %collective-permute-start.1 = (bf16[8,4,32,128]{3,2,1,0:T(8,128)(2,1)}, bf16[8,4,32,128]{3,2,1,0:T(8,128)(2,1)}, u32[]{:S(2)}, u32[]{:S(2)}) collective-permute-start(bf16[8,4,32,128]{3,2,1,0:T(8,128)(2,1)} %get-tuple-element.14), channel_id=1, source_target_pairs={{0,4},{2,6},{4,0},{6,2},{1,5},{3,7},{5,1},{7,3},{8,12},{10,14},{12... | collective-permute-start | bytes 786440 | tf_op jit(solution)/shard_map/ppermute | solution.py:280
  12.7 20.7 %collective-permute-start.2 = (bf16[8,4,32,128]{3,2,1,0:T(8,128)(2,1)}, bf16[8,4,32,128]{3,2,1,0:T(8,128)(2,1)}, u32[]{:S(2)}, u32[]{:S(2)}) collective-permute-start(bf16[8,4,32,128]{3,2,1,0:T(8,128)(2,1)} %get-tuple-element.15), channel_id=1, source_target_pairs={{0,6},{2,4},{4,2},{6,0},{1,7},{3,5},{5,3},{7,1},{8,14},{10,12},{12... | collective-permute-start | bytes 786440 | tf_op jit(solution)/shard_map/ppermute | solution.py:280
  24.6 79.3 %all-to-all-start = ((bf16[32,3,4,32,128]{4,3,2,1,0:T(8,128)(2,1)}), bf16[32,3,4,32,128]{4,3,2,1,0:T(8,128)(2,1)S(1)}, u32[]{:S(2)}, u32[]{:S(2)}) async-start(bf16[32,3,4,32,128]{4,3,2,1,0:T(8,128)(2,1)} %bitcast.10), calls=%async_computation | async-start | bytes 6291456 | tf_op jit(solution)/shard_map/all_to_all | solution.py:289
  30.7 51.2 %copy-start.2 = (bf16[2,256,256]{2,1,0:T(8,128)(2,1)S(1)}, bf16[2,256,256]{2,1,0:T(8,128)(2,1)}, u32[]{:S(2)}) copy-start(bf16[2,256,256]{2,1,0:T(8,128)(2,1)} %constant.20.clone.order_ref) | copy-start | bytes 786436
  30.7 51.2 %copy-start.4 = (s32[2]{0:T(128)S(1)}, s32[2]{0:T(128)}, u32[]{:S(2)}) copy-start(s32[2]{0:T(128)} %pad_add_fusion.me_ref) | copy-start | bytes 28
  34.4 32.9 %collective-permute-start.3 = (bf16[4,4,32,128]{3,2,1,0:T(8,128)(2,1)S(1)}, bf16[4,4,32,128]{3,2,1,0:T(8,128)(2,1)S(1)}, u32[]{:S(2)}, u32[]{:S(2)}) collective-permute-start(bf16[4,4,32,128]{3,2,1,0:T(8,128)(2,1)S(1)} %pad_maximum_fusion.1), channel_id=1, source_target_pairs={{0,1},{1,0},{8,9},{9,8},{16,17},{17,16},{24,25},{25,24},{2,3},{3,2... | collective-permute-start | bytes 393224 | tf_op jit(solution)/shard_map/ppermute | solution.py:283
  36.2 31.1 %collective-permute-start.4 = (bf16[4,4,32,128]{3,2,1,0:T(8,128)(2,1)S(1)}, bf16[4,4,32,128]{3,2,1,0:T(8,128)(2,1)S(1)}, u32[]{:S(2)}, u32[]{:S(2)}) collective-permute-start(bf16[4,4,32,128]{3,2,1,0:T(8,128)(2,1)S(1)} %pad_maximum_fusion.2), channel_id=1, source_target_pairs={{0,8},{1,9},{8,0},{9,1},{16,24},{17,25},{24,16},{25,17},{2,10},{3,... | collective-permute-start | bytes 393224 | tf_op jit(solution)/shard_map/ppermute | solution.py:283
  36.3 32.8 %collective-permute-start.5 = (bf16[4,4,32,128]{3,2,1,0:T(8,128)(2,1)S(1)}, bf16[4,4,32,128]{3,2,1,0:T(8,128)(2,1)S(1)}, u32[]{:S(2)}, u32[]{:S(2)}) collective-permute-start(bf16[4,4,32,128]{3,2,1,0:T(8,128)(2,1)S(1)} %pad_maximum_fusion.3), channel_id=1, source_target_pairs={{0,9},{1,8},{8,1},{9,0},{16,25},{17,24},{24,17},{25,16},{2,11},{3,... | collective-permute-start | bytes 393224 | tf_op jit(solution)/shard_map/ppermute | solution.py:283
  36.8 32.4 %collective-permute-start.6 = (bf16[4,4,32,128]{3,2,1,0:T(8,128)(2,1)S(1)}, bf16[4,4,32,128]{3,2,1,0:T(8,128)(2,1)S(1)}, u32[]{:S(2)}, u32[]{:S(2)}) collective-permute-start(bf16[4,4,32,128]{3,2,1,0:T(8,128)(2,1)S(1)} %pad_maximum_fusion.4), channel_id=1, source_target_pairs={{0,16},{1,17},{8,24},{9,25},{16,0},{17,1},{24,8},{25,9},{2,18},{3,... | collective-permute-start | bytes 393224 | tf_op jit(solution)/shard_map/ppermute | solution.py:283
  38.6 36.9 %collective-permute-start.7 = (bf16[4,4,32,128]{3,2,1,0:T(8,128)(2,1)S(1)}, bf16[4,4,32,128]{3,2,1,0:T(8,128)(2,1)S(1)}, u32[]{:S(2)}, u32[]{:S(2)}) collective-permute-start(bf16[4,4,32,128]{3,2,1,0:T(8,128)(2,1)S(1)} %pad_maximum_fusion.5), channel_id=1, source_target_pairs={{0,17},{1,16},{8,25},{9,24},{16,1},{17,0},{24,9},{25,8},{2,19},{3,... | collective-permute-start | bytes 393224 | tf_op jit(solution)/shard_map/ppermute | solution.py:283
  67.3 14.6 %collective-permute-start.8 = (bf16[4,4,32,128]{3,2,1,0:T(8,128)(2,1)S(1)}, bf16[4,4,32,128]{3,2,1,0:T(8,128)(2,1)S(1)}, u32[]{:S(2)}, u32[]{:S(2)}) collective-permute-start(bf16[4,4,32,128]{3,2,1,0:T(8,128)(2,1)S(1)} %pad_maximum_fusion.6), channel_id=1, source_target_pairs={{0,24},{1,25},{8,16},{9,17},{16,8},{17,9},{24,0},{25,1},{2,26},{3,... | collective-permute-start | bytes 393224 | tf_op jit(solution)/shard_map/ppermute | solution.py:283
  67.3 14.6 %collective-permute-start.9 = (bf16[4,4,32,128]{3,2,1,0:T(8,128)(2,1)S(1)}, bf16[4,4,32,128]{3,2,1,0:T(8,128)(2,1)S(1)}, u32[]{:S(2)}, u32[]{:S(2)}) collective-permute-start(bf16[4,4,32,128]{3,2,1,0:T(8,128)(2,1)S(1)} %pad_maximum_fusion.7), channel_id=1, source_target_pairs={{0,25},{1,24},{8,17},{9,16},{16,9},{17,8},{24,1},{25,0},{2,27},{3,... | collective-permute-start | bytes 393224 | tf_op jit(solution)/shard_map/ppermute | solution.py:283
  67.9 36.0 %copy-start.3 = (s32[2]{0:T(128)S(1)}, s32[2]{0:T(128)}, u32[]{:S(2)}) copy-start(s32[2]{0:T(128)} %broadcast_1_me_ref.2.me_ref) | copy-start | bytes 28
  84.0 1.3 %copy-start = (f32[2,16,128,128]{3,2,1,0:T(8,128)}, f32[2,16,128,128]{3,2,1,0:T(8,128)S(1)}, u32[]{:S(2)}) copy-start(f32[2,16,128,128]{3,2,1,0:T(8,128)S(1)} %shard_map.56.refs_0_) | copy-start | bytes 6291460
  103.9 1.6 %copy-start.1 = (f32[2,16,128,128]{3,2,1,0:T(8,128)S(1)}, f32[2,16,128,128]{3,2,1,0:T(8,128)}, u32[]{:S(2)}) copy-start(f32[2,16,128,128]{3,2,1,0:T(8,128)} %copy-done) | copy-start | bytes 6291460

commit v4 on v3

v4 whole, which is shorter than its diff:
```python
import functools
import math

import jax
import jax.numpy as jnp
import numpy as np
from jax import lax
from jax.experimental import pallas as pl
from jax.experimental.pallas import tpu as pltpu
from jax.sharding import Mesh
from jax.sharding import PartitionSpec as P

BRANCH = 1024
CHAN = 512
TAPS = 4
SPECTRA = 512
GAIN = 2.0**-21
LANES = 128
TILES = BRANCH // LANES
ROWS = 8
BLOCK = 128
EARLY = 1
HEAD_FLOPS = 5 * 10**10
STEP = 8
PIECES = 4
HEAD_VMEM = 32 << 20
TAIL_VMEM = 50 << 20
FILTER_VMEM = 56 << 20

TERMS = {4: (((0, 0),), ((2, 1), (3, 2)), ((1, 3),), ((4, 1), (5, 2))), 1: (((0, 0),),)}


def radix_of(ch_dev):
    return 4 if 2 * ch_dev == 4 * ROWS else 1


def tables(groups, far, near, ch_dev):
    radix = radix_of(ch_dev)
    per = ch_dev // radix
    n = np.arange(BRANCH // radix)
    pieces = []
    for residue in (0, 2, 1, 3) if radix == 4 else (0,):
        chan = radix * np.arange(CHAN // radix).reshape(groups, far, near, per) + residue
        chan = chan.transpose(1, 0, 2, 3)[..., None]
        angle = 2.0 * math.pi / BRANCH * ((chan * n) % BRANCH)
        c, s = np.cos(angle), np.sin(angle)
        if residue == 1:
            pairs = [(c, -s), (-s, -c)]
        elif residue == 3:
            pairs = [(c, -s), (s, c)]
        else:
            pairs = [(c, -s)]
        for re, im in pairs:
            pieces.append(np.stack([re, im], 3).reshape(far, groups * near * 2 * per, -1))
    full = np.stack(pieces) * GAIN
    hi = full.astype(np.float32).astype(jnp.bfloat16)
    lo = (full - hi.astype(np.float64)).astype(np.float32).astype(jnp.bfloat16)
    return np.stack([hi, lo])


def split(x):
    hi = x.astype(jnp.bfloat16)
    return hi, (x - hi.astype(jnp.float32)).astype(jnp.bfloat16)


def product(w, f):
    return lax.dot_general(w, f, (((1,), (1,)), ((), ())), preferred_element_type=jnp.float32)


def filter_kernel(radix, rows, far, first, blocks, apart, x_ref, taps_ref, table_ref, *refs):
    outs, (f_ref, turn_ref, taps_f_ref, w_ref, held_ref, table_sem, x_sem) = refs[:-7], refs[-7:]
    wide = TILES * rows
    step = pl.program_id(0)
    slot = lax.rem(step, 2)
    size = BLOCK // PIECES
    table_copy = pltpu.make_async_copy(table_ref, w_ref, table_sem)

    def fetch(step, slot, piece):
        low, high = (piece * size + TAPS - 1 if piece else 0), (piece + 1) * size + TAPS - 1
        return pltpu.make_async_copy(
            x_ref.at[pl.ds((first + step) * BLOCK + low, high - low)],
            held_ref.at[slot, low:high],
            x_sem.at[slot, piece],
        )

    @pl.when(step == 0)
    def _():
        for piece in range(PIECES):
            fetch(step, slot, piece).start()
        table_copy.start()
        for t in range(TAPS):
            for h in range(TILES):
                tap = taps_ref[t : t + 1, h * LANES : (h + 1) * LANES].astype(jnp.float32)
                taps_f_ref[t, h * rows : (h + 1) * rows, :] = jnp.broadcast_to(tap, (rows, LANES))

    @pl.when(step + 1 < blocks)
    def _():
        for piece in range(PIECES):
            fetch(step + 1, 1 - slot, piece).start()

    def body(n, carry):
        at = pl.multiple_of(n * STEP, STEP)
        for h in range(0, wide, 8):
            x = held_ref[slot, pl.ds(at, STEP + TAPS - 1), h : h + 8, :].astype(jnp.float32)
            w = taps_f_ref[:, h : h + 8, :]
            f = w[0] * x[0:STEP]
            for t in range(1, TAPS):
                f = f + w[t] * x[t : t + STEP]
            f_ref[pl.ds(at, STEP), h : h + 8, :] = f
        return carry

    for piece in range(PIECES):
        fetch(step, slot, piece).wait()
        lax.fori_loop(piece * size // STEP, (piece + 1) * size // STEP, body, 0)

    @pl.when(step == 0)
    def _():
        table_copy.wait()

    me_far, me_near = (lax.axis_index("far"), lax.axis_index(("grp", "near"))) if apart else (0, 0)
    stride = f_ref.shape[1]
    flat = f_ref.reshape(BLOCK * stride, LANES)
    tiles = TILES // radix

    def weights(half, piece):
        return jnp.concatenate([w_ref[half, piece, me_far ^ k] for k in range(far)], 0)

    for first in range(0, rows, 2):
        pair = (first, first + 1)

        def voltage(a):
            return jnp.concatenate(
                [
                    jnp.concatenate(
                        [flat[pl.ds((tiles * a + h) * rows + i, BLOCK, stride=stride), :] for h in range(tiles)], 1
                    )
                    for i in pair
                ],
                0,
            )

        if radix == 4:
            f0, f1, f2, f3 = (voltage(a) for a in range(4))
            even, odd = f0 + f2, f1 + f3
            ops = [split(even + odd), split(f0 - f2), split(f1 - f3), split(even - odd)]
        else:
            ops = [split(voltage(0))]
        sums = []
        for terms in TERMS[radix]:
            y = 0.0
            for piece, at in terms:
                hi, lo = ops[at]
                w_hi, w_lo = weights(0, piece), weights(1, piece)
                y = y + (product(w_hi, hi) + (product(w_hi, lo) + product(w_lo, hi)))
            sums.append(y)
        span = sums[0].shape[0] // far
        for k in range(far):
            for n, i in enumerate(pair):
                part = [
                    y[k * span : (k + 1) * span, n * BLOCK : (n + 1) * BLOCK].reshape(span // ROWS, ROWS, BLOCK)
                    for y in sums
                ]
                block = jnp.concatenate(part, 1).astype(jnp.bfloat16)
                if apart:
                    turn_ref[k, i] = block
                    for r in range(block.shape[0]):
                        outs[k][r, i] = turn_ref[k, i, me_near ^ r]
                else:
                    groups, _, near_size = outs[0].shape[:3]
                    outs[0][:, k, :, 0, i] = block.reshape(groups, near_size, *block.shape[1:])


def channelise(frames, taps, table, first, blocks, rows, groups, near_size, ch_dev, apart):
    radix = radix_of(ch_dev)
    far = table.shape[2]
    near = groups * near_size
    parts = 2 * ch_dev
    wide = TILES * rows
    if apart:
        shape = (near, rows, parts, BLOCK)
        out_shape = [jax.ShapeDtypeStruct(shape, jnp.bfloat16)] * far
        out_specs = [pl.BlockSpec(shape, lambda j: (0, 0, 0, 0))] * far
    else:
        shape = (groups, far, near_size, blocks, rows, parts, BLOCK)
        out_shape = [jax.ShapeDtypeStruct(shape, jnp.bfloat16)]
        out_specs = [pl.BlockSpec(shape[:3] + (1,) + shape[4:], lambda j: (0, 0, 0, j, 0, 0, 0))]
    return pl.pallas_call(
        functools.partial(filter_kernel, radix, rows, far, first, blocks, apart),
        out_shape=out_shape,
        grid=(blocks,),
        in_specs=[
            pl.BlockSpec(memory_space=pltpu.HBM),
            pl.BlockSpec(taps.shape, lambda j: (0, 0)),
            pl.BlockSpec(memory_space=pltpu.HBM),
        ],
        out_specs=out_specs,
        scratch_shapes=[
            pltpu.VMEM((BLOCK, wide + 8, LANES), jnp.float32),
            pltpu.VMEM((far, rows, near, parts, BLOCK), jnp.bfloat16),
            pltpu.VMEM((TAPS, wide, LANES), jnp.float32),
            pltpu.VMEM(table.shape, table.dtype),
            pltpu.VMEM((2, BLOCK + TAPS - 1, wide, LANES), jnp.int32),
            pltpu.SemaphoreType.DMA,
            pltpu.SemaphoreType.DMA((2, PIECES)),
        ],
        compiler_params=pltpu.CompilerParams(vmem_limit_bytes=FILTER_VMEM),
        cost_estimate=pl.CostEstimate(flops=1, bytes_accessed=1, transcendentals=0),
    )(frames, taps, table)


def gram_kernel(radix, ch_dev, rows, groups, far, near_size, pick, blocks, fixed, more, order_ref, *refs):
    arrays, (o_ref, z_ref, out_ref, old_ref, old_sem, out_sem) = refs[:-6], refs[-6:]
    parts = 2 * ch_dev
    both = near_size * rows
    if more:
        before, arrays = arrays[0], arrays[1:]
        fetch = pltpu.make_async_copy(before, old_ref, old_sem)
        fetch.start()
    if fixed:
        me_far, me_group, me_side = 0, 0, 0
    else:
        me_near = lax.axis_index(("grp", "near"))
        me_far, me_group, me_side = lax.axis_index("far"), me_near // near_size, me_near % near_size
    order = order_ref[me_side]
    wide = 2 if fixed and far % 2 == 0 else 1
    for g in range(groups):
        for k in range(0, far, wide):
            at = (me_group ^ g) * far + (me_far ^ k)
            turned = []
            for w in range(wide):
                block = jnp.concatenate(
                    [
                        jnp.concatenate(
                            [
                                pick(arrays, n, k + w, g * near_size + x)[...].reshape(rows * parts, BLOCK)
                                for x in range(near_size)
                            ],
                            0,
                        )
                        for n in range(blocks)
                    ],
                    1,
                )
                y = jnp.dot(order, block, preferred_element_type=jnp.float32)
                turned.append(y.reshape(parts, both, blocks * BLOCK))
            low = at * both if fixed else pl.multiple_of(at * both, both)
            z_ref[:, pl.ds(low, wide * both), :] = jnp.concatenate(turned, 1).astype(z_ref.dtype)
    inputs = z_ref.shape[1]
    per = ch_dev // radix
    if more:
        fetch.wait()
    copies = []
    for c in range(ch_dev):
        at = (c % radix) * 2 * per + c // radix
        z = jnp.concatenate([z_ref[at], z_ref[at + per]], 0).astype(jnp.bfloat16)
        g = product(z, z)
        real = (g[:inputs, :inputs] + g[inputs:, inputs:]) * (1.0 / SPECTRA)
        imag = (g[inputs:, :inputs] - g[:inputs, inputs:]) * (1.0 / SPECTRA)
        if more:
            real, imag = old_ref[0, c] + real, old_ref[1, c] + imag
        out_ref[0, c] = real
        out_ref[1, c] = imag
        if (c + 1) % radix == 0:
            group = pl.ds(c + 1 - radix, radix)
            copies.append(
                pltpu.make_async_copy(out_ref.at[:, group], o_ref.at[:, group], out_sem.at[c // radix])
            )
            copies[-1].start()
    for copy in copies:
        copy.wait()


def correlate(arrays, pick, blocks, before, fixed, flops, rows, groups, far, near_size, ch_dev):
    parts = 2 * ch_dev
    both = near_size * rows
    wide = both * parts
    order = np.zeros((near_size, wide, wide), np.float32)
    for flip in range(near_size):
        for x in range(near_size):
            for i in range(rows):
                for b in range(parts):
                    order[flip, b * both + x * rows + i, ((x ^ flip) * rows + i) * parts + b] = 1.0
    inputs = groups * far * both
    shape = (2, ch_dev, inputs, inputs)
    vmem, hbm = pl.BlockSpec(memory_space=pltpu.VMEM), pl.BlockSpec(memory_space=pltpu.HBM)
    more = before is not None
    radix = radix_of(ch_dev)
    return pl.pallas_call(
        functools.partial(
            gram_kernel, radix, ch_dev, rows, groups, far, near_size, pick, blocks, fixed, more
        ),
        out_shape=jax.ShapeDtypeStruct(shape, jnp.float32),
        in_specs=[vmem] + [hbm] * more + [vmem] * len(arrays),
        out_specs=hbm,
        scratch_shapes=[
            pltpu.VMEM((parts, inputs, blocks * BLOCK), jnp.bfloat16 if fixed else jnp.float32),
            pltpu.VMEM(shape, jnp.float32),
            pltpu.VMEM(shape if more else (8, LANES), jnp.float32),
            pltpu.SemaphoreType.DMA,
            pltpu.SemaphoreType.DMA((ch_dev // radix,)),
        ],
        compiler_params=pltpu.CompilerParams(vmem_limit_bytes=TAIL_VMEM if more else HEAD_VMEM),
        cost_estimate=pl.CostEstimate(flops=flops, bytes_accessed=1, transcendentals=0),
    )(jnp.asarray(order, jnp.bfloat16), *([before] if more else []), *arrays)


def local(samples, taps):
    rows, count = samples.shape[:2]
    groups, far, near_size = lax.axis_size("grp"), lax.axis_size("far"), lax.axis_size("near")
    near = groups * near_size
    ch_dev = CHAN // (near * far)
    frames = samples.reshape(rows, count, TILES, LANES).transpose(1, 2, 0, 3).reshape(count, TILES * rows, LANES)
    table = jnp.asarray(tables(groups, far, near_size, ch_dev))
    sizes = (rows, groups, far, near_size, ch_dev)
    rest = SPECTRA // BLOCK - EARLY

    def cross(x, k):
        return lax.ppermute(x, "far", [(a, a ^ k) for a in range(far)])

    def swap(x, r):
        return lax.ppermute(x, ("grp", "near"), [(a, a ^ r) for a in range(near)])

    early = list(channelise(frames, taps, table, 0, 1, rows, groups, near_size, ch_dev, True))
    frames, early[0] = lax.optimization_barrier((frames, early[0]))
    (late,) = channelise(frames, taps, table, EARLY, rest, rows, groups, near_size, ch_dev, False)
    late = late.reshape(groups * far * near_size, *late.shape[3:])
    late = lax.all_to_all(late, ("grp", "far", "near"), split_axis=0, concat_axis=0, tiled=True)
    crossed = {k: cross(early[k], k) for k in range(far - 1, 0, -1)}
    crossed[0] = early[0]
    parcel = [jnp.stack([crossed[k][r] for k in range(far)], 0) for r in range(near)]
    first = parcel[:1] + [swap(parcel[r], r) for r in range(1, near)]
    head = correlate(first, lambda a, n, k, r: a[r].at[k], 1, None, False, HEAD_FLOPS, *sizes)
    where = lambda k, r: ((r // near_size) * far + k) * near_size + r % near_size
    return correlate([late], lambda a, n, k, r: a[0].at[where(k, r), n], rest, head, True, 1, *sizes)


def solution(mesh):
    groups, members = mesh.shape["grp"], mesh.shape["dev"]
    finer = Mesh(mesh.devices.reshape(groups, members // 2, 2), ("grp", "far", "near"))
    whole = ("grp", "far", "near")
    return jax.shard_map(
        local,
        mesh=finer,
        in_specs=(P(whole, None, None), P()),
        out_specs=P(None, whole, None, None),
        check_vma=False,
    )
```

time: 111 us -> 109 us (0.982)
  waiting for transfers between devices: 59.7 us -> 66.8 us
  local copies, waits for them, and re-layouts: 7.08 us -> 0.09 us
  Pallas kernels: 25.2 us -> 23.6 us
    all_to_all x1, waiting for transfers between devices: 18.6 us -> 23.3 us  [local(): lax.all_to_all(late, ('grp', 'far', 'near'), split_axis=0, concat_axis=0,...]
    slice x4, local copies, waits for them, and re-layouts: 3.62 us -> 0.08 us  [local(): crossed[k][r]]
    unnamed x10 -> x4, local copies, waits for them, and re-layouts: 2.92 us -> 0.01 us
    ppermute x3, waiting for transfers between devices: 0.01 us -> 2.25 us  [cross(): return lax.ppermute(x, 'far', [(a, a ^ k) for a in range(far)])]
    pallas_call x4, Pallas kernels: 25.2 us -> 23.6 us  [the longest x2 16 us: channelise(): pl.pallas_call(functools.partial(filter_kernel, radix, rows, far, first,...]
  transfers between devices with their start and end apart: 11 -> 11, of which waited for: 5 -> 6; matrix products, arithmetic and copies ran while one was open for 4% -> 0% of each run, Pallas kernels for 12% -> 12%
where the time goes in v4:
time: 109 us
  waiting for transfers between devices  66.8 us (61%)
  Pallas kernels  23.6 us (22%)
  starting transfers between devices  18.1 us (17%)
    ppermute x7, waiting for transfers between devices, swap(): return lax.ppermute(x, ('grp', 'near'), [(a, a ^ r) for a in range(near)])  41.2 us
    all_to_all x1, waiting for transfers between devices, local(): lax.all_to_all(late, ('grp', 'far', 'near'), split_axis=0, concat_axis=0,...  23.3 us
    pallas_call x2, Pallas kernels, channelise(): pl.pallas_call(functools.partial(filter_kernel, radix, rows, far, first,...  16 us
    pallas_call x2, Pallas kernels, correlate(): pl.pallas_call(functools.partial(gram_kernel, radix, ch_dev, rows, groups...  7.6 us
    ppermute x7, starting transfers between devices, swap(): return lax.ppermute(x, ('grp', 'near'), [(a, a ^ r) for a in range(near)])  6.23 us
    all_to_all x1, starting transfers between devices, local(): lax.all_to_all(late, ('grp', 'far', 'near'), split_axis=0, concat_axis=0,...  6.21 us
    ppermute x3, starting transfers between devices, cross(): return lax.ppermute(x, 'far', [(a, a ^ k) for a in range(far)])  5.67 us
    ppermute x3, waiting for transfers between devices, cross(): return lax.ppermute(x, 'far', [(a, a ^ k) for a in range(far)])  2.25 us
  transfers between devices with their start and end apart: 11, of which 6 were waited for; matrix products, arithmetic and copies ran while one was open for 0% of the time, Pallas kernels for 12%

profile of v4, /device:TPU:0, one launch (start us, length us, event | category | flops | bytes accessed | tf_op | source)
XLA Modules:
  0.0 108.9 jit_solution(16972221572281503139)
XLA Ops:
  0.0 5.6 %shard_map.55 = (bf16[8,4,32,128]{3,2,1,0:T(8,128)(2,1)}, bf16[8,4,32,128]{3,2,1,0:T(8,128)(2,1)}, bf16[8,4,32,128]{3,2,1,0:T(8,128)(2,1)}, bf16[8,4,32,128]{3,2,1,0:T(8,128)(2,1)}) custom-call(s32[515,32,128]{2,1,0:T(8,128)} %bitcast.6, s32[4,1024]{1,0:T(4,128)} %taps_ref.3, bf16[2,6,4,64,256]{4,3,2,1,0:T(8,128)(2,1)} %constant.4.clone.table_ref), custom_call_target="tpu_custom_call" | custom-call | flops 1 | bytes 1 | tf_op jit(solution)/shard_map/pallas_call | solution.py:187
  5.6 3.1 %collective-permute-start = (bf16[8,4,32,128]{3,2,1,0:T(8,128)(2,1)}, bf16[8,4,32,128]{3,2,1,0:T(8,128)(2,1)S(1)}, u32[]{:S(2)}, u32[]{:S(2)}) collective-permute-start(bf16[8,4,32,128]{3,2,1,0:T(8,128)(2,1)} %get-tuple-element.13), channel_id=1, source_target_pairs={{0,2},{2,0},{4,6},{6,4},{1,3},{3,1},{5,7},{7,5},{8,10},{10,8},{12,... | collective-permute-start | bytes 786440 | tf_op jit(solution)/shard_map/ppermute | solution.py:318
  8.7 2.6 %collective-permute-start.1 = (bf16[8,4,32,128]{3,2,1,0:T(8,128)(2,1)}, bf16[8,4,32,128]{3,2,1,0:T(8,128)(2,1)S(1)}, u32[]{:S(2)}, u32[]{:S(2)}) collective-permute-start(bf16[8,4,32,128]{3,2,1,0:T(8,128)(2,1)} %get-tuple-element.14), channel_id=1, source_target_pairs={{0,4},{2,6},{4,0},{6,2},{1,5},{3,7},{5,1},{7,3},{8,12},{10,14},{12... | collective-permute-start | bytes 786440 | tf_op jit(solution)/shard_map/ppermute | solution.py:318
  11.3 0.0 collective-permute-start.2
  11.3 10.4 %shard_map.57 = bf16[4,4,2,3,4,32,128]{6,5,4,3,2,1,0:T(8,128)(2,1)} custom-call(s32[515,32,128]{2,1,0:T(8,128)} %bitcast.7, s32[4,1024]{1,0:T(4,128)} %taps_ref.3, bf16[2,6,4,64,256]{4,3,2,1,0:T(8,128)(2,1)} %constant.4.clone.table_ref), custom_call_target="tpu_custom_call" | custom-call | flops 1 | bytes 1 | tf_op jit(solution)/shard_map/pallas_call | solution.py:187
  21.7 0.0 copy-start.1
  21.7 6.2 %all-to-all-start = ((bf16[32,3,4,32,128]{4,3,2,1,0:T(8,128)(2,1)}), bf16[32,3,4,32,128]{4,3,2,1,0:T(8,128)(2,1)}, u32[]{:S(2)}, u32[]{:S(2)}) async-start(bf16[32,3,4,32,128]{4,3,2,1,0:T(8,128)(2,1)} %bitcast.8), calls=%async_computation | async-start | bytes 6291456 | tf_op jit(solution)/shard_map/all_to_all | solution.py:327
  27.9 0.0 copy-done.1
  27.9 0.0 copy-start
  28.0 0.0 collective-permute-done
  28.0 2.2 %collective-permute-done.1 = bf16[8,4,32,128]{3,2,1,0:T(8,128)(2,1)S(1)} collective-permute-done((bf16[8,4,32,128]{3,2,1,0:T(8,128)(2,1)}, bf16[8,4,32,128]{3,2,1,0:T(8,128)(2,1)S(1)}, u32[]{:S(2)}, u32[]{:S(2)}) %collective-permute-start.1) | collective-permute-done | bytes 262176 | tf_op jit(solution)/shard_map/ppermute | solution.py:318
  30.3 0.0 collective-permute-done.2
  30.4 1.6 %collective-permute-start.3 = (bf16[4,4,32,128]{3,2,1,0:T(8,128)(2,1)S(1)}, bf16[4,4,32,128]{3,2,1,0:T(8,128)(2,1)S(1)}, u32[]{:S(2)}, u32[]{:S(2)}) collective-permute-start(bf16[4,4,32,128]{3,2,1,0:T(8,128)(2,1)S(1)} %pad_maximum_fusion.1), channel_id=1, source_target_pairs={{0,1},{1,0},{8,9},{9,8},{16,17},{17,16},{24,25},{25,24},{2,3},{3,2... | collective-permute-start | bytes 393224 | tf_op jit(solution)/shard_map/ppermute | solution.py:321
  31.9 0.1 collective-permute-start.4
  32.1 0.7 collective-permute-start.5
  32.8 1.6 %collective-permute-start.6 = (bf16[4,4,32,128]{3,2,1,0:T(8,128)(2,1)S(1)}, bf16[4,4,32,128]{3,2,1,0:T(8,128)(2,1)S(1)}, u32[]{:S(2)}, u32[]{:S(2)}) collective-permute-start(bf16[4,4,32,128]{3,2,1,0:T(8,128)(2,1)S(1)} %pad_maximum_fusion.4), channel_id=1, source_target_pairs={{0,16},{1,17},{8,24},{9,25},{16,0},{17,1},{24,8},{25,9},{2,18},{3,... | collective-permute-start | bytes 393224 | tf_op jit(solution)/shard_map/ppermute | solution.py:321
  34.4 1.5 %collective-permute-start.7 = (bf16[4,4,32,128]{3,2,1,0:T(8,128)(2,1)S(1)}, bf16[4,4,32,128]{3,2,1,0:T(8,128)(2,1)S(1)}, u32[]{:S(2)}, u32[]{:S(2)}) collective-permute-start(bf16[4,4,32,128]{3,2,1,0:T(8,128)(2,1)S(1)} %pad_maximum_fusion.5), channel_id=1, source_target_pairs={{0,17},{1,16},{8,25},{9,24},{16,1},{17,0},{24,9},{25,8},{2,19},{3,... | collective-permute-start | bytes 393224 | tf_op jit(solution)/shard_map/ppermute | solution.py:321
  35.9 25.1 %collective-permute-done.3.refs_1_ = bf16[4,4,32,128]{3,2,1,0:T(8,128)(2,1)S(1)} collective-permute-done((bf16[4,4,32,128]{3,2,1,0:T(8,128)(2,1)S(1)}, bf16[4,4,32,128]{3,2,1,0:T(8,128)(2,1)S(1)}, u32[]{:S(2)}, u32[]{:S(2)}) %collective-permute-start.3) | collective-permute-done | bytes 131104 | tf_op jit(solution)/shard_map/ppermute | solution.py:321
  61.0 0.3 collective-permute-start.8
  61.3 0.0 collective-permute-done.4.refs_2_
  61.4 0.5 collective-permute-start.9
  61.9 3.1 %collective-permute-done.5.refs_3_ = bf16[4,4,32,128]{3,2,1,0:T(8,128)(2,1)S(1)} collective-permute-done((bf16[4,4,32,128]{3,2,1,0:T(8,128)(2,1)S(1)}, bf16[4,4,32,128]{3,2,1,0:T(8,128)(2,1)S(1)}, u32[]{:S(2)}, u32[]{:S(2)}) %collective-permute-start.5) | collective-permute-done | bytes 131104 | tf_op jit(solution)/shard_map/ppermute | solution.py:321
  65.0 0.0 collective-permute-done.6.refs_4_
  65.0 7.2 %collective-permute-done.7.refs_5_ = bf16[4,4,32,128]{3,2,1,0:T(8,128)(2,1)S(1)} collective-permute-done((bf16[4,4,32,128]{3,2,1,0:T(8,128)(2,1)S(1)}, bf16[4,4,32,128]{3,2,1,0:T(8,128)(2,1)S(1)}, u32[]{:S(2)}, u32[]{:S(2)}) %collective-permute-start.7) | collective-permute-done | bytes 131104 | tf_op jit(solution)/shard_map/ppermute | solution.py:321
  72.2 5.8 %collective-permute-done.8.refs_6_ = bf16[4,4,32,128]{3,2,1,0:T(8,128)(2,1)S(1)} collective-permute-done((bf16[4,4,32,128]{3,2,1,0:T(8,128)(2,1)S(1)}, bf16[4,4,32,128]{3,2,1,0:T(8,128)(2,1)S(1)}, u32[]{:S(2)}, u32[]{:S(2)}) %collective-permute-start.8) | collective-permute-done | bytes 131104 | tf_op jit(solution)/shard_map/ppermute | solution.py:321
  78.0 0.0 collective-permute-done.9.refs_7_
  78.0 0.0 copy-done
  78.0 2.2 %shard_map.56.refs_0_ = f32[2,16,128,128]{3,2,1,0:T(8,128)S(1)} custom-call(bf16[2,256,256]{2,1,0:T(8,128)(2,1)S(1)} %copy-done, bf16[4,4,32,128]{3,2,1,0:T(8,128)(2,1)S(1)} %pad_maximum_fusion.refs_0_, bf16[4,4,32,128]{3,2,1,0:T(8,128)(2,1)S(1)} %collective-permute-done.3.refs_1_, bf16[4,4,32,128]{3,2,1,0:T(8,128)(2,1)S(1)} %collective-permute-done.4.refs_2_, ...), custom_call_target="tpu_custom_call" | custom-call | flops 49999998976 | bytes 1 | tf_op jit(solution)/shard_map/pallas_call | solution.py:288
  80.2 23.3 %all-to-all-done.refs_1_ = bf16[32,3,4,32,128]{4,3,2,1,0:T(8,128)(2,1)} async-done(((bf16[32,3,4,32,128]{4,3,2,1,0:T(8,128)(2,1)}), bf16[32,3,4,32,128]{4,3,2,1,0:T(8,128)(2,1)}, u32[]{:S(2)}, u32[]{:S(2)}) %all-to-all-start) | async-done | bytes 3145760 | tf_op jit(solution)/shard_map/all_to_all | solution.py:327
  103.5 5.4 %shard_map.58 = f32[2,16,128,128]{3,2,1,0:T(8,128)} custom-call(bf16[2,256,256]{2,1,0:T(8,128)(2,1)S(1)} %copy-done, f32[2,16,128,128]{3,2,1,0:T(8,128)S(1)} %shard_map.56.refs_0_, bf16[32,3,4,32,128]{4,3,2,1,0:T(8,128)(2,1)} %all-to-all-done.refs_1_), custom_call_target="tpu_custom_call" | custom-call | flops 1 | bytes 1 | tf_op jit(solution)/shard_map/pallas_call | solution.py:288
  (12 shorter events, 0.2 us)
Async XLA Ops:
  5.6 22.4 %collective-permute-start = (bf16[8,4,32,128]{3,2,1,0:T(8,128)(2,1)}, bf16[8,4,32,128]{3,2,1,0:T(8,128)(2,1)S(1)}, u32[]{:S(2)}, u32[]{:S(2)}) collective-permute-start(bf16[8,4,32,128]{3,2,1,0:T(8,128)(2,1)} %get-tuple-element.13), channel_id=1, source_target_pairs={{0,2},{2,0},{4,6},{6,4},{1,3},{3,1},{5,7},{7,5},{8,10},{10,8},{12,... | collective-permute-start | bytes 786440 | tf_op jit(solution)/shard_map/ppermute | solution.py:318
  8.7 21.6 %collective-permute-start.1 = (bf16[8,4,32,128]{3,2,1,0:T(8,128)(2,1)}, bf16[8,4,32,128]{3,2,1,0:T(8,128)(2,1)S(1)}, u32[]{:S(2)}, u32[]{:S(2)}) collective-permute-start(bf16[8,4,32,128]{3,2,1,0:T(8,128)(2,1)} %get-tuple-element.14), channel_id=1, source_target_pairs={{0,4},{2,6},{4,0},{6,2},{1,5},{3,7},{5,1},{7,3},{8,12},{10,14},{12... | collective-permute-start | bytes 786440 | tf_op jit(solution)/shard_map/ppermute | solution.py:318
  11.3 19.0 %collective-permute-start.2 = (bf16[8,4,32,128]{3,2,1,0:T(8,128)(2,1)}, bf16[8,4,32,128]{3,2,1,0:T(8,128)(2,1)S(1)}, u32[]{:S(2)}, u32[]{:S(2)}) collective-permute-start(bf16[8,4,32,128]{3,2,1,0:T(8,128)(2,1)} %get-tuple-element.15), channel_id=1, source_target_pairs={{0,6},{2,4},{4,2},{6,0},{1,7},{3,5},{5,3},{7,1},{8,14},{10,12},{12... | collective-permute-start | bytes 786440 | tf_op jit(solution)/shard_map/ppermute | solution.py:318
  21.7 6.2 %copy-start.1 = (bf16[8,4,32,128]{3,2,1,0:T(8,128)(2,1)S(1)}, bf16[8,4,32,128]{3,2,1,0:T(8,128)(2,1)}, u32[]{:S(2)}) copy-start(bf16[8,4,32,128]{3,2,1,0:T(8,128)(2,1)} %get-tuple-element.12) | copy-start | bytes 786436
  21.7 81.8 %all-to-all-start = ((bf16[32,3,4,32,128]{4,3,2,1,0:T(8,128)(2,1)}), bf16[32,3,4,32,128]{4,3,2,1,0:T(8,128)(2,1)}, u32[]{:S(2)}, u32[]{:S(2)}) async-start(bf16[32,3,4,32,128]{4,3,2,1,0:T(8,128)(2,1)} %bitcast.8), calls=%async_computation | async-start | bytes 6291456 | tf_op jit(solution)/shard_map/all_to_all | solution.py:327
  27.9 50.1 %copy-start = (bf16[2,256,256]{2,1,0:T(8,128)(2,1)S(1)}, bf16[2,256,256]{2,1,0:T(8,128)(2,1)}, u32[]{:S(2)}) copy-start(bf16[2,256,256]{2,1,0:T(8,128)(2,1)} %constant.5.clone.order_ref) | copy-start | bytes 786436
  30.4 30.7 %collective-permute-start.3 = (bf16[4,4,32,128]{3,2,1,0:T(8,128)(2,1)S(1)}, bf16[4,4,32,128]{3,2,1,0:T(8,128)(2,1)S(1)}, u32[]{:S(2)}, u32[]{:S(2)}) collective-permute-start(bf16[4,4,32,128]{3,2,1,0:T(8,128)(2,1)S(1)} %pad_maximum_fusion.1), channel_id=1, source_target_pairs={{0,1},{1,0},{8,9},{9,8},{16,17},{17,16},{24,25},{25,24},{2,3},{3,2... | collective-permute-start | bytes 393224 | tf_op jit(solution)/shard_map/ppermute | solution.py:321
  31.9 29.4 %collective-permute-start.4 = (bf16[4,4,32,128]{3,2,1,0:T(8,128)(2,1)S(1)}, bf16[4,4,32,128]{3,2,1,0:T(8,128)(2,1)S(1)}, u32[]{:S(2)}, u32[]{:S(2)}) collective-permute-start(bf16[4,4,32,128]{3,2,1,0:T(8,128)(2,1)S(1)} %pad_maximum_fusion.2), channel_id=1, source_target_pairs={{0,8},{1,9},{8,0},{9,1},{16,24},{17,25},{24,16},{25,17},{2,10},{3,... | collective-permute-start | bytes 393224 | tf_op jit(solution)/shard_map/ppermute | solution.py:321
  32.1 32.9 %collective-permute-start.5 = (bf16[4,4,32,128]{3,2,1,0:T(8,128)(2,1)S(1)}, bf16[4,4,32,128]{3,2,1,0:T(8,128)(2,1)S(1)}, u32[]{:S(2)}, u32[]{:S(2)}) collective-permute-start(bf16[4,4,32,128]{3,2,1,0:T(8,128)(2,1)S(1)} %pad_maximum_fusion.3), channel_id=1, source_target_pairs={{0,9},{1,8},{8,1},{9,0},{16,25},{17,24},{24,17},{25,16},{2,11},{3,... | collective-permute-start | bytes 393224 | tf_op jit(solution)/shard_map/ppermute | solution.py:321
  32.8 32.2 %collective-permute-start.6 = (bf16[4,4,32,128]{3,2,1,0:T(8,128)(2,1)S(1)}, bf16[4,4,32,128]{3,2,1,0:T(8,128)(2,1)S(1)}, u32[]{:S(2)}, u32[]{:S(2)}) collective-permute-start(bf16[4,4,32,128]{3,2,1,0:T(8,128)(2,1)S(1)} %pad_maximum_fusion.4), channel_id=1, source_target_pairs={{0,16},{1,17},{8,24},{9,25},{16,0},{17,1},{24,8},{25,9},{2,18},{3,... | collective-permute-start | bytes 393224 | tf_op jit(solution)/shard_map/ppermute | solution.py:321
  34.4 37.8 %collective-permute-start.7 = (bf16[4,4,32,128]{3,2,1,0:T(8,128)(2,1)S(1)}, bf16[4,4,32,128]{3,2,1,0:T(8,128)(2,1)S(1)}, u32[]{:S(2)}, u32[]{:S(2)}) collective-permute-start(bf16[4,4,32,128]{3,2,1,0:T(8,128)(2,1)S(1)} %pad_maximum_fusion.5), channel_id=1, source_target_pairs={{0,17},{1,16},{8,25},{9,24},{16,1},{17,0},{24,9},{25,8},{2,19},{3,... | collective-permute-start | bytes 393224 | tf_op jit(solution)/shard_map/ppermute | solution.py:321
  61.0 17.0 %collective-permute-start.8 = (bf16[4,4,32,128]{3,2,1,0:T(8,128)(2,1)S(1)}, bf16[4,4,32,128]{3,2,1,0:T(8,128)(2,1)S(1)}, u32[]{:S(2)}, u32[]{:S(2)}) collective-permute-start(bf16[4,4,32,128]{3,2,1,0:T(8,128)(2,1)S(1)} %pad_maximum_fusion.6), channel_id=1, source_target_pairs={{0,24},{1,25},{8,16},{9,17},{16,8},{17,9},{24,0},{25,1},{2,26},{3,... | collective-permute-start | bytes 393224 | tf_op jit(solution)/shard_map/ppermute | solution.py:321
  61.4 16.7 %collective-permute-start.9 = (bf16[4,4,32,128]{3,2,1,0:T(8,128)(2,1)S(1)}, bf16[4,4,32,128]{3,2,1,0:T(8,128)(2,1)S(1)}, u32[]{:S(2)}, u32[]{:S(2)}) collective-permute-start(bf16[4,4,32,128]{3,2,1,0:T(8,128)(2,1)S(1)} %pad_maximum_fusion.7), channel_id=1, source_target_pairs={{0,25},{1,24},{8,17},{9,16},{16,9},{17,8},{24,1},{25,0},{2,27},{3,... | collective-permute-start | bytes 393224 | tf_op jit(solution)/shard_map/ppermute | solution.py:321

commit v5 on v4

--- a/solution.py
+++ b/solution.py
@@ -21,10 +21,11 @@
 BLOCK = 128
 EARLY = 1
 HEAD_FLOPS = 5 * 10**10
+GROUP = 4
 STEP = 8
 PIECES = 4
 HEAD_VMEM = 32 << 20
-TAIL_VMEM = 50 << 20
+TAIL_VMEM = 32 << 20
 FILTER_VMEM = 56 << 20
 
 TERMS = {4: (((0, 0),), ((2, 1), (3, 2)), ((1, 3),), ((4, 1), (5, 2))), 1: (((0, 0),),)}
@@ -208,70 +209,72 @@
     )(frames, taps, table)
 
 
-def gram_kernel(radix, ch_dev, rows, groups, far, near_size, pick, blocks, fixed, more, order_ref, *refs):
-    arrays, (o_ref, z_ref, out_ref, old_ref, old_sem, out_sem) = refs[:-6], refs[-6:]
+def turn(order, views, rows, parts, both):
+    blocks = [jnp.concatenate([v[...].reshape(rows * parts, BLOCK) for v in near], 0) for near in views]
+    y = jnp.dot(order, jnp.concatenate(blocks, 1), preferred_element_type=jnp.float32)
+    return y.reshape(parts, both, len(views) * BLOCK)
+
+
+def head_kernel(rows, groups, far, near_size, parts, order_ref, *refs):
+    arrays, (o_ref, z_ref) = refs[:-2], refs[-2:]
+    both = near_size * rows
+    me_near, me_far = lax.axis_index(("grp", "near")), lax.axis_index("far")
+    me_group, me_side = me_near // near_size, me_near % near_size
+    order = order_ref[me_side]
+    for g in range(groups):
+        for k in range(far):
+            at = (me_group ^ g) * far + (me_far ^ k)
+            near = [arrays[g * near_size + x].at[k] for x in range(near_size)]
+            z_ref[:, pl.ds(pl.multiple_of(at * both, both), both), :] = turn(order, [near], rows, parts, both)
+    o_ref[...] = z_ref[...].astype(o_ref.dtype)
+
+
+def gram_kernel(radix, ch_dev, rows, groups, far, near_size, order_ref, early_ref, late_ref, *refs):
+    o_ref, z_ref, out_ref, early_sem, out_sem = refs
     parts = 2 * ch_dev
     both = near_size * rows
-    if more:
-        before, arrays = arrays[0], arrays[1:]
-        fetch = pltpu.make_async_copy(before, old_ref, old_sem)
-        fetch.start()
-    if fixed:
-        me_far, me_group, me_side = 0, 0, 0
-    else:
-        me_near = lax.axis_index(("grp", "near"))
-        me_far, me_group, me_side = lax.axis_index("far"), me_near // near_size, me_near % near_size
-    order = order_ref[me_side]
-    wide = 2 if fixed and far % 2 == 0 else 1
+    pieces = early_sem.shape[0]
+    size = parts // pieces
+    fetches = []
+    for n in range(pieces):
+        part = pl.ds(n * size, size)
+        fetches.append(pltpu.make_async_copy(early_ref.at[part], z_ref.at[part, :, 0:BLOCK], early_sem.at[n]))
+        fetches[-1].start()
+    order = order_ref[0]
+    wide = 2 if far % 2 == 0 else 1
     for g in range(groups):
         for k in range(0, far, wide):
-            at = (me_group ^ g) * far + (me_far ^ k)
             turned = []
             for w in range(wide):
-                block = jnp.concatenate(
-                    [
-                        jnp.concatenate(
-                            [
-                                pick(arrays, n, k + w, g * near_size + x)[...].reshape(rows * parts, BLOCK)
-                                for x in range(near_size)
-                            ],
-                            0,
-                        )
-                        for n in range(blocks)
-                    ],
-                    1,
-                )
-                y = jnp.dot(order, block, preferred_element_type=jnp.float32)
-                turned.append(y.reshape(parts, both, blocks * BLOCK))
-            low = at * both if fixed else pl.multiple_of(at * both, both)
-            z_ref[:, pl.ds(low, wide * both), :] = jnp.concatenate(turned, 1).astype(z_ref.dtype)
+                at = (g * far + k + w) * near_size
+                views = [
+                    [late_ref.at[at + x, n] for x in range(near_size)] for n in range(late_ref.shape[1])
+                ]
+                turned.append(turn(order, views, rows, parts, both))
+            low = (g * far + k) * both
+            z_ref[:, low : low + wide * both, BLOCK:] = jnp.concatenate(turned, 1).astype(z_ref.dtype)
+    for fetch in fetches:
+        fetch.wait()
     inputs = z_ref.shape[1]
     per = ch_dev // radix
-    if more:
-        fetch.wait()
     copies = []
     for c in range(ch_dev):
         at = (c % radix) * 2 * per + c // radix
-        z = jnp.concatenate([z_ref[at], z_ref[at + per]], 0).astype(jnp.bfloat16)
+        z = jnp.concatenate([z_ref[at], z_ref[at + per]], 0)
         g = product(z, z)
-        real = (g[:inputs, :inputs] + g[inputs:, inputs:]) * (1.0 / SPECTRA)
-        imag = (g[inputs:, :inputs] - g[:inputs, inputs:]) * (1.0 / SPECTRA)
-        if more:
-            real, imag = old_ref[0, c] + real, old_ref[1, c] + imag
-        out_ref[0, c] = real
-        out_ref[1, c] = imag
-        if (c + 1) % radix == 0:
-            group = pl.ds(c + 1 - radix, radix)
+        out_ref[0, c] = (g[:inputs, :inputs] + g[inputs:, inputs:]) * (1.0 / SPECTRA)
+        out_ref[1, c] = (g[inputs:, :inputs] - g[:inputs, inputs:]) * (1.0 / SPECTRA)
+        if (c + 1) % GROUP == 0:
+            group = pl.ds(c + 1 - GROUP, GROUP)
             copies.append(
-                pltpu.make_async_copy(out_ref.at[:, group], o_ref.at[:, group], out_sem.at[c // radix])
+                pltpu.make_async_copy(out_ref.at[:, group], o_ref.at[:, group], out_sem.at[c // GROUP])
             )
             copies[-1].start()
     for copy in copies:
         copy.wait()
 
 
-def correlate(arrays, pick, blocks, before, fixed, flops, rows, groups, far, near_size, ch_dev):
-    parts = 2 * ch_dev
+def order_of(rows, near_size, parts):
     both = near_size * rows
     wide = both * parts
     order = np.zeros((near_size, wide, wide), np.float32)
@@ -280,28 +283,41 @@
             for i in range(rows):
                 for b in range(parts):
                     order[flip, b * both + x * rows + i, ((x ^ flip) * rows + i) * parts + b] = 1.0
-    inputs = groups * far * both
+    return jnp.asarray(order, jnp.bfloat16)
+
+
+def collect(arrays, rows, groups, far, near_size, ch_dev):
+    parts, inputs = 2 * ch_dev, groups * far * near_size * rows
+    vmem = pl.BlockSpec(memory_space=pltpu.VMEM)
+    return pl.pallas_call(
+        functools.partial(head_kernel, rows, groups, far, near_size, parts),
+        out_shape=jax.ShapeDtypeStruct((parts, inputs, BLOCK), jnp.bfloat16),
+        in_specs=[vmem] * (1 + len(arrays)),
+        out_specs=vmem,
+        scratch_shapes=[pltpu.VMEM((parts, inputs, BLOCK), jnp.float32)],
+        compiler_params=pltpu.CompilerParams(vmem_limit_bytes=HEAD_VMEM),
+        cost_estimate=pl.CostEstimate(flops=HEAD_FLOPS, bytes_accessed=1, transcendentals=0),
+    )(order_of(rows, near_size, parts), *arrays)
+
+
+def correlate(early, late, rows, groups, far, near_size, ch_dev):
+    parts, inputs = 2 * ch_dev, groups * far * near_size * rows
     shape = (2, ch_dev, inputs, inputs)
     vmem, hbm = pl.BlockSpec(memory_space=pltpu.VMEM), pl.BlockSpec(memory_space=pltpu.HBM)
-    more = before is not None
-    radix = radix_of(ch_dev)
     return pl.pallas_call(
-        functools.partial(
-            gram_kernel, radix, ch_dev, rows, groups, far, near_size, pick, blocks, fixed, more
-        ),
+        functools.partial(gram_kernel, radix_of(ch_dev), ch_dev, rows, groups, far, near_size),
         out_shape=jax.ShapeDtypeStruct(shape, jnp.float32),
-        in_specs=[vmem] + [hbm] * more + [vmem] * len(arrays),
+        in_specs=[vmem, hbm, vmem],
         out_specs=hbm,
         scratch_shapes=[
-            pltpu.VMEM((parts, inputs, blocks * BLOCK), jnp.bfloat16 if fixed else jnp.float32),
+            pltpu.VMEM((parts, inputs, SPECTRA), jnp.bfloat16),
             pltpu.VMEM(shape, jnp.float32),
-            pltpu.VMEM(shape if more else (8, LANES), jnp.float32),
-            pltpu.SemaphoreType.DMA,
-            pltpu.SemaphoreType.DMA((ch_dev // radix,)),
+            pltpu.SemaphoreType.DMA((4,)),
+            pltpu.SemaphoreType.DMA((ch_dev // GROUP,)),
         ],
-        compiler_params=pltpu.CompilerParams(vmem_limit_bytes=TAIL_VMEM if more else HEAD_VMEM),
-        cost_estimate=pl.CostEstimate(flops=flops, bytes_accessed=1, transcendentals=0),
-    )(jnp.asarray(order, jnp.bfloat16), *([before] if more else []), *arrays)
+        compiler_params=pltpu.CompilerParams(vmem_limit_bytes=TAIL_VMEM),
+        cost_estimate=pl.CostEstimate(flops=1, bytes_accessed=1, transcendentals=0),
+    )(order_of(rows, near_size, parts), pltpu.with_memory_space_constraint(early, pltpu.HBM), late)
 
 
 def local(samples, taps):
@@ -329,9 +345,7 @@
     crossed[0] = early[0]
     parcel = [jnp.stack([crossed[k][r] for k in range(far)], 0) for r in range(near)]
     first = parcel[:1] + [swap(parcel[r], r) for r in range(1, near)]
-    head = correlate(first, lambda a, n, k, r: a[r].at[k], 1, None, False, HEAD_FLOPS, *sizes)
-    where = lambda k, r: ((r // near_size) * far + k) * near_size + r % near_size
-    return correlate([late], lambda a, n, k, r: a[0].at[where(k, r), n], rest, head, True, 1, *sizes)
+    return correlate(collect(first, *sizes), late, *sizes)
 
 
 def solution(mesh):

time: 109 us -> 107 us (0.982)
  local copies, waits for them, and re-layouts: 0.09 us -> 4.62 us
  Pallas kernels: 23.6 us -> 20.2 us
  waiting for transfers between devices: 66.8 us -> 63.5 us
    slice x4, local copies, waits for them, and re-layouts: 0.08 us -> 3.62 us  [local(): crossed[k][r]]
    pallas_call x2, Pallas kernels: 7.6 us -> 4.29 us  [the longest x1 3.42 us: correlate(): pl.pallas_call(functools.partial(gram_kernel, radix_of(ch_dev), ch_dev, r...]
    ppermute x7, waiting for transfers between devices: 41.2 us -> 39.2 us  [swap(): return lax.ppermute(x, ('grp', 'near'), [(a, a ^ r) for a in range(near)])]
    ppermute x3, waiting for transfers between devices: 2.25 us -> 0.83 us  [cross(): return lax.ppermute(x, 'far', [(a, a ^ k) for a in range(far)])]
  transfers between devices with their start and end apart: 11 -> 11, of which waited for: 6 -> 6; matrix products, arithmetic and copies ran while one was open for 0% -> 4% of each run, Pallas kernels for 12% -> 10%
where the time goes in v5:
time: 107 us
  waiting for transfers between devices  63.5 us (59%)
  Pallas kernels  20.2 us (19%)
  starting transfers between devices  18.1 us (17%)
  local copies, waits for them, and re-layouts  4.62 us (4%)
    ppermute x7, waiting for transfers between devices, swap(): return lax.ppermute(x, ('grp', 'near'), [(a, a ^ r) for a in range(near)])  39.2 us
    all_to_all x1, waiting for transfers between devices, local(): lax.all_to_all(late, ('grp', 'far', 'near'), split_axis=0, concat_axis=0,...  23.5 us
    pallas_call x2, Pallas kernels, channelise(): pl.pallas_call(functools.partial(filter_kernel, radix, rows, far, first,...  15.9 us
    ppermute x7, starting transfers between devices, swap(): return lax.ppermute(x, ('grp', 'near'), [(a, a ^ r) for a in range(near)])  6.36 us
    all_to_all x1, starting transfers between devices, local(): lax.all_to_all(late, ('grp', 'far', 'near'), split_axis=0, concat_axis=0,...  6.08 us
    ppermute x3, starting transfers between devices, cross(): return lax.ppermute(x, 'far', [(a, a ^ k) for a in range(far)])  5.67 us
    slice x4, local copies, waits for them, and re-layouts, local(): crossed[k][r]  3.62 us
    pallas_call x1, Pallas kernels, correlate(): pl.pallas_call(functools.partial(gram_kernel, radix_of(ch_dev), ch_dev, r...  3.42 us
  transfers between devices with their start and end apart: 11, of which 6 were waited for; matrix products, arithmetic and copies ran while one was open for 4% of the time, Pallas kernels for 10%

profile of v5, /device:TPU:0, one launch (start us, length us, event | category | flops | bytes accessed | tf_op | source)
XLA Modules:
  0.0 106.7 jit_solution(4547731068372177588)
XLA Ops:
  0.0 5.6 %shard_map.55 = (bf16[8,4,32,128]{3,2,1,0:T(8,128)(2,1)}, bf16[8,4,32,128]{3,2,1,0:T(8,128)(2,1)}, bf16[8,4,32,128]{3,2,1,0:T(8,128)(2,1)}, bf16[8,4,32,128]{3,2,1,0:T(8,128)(2,1)}) custom-call(s32[515,32,128]{2,1,0:T(8,128)} %bitcast.6, s32[4,1024]{1,0:T(4,128)} %taps_ref.3, bf16[2,6,4,64,256]{4,3,2,1,0:T(8,128)(2,1)} %constant.4.clone.table_ref), custom_call_target="tpu_custom_call" | custom-call | flops 1 | bytes 1 | tf_op jit(solution)/shard_map/pallas_call | solution.py:188
  5.6 3.1 %collective-permute-start = (bf16[8,4,32,128]{3,2,1,0:T(8,128)(2,1)}, bf16[8,4,32,128]{3,2,1,0:T(8,128)(2,1)}, u32[]{:S(2)}, u32[]{:S(2)}) collective-permute-start(bf16[8,4,32,128]{3,2,1,0:T(8,128)(2,1)} %get-tuple-element.13), channel_id=1, source_target_pairs={{0,2},{2,0},{4,6},{6,4},{1,3},{3,1},{5,7},{7,5},{8,10},{10,8},{12,... | collective-permute-start | bytes 786440 | tf_op jit(solution)/shard_map/ppermute | solution.py:334
  8.7 2.6 %collective-permute-start.1 = (bf16[8,4,32,128]{3,2,1,0:T(8,128)(2,1)}, bf16[8,4,32,128]{3,2,1,0:T(8,128)(2,1)}, u32[]{:S(2)}, u32[]{:S(2)}) collective-permute-start(bf16[8,4,32,128]{3,2,1,0:T(8,128)(2,1)} %get-tuple-element.14), channel_id=1, source_target_pairs={{0,4},{2,6},{4,0},{6,2},{1,5},{3,7},{5,1},{7,3},{8,12},{10,14},{12... | collective-permute-start | bytes 786440 | tf_op jit(solution)/shard_map/ppermute | solution.py:334
  11.3 0.0 collective-permute-start.2
  11.3 10.3 %shard_map.57 = bf16[4,4,2,3,4,32,128]{6,5,4,3,2,1,0:T(8,128)(2,1)} custom-call(s32[515,32,128]{2,1,0:T(8,128)} %bitcast.7, s32[4,1024]{1,0:T(4,128)} %taps_ref.3, bf16[2,6,4,64,256]{4,3,2,1,0:T(8,128)(2,1)} %constant.4.clone.table_ref), custom_call_target="tpu_custom_call" | custom-call | flops 1 | bytes 1 | tf_op jit(solution)/shard_map/pallas_call | solution.py:188
  21.6 6.1 %all-to-all-start = ((bf16[32,3,4,32,128]{4,3,2,1,0:T(8,128)(2,1)}), bf16[32,3,4,32,128]{4,3,2,1,0:T(8,128)(2,1)S(1)}, u32[]{:S(2)}, u32[]{:S(2)}) async-start(bf16[32,3,4,32,128]{4,3,2,1,0:T(8,128)(2,1)} %bitcast.8), calls=%async_computation | async-start | bytes 6291456 | tf_op jit(solution)/shard_map/all_to_all | solution.py:343
  27.7 0.0 copy-start.1
  27.7 0.9 fusion
  28.6 0.0 collective-permute-done
  28.7 0.9 fusion.1
  29.6 0.8 collective-permute-done.1
  30.4 0.9 fusion.2
  31.3 0.0 collective-permute-done.2
  31.3 0.9 fusion.3
  32.2 1.6 %collective-permute-start.3 = (bf16[4,4,32,128]{3,2,1,0:T(8,128)(2,1)S(1)}, bf16[4,4,32,128]{3,2,1,0:T(8,128)(2,1)S(1)}, u32[]{:S(2)}, u32[]{:S(2)}) collective-permute-start(bf16[4,4,32,128]{3,2,1,0:T(8,128)(2,1)S(1)} %pad_maximum_fusion.1), channel_id=1, source_target_pairs={{0,1},{1,0},{8,9},{9,8},{16,17},{17,16},{24,25},{25,24},{2,3},{3,2... | collective-permute-start | bytes 393224 | tf_op jit(solution)/shard_map/ppermute | solution.py:337
  33.8 0.1 collective-permute-start.4
  33.9 0.7 collective-permute-start.5
  34.6 1.6 %collective-permute-start.6 = (bf16[4,4,32,128]{3,2,1,0:T(8,128)(2,1)S(1)}, bf16[4,4,32,128]{3,2,1,0:T(8,128)(2,1)S(1)}, u32[]{:S(2)}, u32[]{:S(2)}) collective-permute-start(bf16[4,4,32,128]{3,2,1,0:T(8,128)(2,1)S(1)} %pad_maximum_fusion.4), channel_id=1, source_target_pairs={{0,16},{1,17},{8,24},{9,25},{16,0},{17,1},{24,8},{25,9},{2,18},{3,... | collective-permute-start | bytes 393224 | tf_op jit(solution)/shard_map/ppermute | solution.py:337
  36.2 1.5 %collective-permute-start.7 = (bf16[4,4,32,128]{3,2,1,0:T(8,128)(2,1)S(1)}, bf16[4,4,32,128]{3,2,1,0:T(8,128)(2,1)S(1)}, u32[]{:S(2)}, u32[]{:S(2)}) collective-permute-start(bf16[4,4,32,128]{3,2,1,0:T(8,128)(2,1)S(1)} %pad_maximum_fusion.5), channel_id=1, source_target_pairs={{0,17},{1,16},{8,25},{9,24},{16,1},{17,0},{24,9},{25,8},{2,19},{3,... | collective-permute-start | bytes 393224 | tf_op jit(solution)/shard_map/ppermute | solution.py:337
  37.8 23.1 %collective-permute-done.3.refs_1_ = bf16[4,4,32,128]{3,2,1,0:T(8,128)(2,1)S(1)} collective-permute-done((bf16[4,4,32,128]{3,2,1,0:T(8,128)(2,1)S(1)}, bf16[4,4,32,128]{3,2,1,0:T(8,128)(2,1)S(1)}, u32[]{:S(2)}, u32[]{:S(2)}) %collective-permute-start.3) | collective-permute-done | bytes 131104 | tf_op jit(solution)/shard_map/ppermute | solution.py:337
  60.8 0.2 collective-permute-start.8
  61.0 0.0 collective-permute-done.4.refs_2_
  61.0 0.8 collective-permute-start.9
  61.8 3.0 %collective-permute-done.5.refs_3_ = bf16[4,4,32,128]{3,2,1,0:T(8,128)(2,1)S(1)} collective-permute-done((bf16[4,4,32,128]{3,2,1,0:T(8,128)(2,1)S(1)}, bf16[4,4,32,128]{3,2,1,0:T(8,128)(2,1)S(1)}, u32[]{:S(2)}, u32[]{:S(2)}) %collective-permute-start.5) | collective-permute-done | bytes 131104 | tf_op jit(solution)/shard_map/ppermute | solution.py:337
  64.8 0.0 collective-permute-done.6.refs_4_
  64.8 7.2 %collective-permute-done.7.refs_5_ = bf16[4,4,32,128]{3,2,1,0:T(8,128)(2,1)S(1)} collective-permute-done((bf16[4,4,32,128]{3,2,1,0:T(8,128)(2,1)S(1)}, bf16[4,4,32,128]{3,2,1,0:T(8,128)(2,1)S(1)}, u32[]{:S(2)}, u32[]{:S(2)}) %collective-permute-start.7) | collective-permute-done | bytes 131104 | tf_op jit(solution)/shard_map/ppermute | solution.py:337
  72.0 6.0 %collective-permute-done.8.refs_6_ = bf16[4,4,32,128]{3,2,1,0:T(8,128)(2,1)S(1)} collective-permute-done((bf16[4,4,32,128]{3,2,1,0:T(8,128)(2,1)S(1)}, bf16[4,4,32,128]{3,2,1,0:T(8,128)(2,1)S(1)}, u32[]{:S(2)}, u32[]{:S(2)}) %collective-permute-start.8) | collective-permute-done | bytes 131104 | tf_op jit(solution)/shard_map/ppermute | solution.py:337
  78.0 0.0 collective-permute-done.9.refs_7_
  78.0 0.0 copy-done.1
  78.0 0.9 shard_map.56.early_ref
  78.9 0.0 copy-start
  78.9 1.0 copy-done
  79.9 23.5 %all-to-all-done.late_ref = bf16[32,3,4,32,128]{4,3,2,1,0:T(8,128)(2,1)S(1)} async-done(((bf16[32,3,4,32,128]{4,3,2,1,0:T(8,128)(2,1)}), bf16[32,3,4,32,128]{4,3,2,1,0:T(8,128)(2,1)S(1)}, u32[]{:S(2)}, u32[]{:S(2)}) %all-to-all-start) | async-done | bytes 3145760 | tf_op jit(solution)/shard_map/all_to_all | solution.py:343
  103.3 3.4 %shard_map.58 = f32[2,16,128,128]{3,2,1,0:T(8,128)} custom-call(bf16[2,256,256]{2,1,0:T(8,128)(2,1)S(1)} %copy-done.1, bf16[32,128,128]{2,1,0:T(8,128)(2,1)} %copy-done, bf16[32,3,4,32,128]{4,3,2,1,0:T(8,128)(2,1)S(1)} %all-to-all-done.late_ref), custom_call_target="tpu_custom_call" | custom-call | flops 1 | bytes 1 | tf_op jit(solution)/shard_map/pallas_call | solution.py:307
  (8 shorter events, 0.2 us)
Async XLA Ops:
  5.6 23.0 %collective-permute-start = (bf16[8,4,32,128]{3,2,1,0:T(8,128)(2,1)}, bf16[8,4,32,128]{3,2,1,0:T(8,128)(2,1)}, u32[]{:S(2)}, u32[]{:S(2)}) collective-permute-start(bf16[8,4,32,128]{3,2,1,0:T(8,128)(2,1)} %get-tuple-element.13), channel_id=1, source_target_pairs={{0,2},{2,0},{4,6},{6,4},{1,3},{3,1},{5,7},{7,5},{8,10},{10,8},{12,... | collective-permute-start | bytes 786440 | tf_op jit(solution)/shard_map/ppermute | solution.py:334
  8.7 21.7 %collective-permute-start.1 = (bf16[8,4,32,128]{3,2,1,0:T(8,128)(2,1)}, bf16[8,4,32,128]{3,2,1,0:T(8,128)(2,1)}, u32[]{:S(2)}, u32[]{:S(2)}) collective-permute-start(bf16[8,4,32,128]{3,2,1,0:T(8,128)(2,1)} %get-tuple-element.14), channel_id=1, source_target_pairs={{0,4},{2,6},{4,0},{6,2},{1,5},{3,7},{5,1},{7,3},{8,12},{10,14},{12... | collective-permute-start | bytes 786440 | tf_op jit(solution)/shard_map/ppermute | solution.py:334
  11.3 20.0 %collective-permute-start.2 = (bf16[8,4,32,128]{3,2,1,0:T(8,128)(2,1)}, bf16[8,4,32,128]{3,2,1,0:T(8,128)(2,1)}, u32[]{:S(2)}, u32[]{:S(2)}) collective-permute-start(bf16[8,4,32,128]{3,2,1,0:T(8,128)(2,1)} %get-tuple-element.15), channel_id=1, source_target_pairs={{0,6},{2,4},{4,2},{6,0},{1,7},{3,5},{5,3},{7,1},{8,14},{10,12},{12... | collective-permute-start | bytes 786440 | tf_op jit(solution)/shard_map/ppermute | solution.py:334
  21.6 81.7 %all-to-all-start = ((bf16[32,3,4,32,128]{4,3,2,1,0:T(8,128)(2,1)}), bf16[32,3,4,32,128]{4,3,2,1,0:T(8,128)(2,1)S(1)}, u32[]{:S(2)}, u32[]{:S(2)}) async-start(bf16[32,3,4,32,128]{4,3,2,1,0:T(8,128)(2,1)} %bitcast.8), calls=%async_computation | async-start | bytes 6291456 | tf_op jit(solution)/shard_map/all_to_all | solution.py:343
  27.7 50.3 %copy-start.1 = (bf16[2,256,256]{2,1,0:T(8,128)(2,1)S(1)}, bf16[2,256,256]{2,1,0:T(8,128)(2,1)}, u32[]{:S(2)}) copy-start(bf16[2,256,256]{2,1,0:T(8,128)(2,1)} %constant.5.clone.order_ref) | copy-start | bytes 786436
  32.2 28.6 %collective-permute-start.3 = (bf16[4,4,32,128]{3,2,1,0:T(8,128)(2,1)S(1)}, bf16[4,4,32,128]{3,2,1,0:T(8,128)(2,1)S(1)}, u32[]{:S(2)}, u32[]{:S(2)}) collective-permute-start(bf16[4,4,32,128]{3,2,1,0:T(8,128)(2,1)S(1)} %pad_maximum_fusion.1), channel_id=1, source_target_pairs={{0,1},{1,0},{8,9},{9,8},{16,17},{17,16},{24,25},{25,24},{2,3},{3,2... | collective-permute-start | bytes 393224 | tf_op jit(solution)/shard_map/ppermute | solution.py:337
  33.8 27.2 %collective-permute-start.4 = (bf16[4,4,32,128]{3,2,1,0:T(8,128)(2,1)S(1)}, bf16[4,4,32,128]{3,2,1,0:T(8,128)(2,1)S(1)}, u32[]{:S(2)}, u32[]{:S(2)}) collective-permute-start(bf16[4,4,32,128]{3,2,1,0:T(8,128)(2,1)S(1)} %pad_maximum_fusion.2), channel_id=1, source_target_pairs={{0,8},{1,9},{8,0},{9,1},{16,24},{17,25},{24,16},{25,17},{2,10},{3,... | collective-permute-start | bytes 393224 | tf_op jit(solution)/shard_map/ppermute | solution.py:337
  33.9 30.9 %collective-permute-start.5 = (bf16[4,4,32,128]{3,2,1,0:T(8,128)(2,1)S(1)}, bf16[4,4,32,128]{3,2,1,0:T(8,128)(2,1)S(1)}, u32[]{:S(2)}, u32[]{:S(2)}) collective-permute-start(bf16[4,4,32,128]{3,2,1,0:T(8,128)(2,1)S(1)} %pad_maximum_fusion.3), channel_id=1, source_target_pairs={{0,9},{1,8},{8,1},{9,0},{16,25},{17,24},{24,17},{25,16},{2,11},{3,... | collective-permute-start | bytes 393224 | tf_op jit(solution)/shard_map/ppermute | solution.py:337
  34.6 30.2 %collective-permute-start.6 = (bf16[4,4,32,128]{3,2,1,0:T(8,128)(2,1)S(1)}, bf16[4,4,32,128]{3,2,1,0:T(8,128)(2,1)S(1)}, u32[]{:S(2)}, u32[]{:S(2)}) collective-permute-start(bf16[4,4,32,128]{3,2,1,0:T(8,128)(2,1)S(1)} %pad_maximum_fusion.4), channel_id=1, source_target_pairs={{0,16},{1,17},{8,24},{9,25},{16,0},{17,1},{24,8},{25,9},{2,18},{3,... | collective-permute-start | bytes 393224 | tf_op jit(solution)/shard_map/ppermute | solution.py:337
  36.2 35.8 %collective-permute-start.7 = (bf16[4,4,32,128]{3,2,1,0:T(8,128)(2,1)S(1)}, bf16[4,4,32,128]{3,2,1,0:T(8,128)(2,1)S(1)}, u32[]{:S(2)}, u32[]{:S(2)}) collective-permute-start(bf16[4,4,32,128]{3,2,1,0:T(8,128)(2,1)S(1)} %pad_maximum_fusion.5), channel_id=1, source_target_pairs={{0,17},{1,16},{8,25},{9,24},{16,1},{17,0},{24,9},{25,8},{2,19},{3,... | collective-permute-start | bytes 393224 | tf_op jit(solution)/shard_map/ppermute | solution.py:337
  60.8 17.1 %collective-permute-start.8 = (bf16[4,4,32,128]{3,2,1,0:T(8,128)(2,1)S(1)}, bf16[4,4,32,128]{3,2,1,0:T(8,128)(2,1)S(1)}, u32[]{:S(2)}, u32[]{:S(2)}) collective-permute-start(bf16[4,4,32,128]{3,2,1,0:T(8,128)(2,1)S(1)} %pad_maximum_fusion.6), channel_id=1, source_target_pairs={{0,24},{1,25},{8,16},{9,17},{16,8},{17,9},{24,0},{25,1},{2,26},{3,... | collective-permute-start | bytes 393224 | tf_op jit(solution)/shard_map/ppermute | solution.py:337
  61.0 16.9 %collective-permute-start.9 = (bf16[4,4,32,128]{3,2,1,0:T(8,128)(2,1)S(1)}, bf16[4,4,32,128]{3,2,1,0:T(8,128)(2,1)S(1)}, u32[]{:S(2)}, u32[]{:S(2)}) collective-permute-start(bf16[4,4,32,128]{3,2,1,0:T(8,128)(2,1)S(1)} %pad_maximum_fusion.7), channel_id=1, source_target_pairs={{0,25},{1,24},{8,17},{9,16},{16,9},{17,8},{24,1},{25,0},{2,27},{3,... | collective-permute-start | bytes 393224 | tf_op jit(solution)/shard_map/ppermute | solution.py:337
  78.9 1.0 copy-start

commit v6 on v5

--- a/solution.py
+++ b/solution.py
@@ -23,7 +23,7 @@
 HEAD_FLOPS = 5 * 10**10
 GROUP = 4
 STEP = 8
-PIECES = 4
+PIECES = 2
 HEAD_VMEM = 32 << 20
 TAIL_VMEM = 32 << 20
 FILTER_VMEM = 56 << 20
@@ -74,7 +74,11 @@
     step = pl.program_id(0)
     slot = lax.rem(step, 2)
     size = BLOCK // PIECES
-    table_copy = pltpu.make_async_copy(table_ref, w_ref, table_sem)
+    table_copies = [
+        pltpu.make_async_copy(table_ref.at[half, n], w_ref.at[half, n], table_sem.at[half, n])
+        for n in range(w_ref.shape[1])
+        for half in range(2)
+    ]
 
     def fetch(step, slot, piece):
         low, high = (piece * size + TAPS - 1 if piece else 0), (piece + 1) * size + TAPS - 1
@@ -88,7 +92,8 @@
     def _():
         for piece in range(PIECES):
             fetch(step, slot, piece).start()
-        table_copy.start()
+        for copy in table_copies:
+            copy.start()
         for t in range(TAPS):
             for h in range(TILES):
                 tap = taps_ref[t : t + 1, h * LANES : (h + 1) * LANES].astype(jnp.float32)
@@ -116,7 +121,8 @@
 
     @pl.when(step == 0)
     def _():
-        table_copy.wait()
+        for copy in table_copies:
+            copy.wait()
 
     me_far, me_near = (lax.axis_index("far"), lax.axis_index(("grp", "near"))) if apart else (0, 0)
     stride = f_ref.shape[1]
@@ -201,7 +207,7 @@
             pltpu.VMEM((TAPS, wide, LANES), jnp.float32),
             pltpu.VMEM(table.shape, table.dtype),
             pltpu.VMEM((2, BLOCK + TAPS - 1, wide, LANES), jnp.int32),
-            pltpu.SemaphoreType.DMA,
+            pltpu.SemaphoreType.DMA(table.shape[:2]),
             pltpu.SemaphoreType.DMA((2, PIECES)),
         ],
         compiler_params=pltpu.CompilerParams(vmem_limit_bytes=FILTER_VMEM),

time: 107 us -> 107 us (level)
    all_to_all x1, waiting for transfers between devices: 23.5 us -> 22.3 us  [local(): lax.all_to_all(late, ('grp', 'far', 'near'), split_axis=0, concat_axis=0,...]
    ppermute x7, waiting for transfers between devices: 39.2 us -> 40.4 us  [swap(): return lax.ppermute(x, ('grp', 'near'), [(a, a ^ r) for a in range(near)])]
  transfers between devices with their start and end apart: 11 -> 11, of which waited for: 6 -> 6; matrix products, arithmetic and copies ran while one was open for 4% -> 4% of each run, Pallas kernels for 10% -> 11%
where the time goes in v6:
time: 107 us
  waiting for transfers between devices  63 us (59%)
  Pallas kernels  21.1 us (20%)
  starting transfers between devices  17.5 us (16%)
  local copies, waits for them, and re-layouts  4.62 us (4%)
    ppermute x7, waiting for transfers between devices, swap(): return lax.ppermute(x, ('grp', 'near'), [(a, a ^ r) for a in range(near)])  40.4 us
    all_to_all x1, waiting for transfers between devices, local(): lax.all_to_all(late, ('grp', 'far', 'near'), split_axis=0, concat_axis=0,...  22.3 us
    pallas_call x2, Pallas kernels, channelise(): pl.pallas_call(functools.partial(filter_kernel, radix, rows, far, first,...  16.8 us
    all_to_all x1, starting transfers between devices, local(): lax.all_to_all(late, ('grp', 'far', 'near'), split_axis=0, concat_axis=0,...  6.07 us
    ppermute x7, starting transfers between devices, swap(): return lax.ppermute(x, ('grp', 'near'), [(a, a ^ r) for a in range(near)])  5.72 us
    ppermute x3, starting transfers between devices, cross(): return lax.ppermute(x, 'far', [(a, a ^ k) for a in range(far)])  5.68 us
    slice x4, local copies, waits for them, and re-layouts, local(): crossed[k][r]  3.62 us
    pallas_call x1, Pallas kernels, correlate(): pl.pallas_call(functools.partial(gram_kernel, radix_of(ch_dev), ch_dev, r...  3.42 us
  transfers between devices with their start and end apart: 11, of which 6 were waited for; matrix products, arithmetic and copies ran while one was open for 4% of the time, Pallas kernels for 11%

profile of v6, /device:TPU:0, one launch (start us, length us, event | category | flops | bytes accessed | tf_op | source)
XLA Modules:
  0.0 106.5 jit_solution(17753074822352011061)
XLA Ops:
  0.0 6.0 %shard_map.55 = (bf16[8,4,32,128]{3,2,1,0:T(8,128)(2,1)}, bf16[8,4,32,128]{3,2,1,0:T(8,128)(2,1)}, bf16[8,4,32,128]{3,2,1,0:T(8,128)(2,1)}, bf16[8,4,32,128]{3,2,1,0:T(8,128)(2,1)}) custom-call(s32[515,32,128]{2,1,0:T(8,128)} %bitcast.6, s32[4,1024]{1,0:T(4,128)} %taps_ref.3, bf16[2,6,4,64,256]{4,3,2,1,0:T(8,128)(2,1)} %constant.4.clone.table_ref), custom_call_target="tpu_custom_call" | custom-call | flops 1 | bytes 1 | tf_op jit(solution)/shard_map/pallas_call | solution.py:194
  6.1 3.1 %collective-permute-start = (bf16[8,4,32,128]{3,2,1,0:T(8,128)(2,1)}, bf16[8,4,32,128]{3,2,1,0:T(8,128)(2,1)}, u32[]{:S(2)}, u32[]{:S(2)}) collective-permute-start(bf16[8,4,32,128]{3,2,1,0:T(8,128)(2,1)} %get-tuple-element.13), channel_id=1, source_target_pairs={{0,2},{2,0},{4,6},{6,4},{1,3},{3,1},{5,7},{7,5},{8,10},{10,8},{12,... | collective-permute-start | bytes 786440 | tf_op jit(solution)/shard_map/ppermute | solution.py:340
  9.1 2.6 %collective-permute-start.1 = (bf16[8,4,32,128]{3,2,1,0:T(8,128)(2,1)}, bf16[8,4,32,128]{3,2,1,0:T(8,128)(2,1)}, u32[]{:S(2)}, u32[]{:S(2)}) collective-permute-start(bf16[8,4,32,128]{3,2,1,0:T(8,128)(2,1)} %get-tuple-element.14), channel_id=1, source_target_pairs={{0,4},{2,6},{4,0},{6,2},{1,5},{3,7},{5,1},{7,3},{8,12},{10,14},{12... | collective-permute-start | bytes 786440 | tf_op jit(solution)/shard_map/ppermute | solution.py:340
  11.7 0.0 collective-permute-start.2
  11.7 10.8 %shard_map.57 = bf16[4,4,2,3,4,32,128]{6,5,4,3,2,1,0:T(8,128)(2,1)} custom-call(s32[515,32,128]{2,1,0:T(8,128)} %bitcast.7, s32[4,1024]{1,0:T(4,128)} %taps_ref.3, bf16[2,6,4,64,256]{4,3,2,1,0:T(8,128)(2,1)} %constant.4.clone.table_ref), custom_call_target="tpu_custom_call" | custom-call | flops 1 | bytes 1 | tf_op jit(solution)/shard_map/pallas_call | solution.py:194
  22.5 6.1 %all-to-all-start = ((bf16[32,3,4,32,128]{4,3,2,1,0:T(8,128)(2,1)}), bf16[32,3,4,32,128]{4,3,2,1,0:T(8,128)(2,1)S(1)}, u32[]{:S(2)}, u32[]{:S(2)}) async-start(bf16[32,3,4,32,128]{4,3,2,1,0:T(8,128)(2,1)} %bitcast.8), calls=%async_computation | async-start | bytes 6291456 | tf_op jit(solution)/shard_map/all_to_all | solution.py:349
  28.6 0.0 copy-start.1
  28.6 0.9 fusion
  29.6 0.0 collective-permute-done
  29.6 0.9 fusion.1
  30.5 0.4 collective-permute-done.1
  30.8 0.9 fusion.2
  31.7 0.0 collective-permute-done.2
  31.7 0.9 fusion.3
  32.7 1.6 %collective-permute-start.3 = (bf16[4,4,32,128]{3,2,1,0:T(8,128)(2,1)S(1)}, bf16[4,4,32,128]{3,2,1,0:T(8,128)(2,1)S(1)}, u32[]{:S(2)}, u32[]{:S(2)}) collective-permute-start(bf16[4,4,32,128]{3,2,1,0:T(8,128)(2,1)S(1)} %pad_maximum_fusion.1), channel_id=1, source_target_pairs={{0,1},{1,0},{8,9},{9,8},{16,17},{17,16},{24,25},{25,24},{2,3},{3,2... | collective-permute-start | bytes 393224 | tf_op jit(solution)/shard_map/ppermute | solution.py:343
  34.2 0.1 collective-permute-start.4
  34.3 0.7 collective-permute-start.5
  35.1 1.6 %collective-permute-start.6 = (bf16[4,4,32,128]{3,2,1,0:T(8,128)(2,1)S(1)}, bf16[4,4,32,128]{3,2,1,0:T(8,128)(2,1)S(1)}, u32[]{:S(2)}, u32[]{:S(2)}) collective-permute-start(bf16[4,4,32,128]{3,2,1,0:T(8,128)(2,1)S(1)} %pad_maximum_fusion.4), channel_id=1, source_target_pairs={{0,16},{1,17},{8,24},{9,25},{16,0},{17,1},{24,8},{25,9},{2,18},{3,... | collective-permute-start | bytes 393224 | tf_op jit(solution)/shard_map/ppermute | solution.py:343
  36.7 1.5 %collective-permute-start.7 = (bf16[4,4,32,128]{3,2,1,0:T(8,128)(2,1)S(1)}, bf16[4,4,32,128]{3,2,1,0:T(8,128)(2,1)S(1)}, u32[]{:S(2)}, u32[]{:S(2)}) collective-permute-start(bf16[4,4,32,128]{3,2,1,0:T(8,128)(2,1)S(1)} %pad_maximum_fusion.5), channel_id=1, source_target_pairs={{0,17},{1,16},{8,25},{9,24},{16,1},{17,0},{24,9},{25,8},{2,19},{3,... | collective-permute-start | bytes 393224 | tf_op jit(solution)/shard_map/ppermute | solution.py:343
  38.2 24.7 %collective-permute-done.3.refs_1_ = bf16[4,4,32,128]{3,2,1,0:T(8,128)(2,1)S(1)} collective-permute-done((bf16[4,4,32,128]{3,2,1,0:T(8,128)(2,1)S(1)}, bf16[4,4,32,128]{3,2,1,0:T(8,128)(2,1)S(1)}, u32[]{:S(2)}, u32[]{:S(2)}) %collective-permute-start.3) | collective-permute-done | bytes 131104 | tf_op jit(solution)/shard_map/ppermute | solution.py:343
  62.9 0.0 collective-permute-start.8
  62.9 0.0 collective-permute-done.4.refs_2_
  62.9 0.3 collective-permute-start.9
  63.2 3.4 %collective-permute-done.5.refs_3_ = bf16[4,4,32,128]{3,2,1,0:T(8,128)(2,1)S(1)} collective-permute-done((bf16[4,4,32,128]{3,2,1,0:T(8,128)(2,1)S(1)}, bf16[4,4,32,128]{3,2,1,0:T(8,128)(2,1)S(1)}, u32[]{:S(2)}, u32[]{:S(2)}) %collective-permute-start.5) | collective-permute-done | bytes 131104 | tf_op jit(solution)/shard_map/ppermute | solution.py:343
  66.6 0.0 collective-permute-done.6.refs_4_
  66.6 6.8 %collective-permute-done.7.refs_5_ = bf16[4,4,32,128]{3,2,1,0:T(8,128)(2,1)S(1)} collective-permute-done((bf16[4,4,32,128]{3,2,1,0:T(8,128)(2,1)S(1)}, bf16[4,4,32,128]{3,2,1,0:T(8,128)(2,1)S(1)}, u32[]{:S(2)}, u32[]{:S(2)}) %collective-permute-start.7) | collective-permute-done | bytes 131104 | tf_op jit(solution)/shard_map/ppermute | solution.py:343
  73.3 5.6 %collective-permute-done.8.refs_6_ = bf16[4,4,32,128]{3,2,1,0:T(8,128)(2,1)S(1)} collective-permute-done((bf16[4,4,32,128]{3,2,1,0:T(8,128)(2,1)S(1)}, bf16[4,4,32,128]{3,2,1,0:T(8,128)(2,1)S(1)}, u32[]{:S(2)}, u32[]{:S(2)}) %collective-permute-start.8) | collective-permute-done | bytes 131104 | tf_op jit(solution)/shard_map/ppermute | solution.py:343
  78.9 0.0 collective-permute-done.9.refs_7_
  78.9 0.0 copy-done.1
  78.9 0.9 shard_map.56.early_ref
  79.8 0.0 copy-start
  79.8 1.0 copy-done
  80.8 22.3 %all-to-all-done.late_ref = bf16[32,3,4,32,128]{4,3,2,1,0:T(8,128)(2,1)S(1)} async-done(((bf16[32,3,4,32,128]{4,3,2,1,0:T(8,128)(2,1)}), bf16[32,3,4,32,128]{4,3,2,1,0:T(8,128)(2,1)S(1)}, u32[]{:S(2)}, u32[]{:S(2)}) %all-to-all-start) | async-done | bytes 3145760 | tf_op jit(solution)/shard_map/all_to_all | solution.py:349
  103.1 3.4 %shard_map.58 = f32[2,16,128,128]{3,2,1,0:T(8,128)} custom-call(bf16[2,256,256]{2,1,0:T(8,128)(2,1)S(1)} %copy-done.1, bf16[32,128,128]{2,1,0:T(8,128)(2,1)} %copy-done, bf16[32,3,4,32,128]{4,3,2,1,0:T(8,128)(2,1)S(1)} %all-to-all-done.late_ref), custom_call_target="tpu_custom_call" | custom-call | flops 1 | bytes 1 | tf_op jit(solution)/shard_map/pallas_call | solution.py:313
  (8 shorter events, 0.2 us)
Async XLA Ops:
  6.1 23.5 %collective-permute-start = (bf16[8,4,32,128]{3,2,1,0:T(8,128)(2,1)}, bf16[8,4,32,128]{3,2,1,0:T(8,128)(2,1)}, u32[]{:S(2)}, u32[]{:S(2)}) collective-permute-start(bf16[8,4,32,128]{3,2,1,0:T(8,128)(2,1)} %get-tuple-element.13), channel_id=1, source_target_pairs={{0,2},{2,0},{4,6},{6,4},{1,3},{3,1},{5,7},{7,5},{8,10},{10,8},{12,... | collective-permute-start | bytes 786440 | tf_op jit(solution)/shard_map/ppermute | solution.py:340
  9.1 21.7 %collective-permute-start.1 = (bf16[8,4,32,128]{3,2,1,0:T(8,128)(2,1)}, bf16[8,4,32,128]{3,2,1,0:T(8,128)(2,1)}, u32[]{:S(2)}, u32[]{:S(2)}) collective-permute-start(bf16[8,4,32,128]{3,2,1,0:T(8,128)(2,1)} %get-tuple-element.14), channel_id=1, source_target_pairs={{0,4},{2,6},{4,0},{6,2},{1,5},{3,7},{5,1},{7,3},{8,12},{10,14},{12... | collective-permute-start | bytes 786440 | tf_op jit(solution)/shard_map/ppermute | solution.py:340
  11.7 20.0 %collective-permute-start.2 = (bf16[8,4,32,128]{3,2,1,0:T(8,128)(2,1)}, bf16[8,4,32,128]{3,2,1,0:T(8,128)(2,1)}, u32[]{:S(2)}, u32[]{:S(2)}) collective-permute-start(bf16[8,4,32,128]{3,2,1,0:T(8,128)(2,1)} %get-tuple-element.15), channel_id=1, source_target_pairs={{0,6},{2,4},{4,2},{6,0},{1,7},{3,5},{5,3},{7,1},{8,14},{10,12},{12... | collective-permute-start | bytes 786440 | tf_op jit(solution)/shard_map/ppermute | solution.py:340
  22.5 80.6 %all-to-all-start = ((bf16[32,3,4,32,128]{4,3,2,1,0:T(8,128)(2,1)}), bf16[32,3,4,32,128]{4,3,2,1,0:T(8,128)(2,1)S(1)}, u32[]{:S(2)}, u32[]{:S(2)}) async-start(bf16[32,3,4,32,128]{4,3,2,1,0:T(8,128)(2,1)} %bitcast.8), calls=%async_computation | async-start | bytes 6291456 | tf_op jit(solution)/shard_map/all_to_all | solution.py:349
  28.6 50.3 %copy-start.1 = (bf16[2,256,256]{2,1,0:T(8,128)(2,1)S(1)}, bf16[2,256,256]{2,1,0:T(8,128)(2,1)}, u32[]{:S(2)}) copy-start(bf16[2,256,256]{2,1,0:T(8,128)(2,1)} %constant.5.clone.order_ref) | copy-start | bytes 786436
  32.7 30.2 %collective-permute-start.3 = (bf16[4,4,32,128]{3,2,1,0:T(8,128)(2,1)S(1)}, bf16[4,4,32,128]{3,2,1,0:T(8,128)(2,1)S(1)}, u32[]{:S(2)}, u32[]{:S(2)}) collective-permute-start(bf16[4,4,32,128]{3,2,1,0:T(8,128)(2,1)S(1)} %pad_maximum_fusion.1), channel_id=1, source_target_pairs={{0,1},{1,0},{8,9},{9,8},{16,17},{17,16},{24,25},{25,24},{2,3},{3,2... | collective-permute-start | bytes 393224 | tf_op jit(solution)/shard_map/ppermute | solution.py:343
  34.2 28.6 %collective-permute-start.4 = (bf16[4,4,32,128]{3,2,1,0:T(8,128)(2,1)S(1)}, bf16[4,4,32,128]{3,2,1,0:T(8,128)(2,1)S(1)}, u32[]{:S(2)}, u32[]{:S(2)}) collective-permute-start(bf16[4,4,32,128]{3,2,1,0:T(8,128)(2,1)S(1)} %pad_maximum_fusion.2), channel_id=1, source_target_pairs={{0,8},{1,9},{8,0},{9,1},{16,24},{17,25},{24,16},{25,17},{2,10},{3,... | collective-permute-start | bytes 393224 | tf_op jit(solution)/shard_map/ppermute | solution.py:343
  34.3 32.2 %collective-permute-start.5 = (bf16[4,4,32,128]{3,2,1,0:T(8,128)(2,1)S(1)}, bf16[4,4,32,128]{3,2,1,0:T(8,128)(2,1)S(1)}, u32[]{:S(2)}, u32[]{:S(2)}) collective-permute-start(bf16[4,4,32,128]{3,2,1,0:T(8,128)(2,1)S(1)} %pad_maximum_fusion.3), channel_id=1, source_target_pairs={{0,9},{1,8},{8,1},{9,0},{16,25},{17,24},{24,17},{25,16},{2,11},{3,... | collective-permute-start | bytes 393224 | tf_op jit(solution)/shard_map/ppermute | solution.py:343
  35.1 31.5 %collective-permute-start.6 = (bf16[4,4,32,128]{3,2,1,0:T(8,128)(2,1)S(1)}, bf16[4,4,32,128]{3,2,1,0:T(8,128)(2,1)S(1)}, u32[]{:S(2)}, u32[]{:S(2)}) collective-permute-start(bf16[4,4,32,128]{3,2,1,0:T(8,128)(2,1)S(1)} %pad_maximum_fusion.4), channel_id=1, source_target_pairs={{0,16},{1,17},{8,24},{9,25},{16,0},{17,1},{24,8},{25,9},{2,18},{3,... | collective-permute-start | bytes 393224 | tf_op jit(solution)/shard_map/ppermute | solution.py:343
  36.7 36.7 %collective-permute-start.7 = (bf16[4,4,32,128]{3,2,1,0:T(8,128)(2,1)S(1)}, bf16[4,4,32,128]{3,2,1,0:T(8,128)(2,1)S(1)}, u32[]{:S(2)}, u32[]{:S(2)}) collective-permute-start(bf16[4,4,32,128]{3,2,1,0:T(8,128)(2,1)S(1)} %pad_maximum_fusion.5), channel_id=1, source_target_pairs={{0,17},{1,16},{8,25},{9,24},{16,1},{17,0},{24,9},{25,8},{2,19},{3,... | collective-permute-start | bytes 393224 | tf_op jit(solution)/shard_map/ppermute | solution.py:343
  62.9 16.0 %collective-permute-start.8 = (bf16[4,4,32,128]{3,2,1,0:T(8,128)(2,1)S(1)}, bf16[4,4,32,128]{3,2,1,0:T(8,128)(2,1)S(1)}, u32[]{:S(2)}, u32[]{:S(2)}) collective-permute-start(bf16[4,4,32,128]{3,2,1,0:T(8,128)(2,1)S(1)} %pad_maximum_fusion.6), channel_id=1, source_target_pairs={{0,24},{1,25},{8,16},{9,17},{16,8},{17,9},{24,0},{25,1},{2,26},{3,... | collective-permute-start | bytes 393224 | tf_op jit(solution)/shard_map/ppermute | solution.py:343
  62.9 16.0 %collective-permute-start.9 = (bf16[4,4,32,128]{3,2,1,0:T(8,128)(2,1)S(1)}, bf16[4,4,32,128]{3,2,1,0:T(8,128)(2,1)S(1)}, u32[]{:S(2)}, u32[]{:S(2)}) collective-permute-start(bf16[4,4,32,128]{3,2,1,0:T(8,128)(2,1)S(1)} %pad_maximum_fusion.7), channel_id=1, source_target_pairs={{0,25},{1,24},{8,17},{9,16},{16,9},{17,8},{24,1},{25,0},{2,27},{3,... | collective-permute-start | bytes 393224 | tf_op jit(solution)/shard_map/ppermute | solution.py:343
  79.8 1.0 copy-start

commit v7 on v6

--- a/solution.py
+++ b/solution.py
@@ -69,7 +69,7 @@
 
 
 def filter_kernel(radix, rows, far, first, blocks, apart, x_ref, taps_ref, table_ref, *refs):
-    outs, (f_ref, turn_ref, taps_f_ref, w_ref, held_ref, table_sem, x_sem) = refs[:-7], refs[-7:]
+    outs, (f_ref, taps_f_ref, w_ref, held_ref, table_sem, x_sem) = refs[:-6], refs[-6:]
     wide = TILES * rows
     step = pl.program_id(0)
     slot = lax.rem(step, 2)
@@ -169,9 +169,8 @@
                 ]
                 block = jnp.concatenate(part, 1).astype(jnp.bfloat16)
                 if apart:
-                    turn_ref[k, i] = block
-                    for r in range(block.shape[0]):
-                        outs[k][r, i] = turn_ref[k, i, me_near ^ r]
+                    for p in range(block.shape[0]):
+                        outs[k][me_near ^ p, i] = block[p]
                 else:
                     groups, _, near_size = outs[0].shape[:3]
                     outs[0][:, k, :, 0, i] = block.reshape(groups, near_size, *block.shape[1:])
@@ -203,7 +202,6 @@
         out_specs=out_specs,
         scratch_shapes=[
             pltpu.VMEM((BLOCK, wide + 8, LANES), jnp.float32),
-            pltpu.VMEM((far, rows, near, parts, BLOCK), jnp.bfloat16),
             pltpu.VMEM((TAPS, wide, LANES), jnp.float32),
             pltpu.VMEM(table.shape, table.dtype),
             pltpu.VMEM((2, BLOCK + TAPS - 1, wide, LANES), jnp.int32),

time: 107 us -> 107 us (level)
  no operation moved by 1% of the time
where the time goes in v7:
time: 107 us; the launch traced here: 106 us
  waiting for transfers between devices  62.9 us (59%)
  Pallas kernels  21 us (20%)
  starting transfers between devices  17.5 us (16%)
  local copies, waits for them, and re-layouts  4.62 us (4%)
    ppermute x7, waiting for transfers between devices, swap(): return lax.ppermute(x, ('grp', 'near'), [(a, a ^ r) for a in range(near)])  40.4 us
    all_to_all x1, waiting for transfers between devices, local(): lax.all_to_all(late, ('grp', 'far', 'near'), split_axis=0, concat_axis=0,...  22.2 us
    pallas_call x2, Pallas kernels, channelise(): pl.pallas_call(functools.partial(filter_kernel, radix, rows, far, first,...  16.7 us
    all_to_all x1, starting transfers between devices, local(): lax.all_to_all(late, ('grp', 'far', 'near'), split_axis=0, concat_axis=0,...  6.07 us
    ppermute x7, starting transfers between devices, swap(): return lax.ppermute(x, ('grp', 'near'), [(a, a ^ r) for a in range(near)])  5.74 us
    ppermute x3, starting transfers between devices, cross(): return lax.ppermute(x, 'far', [(a, a ^ k) for a in range(far)])  5.68 us
    slice x4, local copies, waits for them, and re-layouts, local(): crossed[k][r]  3.62 us
    pallas_call x1, Pallas kernels, correlate(): pl.pallas_call(functools.partial(gram_kernel, radix_of(ch_dev), ch_dev, r...  3.42 us
  transfers between devices with their start and end apart: 11, of which 6 were waited for; matrix products, arithmetic and copies ran while one was open for 4% of the time, Pallas kernels for 11%

profile of v7, /device:TPU:0, one launch (start us, length us, event | category | flops | bytes accessed | tf_op | source)
XLA Modules:
  0.0 106.3 jit_solution(8203487705258024619)
XLA Ops:
  0.0 5.9 %shard_map.55 = (bf16[8,4,32,128]{3,2,1,0:T(8,128)(2,1)}, bf16[8,4,32,128]{3,2,1,0:T(8,128)(2,1)}, bf16[8,4,32,128]{3,2,1,0:T(8,128)(2,1)}, bf16[8,4,32,128]{3,2,1,0:T(8,128)(2,1)}) custom-call(s32[515,32,128]{2,1,0:T(8,128)} %bitcast.6, s32[4,1024]{1,0:T(4,128)} %taps_ref.3, bf16[2,6,4,64,256]{4,3,2,1,0:T(8,128)(2,1)} %constant.4.clone.table_ref), custom_call_target="tpu_custom_call" | custom-call | flops 1 | bytes 1 | tf_op jit(solution)/shard_map/pallas_call | solution.py:193
  5.9 3.1 %collective-permute-start = (bf16[8,4,32,128]{3,2,1,0:T(8,128)(2,1)}, bf16[8,4,32,128]{3,2,1,0:T(8,128)(2,1)}, u32[]{:S(2)}, u32[]{:S(2)}) collective-permute-start(bf16[8,4,32,128]{3,2,1,0:T(8,128)(2,1)} %get-tuple-element.13), channel_id=1, source_target_pairs={{0,2},{2,0},{4,6},{6,4},{1,3},{3,1},{5,7},{7,5},{8,10},{10,8},{12,... | collective-permute-start | bytes 786440 | tf_op jit(solution)/shard_map/ppermute | solution.py:338
  9.0 2.6 %collective-permute-start.1 = (bf16[8,4,32,128]{3,2,1,0:T(8,128)(2,1)}, bf16[8,4,32,128]{3,2,1,0:T(8,128)(2,1)}, u32[]{:S(2)}, u32[]{:S(2)}) collective-permute-start(bf16[8,4,32,128]{3,2,1,0:T(8,128)(2,1)} %get-tuple-element.14), channel_id=1, source_target_pairs={{0,4},{2,6},{4,0},{6,2},{1,5},{3,7},{5,1},{7,3},{8,12},{10,14},{12... | collective-permute-start | bytes 786440 | tf_op jit(solution)/shard_map/ppermute | solution.py:338
  11.6 0.0 collective-permute-start.2
  11.6 10.8 %shard_map.57 = bf16[4,4,2,3,4,32,128]{6,5,4,3,2,1,0:T(8,128)(2,1)} custom-call(s32[515,32,128]{2,1,0:T(8,128)} %bitcast.7, s32[4,1024]{1,0:T(4,128)} %taps_ref.3, bf16[2,6,4,64,256]{4,3,2,1,0:T(8,128)(2,1)} %constant.4.clone.table_ref), custom_call_target="tpu_custom_call" | custom-call | flops 1 | bytes 1 | tf_op jit(solution)/shard_map/pallas_call | solution.py:193
  22.4 6.1 %all-to-all-start = ((bf16[32,3,4,32,128]{4,3,2,1,0:T(8,128)(2,1)}), bf16[32,3,4,32,128]{4,3,2,1,0:T(8,128)(2,1)S(1)}, u32[]{:S(2)}, u32[]{:S(2)}) async-start(bf16[32,3,4,32,128]{4,3,2,1,0:T(8,128)(2,1)} %bitcast.8), calls=%async_computation | async-start | bytes 6291456 | tf_op jit(solution)/shard_map/all_to_all | solution.py:347
  28.5 0.0 copy-start.1
  28.5 0.9 fusion
  29.4 0.0 collective-permute-done
  29.4 0.9 fusion.1
  30.3 0.4 collective-permute-done.1
  30.7 0.9 fusion.2
  31.6 0.0 collective-permute-done.2
  31.6 0.9 fusion.3
  32.5 1.6 %collective-permute-start.3 = (bf16[4,4,32,128]{3,2,1,0:T(8,128)(2,1)S(1)}, bf16[4,4,32,128]{3,2,1,0:T(8,128)(2,1)S(1)}, u32[]{:S(2)}, u32[]{:S(2)}) collective-permute-start(bf16[4,4,32,128]{3,2,1,0:T(8,128)(2,1)S(1)} %pad_maximum_fusion.1), channel_id=1, source_target_pairs={{0,1},{1,0},{8,9},{9,8},{16,17},{17,16},{24,25},{25,24},{2,3},{3,2... | collective-permute-start | bytes 393224 | tf_op jit(solution)/shard_map/ppermute | solution.py:341
  34.1 0.1 collective-permute-start.4
  34.2 0.7 collective-permute-start.5
  35.0 1.6 %collective-permute-start.6 = (bf16[4,4,32,128]{3,2,1,0:T(8,128)(2,1)S(1)}, bf16[4,4,32,128]{3,2,1,0:T(8,128)(2,1)S(1)}, u32[]{:S(2)}, u32[]{:S(2)}) collective-permute-start(bf16[4,4,32,128]{3,2,1,0:T(8,128)(2,1)S(1)} %pad_maximum_fusion.4), channel_id=1, source_target_pairs={{0,16},{1,17},{8,24},{9,25},{16,0},{17,1},{24,8},{25,9},{2,18},{3,... | collective-permute-start | bytes 393224 | tf_op jit(solution)/shard_map/ppermute | solution.py:341
  36.6 1.5 %collective-permute-start.7 = (bf16[4,4,32,128]{3,2,1,0:T(8,128)(2,1)S(1)}, bf16[4,4,32,128]{3,2,1,0:T(8,128)(2,1)S(1)}, u32[]{:S(2)}, u32[]{:S(2)}) collective-permute-start(bf16[4,4,32,128]{3,2,1,0:T(8,128)(2,1)S(1)} %pad_maximum_fusion.5), channel_id=1, source_target_pairs={{0,17},{1,16},{8,25},{9,24},{16,1},{17,0},{24,9},{25,8},{2,19},{3,... | collective-permute-start | bytes 393224 | tf_op jit(solution)/shard_map/ppermute | solution.py:341
  38.1 24.6 %collective-permute-done.3.refs_1_ = bf16[4,4,32,128]{3,2,1,0:T(8,128)(2,1)S(1)} collective-permute-done((bf16[4,4,32,128]{3,2,1,0:T(8,128)(2,1)S(1)}, bf16[4,4,32,128]{3,2,1,0:T(8,128)(2,1)S(1)}, u32[]{:S(2)}, u32[]{:S(2)}) %collective-permute-start.3) | collective-permute-done | bytes 131104 | tf_op jit(solution)/shard_map/ppermute | solution.py:341
  62.7 0.0 collective-permute-start.8
  62.7 0.0 collective-permute-done.4.refs_2_
  62.7 0.3 collective-permute-start.9
  63.1 3.4 %collective-permute-done.5.refs_3_ = bf16[4,4,32,128]{3,2,1,0:T(8,128)(2,1)S(1)} collective-permute-done((bf16[4,4,32,128]{3,2,1,0:T(8,128)(2,1)S(1)}, bf16[4,4,32,128]{3,2,1,0:T(8,128)(2,1)S(1)}, u32[]{:S(2)}, u32[]{:S(2)}) %collective-permute-start.5) | collective-permute-done | bytes 131104 | tf_op jit(solution)/shard_map/ppermute | solution.py:341
  66.4 0.0 collective-permute-done.6.refs_4_
  66.4 6.8 %collective-permute-done.7.refs_5_ = bf16[4,4,32,128]{3,2,1,0:T(8,128)(2,1)S(1)} collective-permute-done((bf16[4,4,32,128]{3,2,1,0:T(8,128)(2,1)S(1)}, bf16[4,4,32,128]{3,2,1,0:T(8,128)(2,1)S(1)}, u32[]{:S(2)}, u32[]{:S(2)}) %collective-permute-start.7) | collective-permute-done | bytes 131104 | tf_op jit(solution)/shard_map/ppermute | solution.py:341
  73.2 5.6 %collective-permute-done.8.refs_6_ = bf16[4,4,32,128]{3,2,1,0:T(8,128)(2,1)S(1)} collective-permute-done((bf16[4,4,32,128]{3,2,1,0:T(8,128)(2,1)S(1)}, bf16[4,4,32,128]{3,2,1,0:T(8,128)(2,1)S(1)}, u32[]{:S(2)}, u32[]{:S(2)}) %collective-permute-start.8) | collective-permute-done | bytes 131104 | tf_op jit(solution)/shard_map/ppermute | solution.py:341
  78.8 0.0 collective-permute-done.9.refs_7_
  78.8 0.0 copy-done.1
  78.8 0.9 shard_map.56.early_ref
  79.7 0.0 copy-start
  79.7 1.0 copy-done
  80.7 22.2 %all-to-all-done.late_ref = bf16[32,3,4,32,128]{4,3,2,1,0:T(8,128)(2,1)S(1)} async-done(((bf16[32,3,4,32,128]{4,3,2,1,0:T(8,128)(2,1)}), bf16[32,3,4,32,128]{4,3,2,1,0:T(8,128)(2,1)S(1)}, u32[]{:S(2)}, u32[]{:S(2)}) %all-to-all-start) | async-done | bytes 3145760 | tf_op jit(solution)/shard_map/all_to_all | solution.py:347
  102.9 3.4 %shard_map.58 = f32[2,16,128,128]{3,2,1,0:T(8,128)} custom-call(bf16[2,256,256]{2,1,0:T(8,128)(2,1)S(1)} %copy-done.1, bf16[32,128,128]{2,1,0:T(8,128)(2,1)} %copy-done, bf16[32,3,4,32,128]{4,3,2,1,0:T(8,128)(2,1)S(1)} %all-to-all-done.late_ref), custom_call_target="tpu_custom_call" | custom-call | flops 1 | bytes 1 | tf_op jit(solution)/shard_map/pallas_call | solution.py:311
  (8 shorter events, 0.2 us)
Async XLA Ops:
  5.9 23.5 %collective-permute-start = (bf16[8,4,32,128]{3,2,1,0:T(8,128)(2,1)}, bf16[8,4,32,128]{3,2,1,0:T(8,128)(2,1)}, u32[]{:S(2)}, u32[]{:S(2)}) collective-permute-start(bf16[8,4,32,128]{3,2,1,0:T(8,128)(2,1)} %get-tuple-element.13), channel_id=1, source_target_pairs={{0,2},{2,0},{4,6},{6,4},{1,3},{3,1},{5,7},{7,5},{8,10},{10,8},{12,... | collective-permute-start | bytes 786440 | tf_op jit(solution)/shard_map/ppermute | solution.py:338
  9.0 21.7 %collective-permute-start.1 = (bf16[8,4,32,128]{3,2,1,0:T(8,128)(2,1)}, bf16[8,4,32,128]{3,2,1,0:T(8,128)(2,1)}, u32[]{:S(2)}, u32[]{:S(2)}) collective-permute-start(bf16[8,4,32,128]{3,2,1,0:T(8,128)(2,1)} %get-tuple-element.14), channel_id=1, source_target_pairs={{0,4},{2,6},{4,0},{6,2},{1,5},{3,7},{5,1},{7,3},{8,12},{10,14},{12... | collective-permute-start | bytes 786440 | tf_op jit(solution)/shard_map/ppermute | solution.py:338
  11.6 20.0 %collective-permute-start.2 = (bf16[8,4,32,128]{3,2,1,0:T(8,128)(2,1)}, bf16[8,4,32,128]{3,2,1,0:T(8,128)(2,1)}, u32[]{:S(2)}, u32[]{:S(2)}) collective-permute-start(bf16[8,4,32,128]{3,2,1,0:T(8,128)(2,1)} %get-tuple-element.15), channel_id=1, source_target_pairs={{0,6},{2,4},{4,2},{6,0},{1,7},{3,5},{5,3},{7,1},{8,14},{10,12},{12... | collective-permute-start | bytes 786440 | tf_op jit(solution)/shard_map/ppermute | solution.py:338
  22.4 80.5 %all-to-all-start = ((bf16[32,3,4,32,128]{4,3,2,1,0:T(8,128)(2,1)}), bf16[32,3,4,32,128]{4,3,2,1,0:T(8,128)(2,1)S(1)}, u32[]{:S(2)}, u32[]{:S(2)}) async-start(bf16[32,3,4,32,128]{4,3,2,1,0:T(8,128)(2,1)} %bitcast.8), calls=%async_computation | async-start | bytes 6291456 | tf_op jit(solution)/shard_map/all_to_all | solution.py:347
  28.5 50.4 %copy-start.1 = (bf16[2,256,256]{2,1,0:T(8,128)(2,1)S(1)}, bf16[2,256,256]{2,1,0:T(8,128)(2,1)}, u32[]{:S(2)}) copy-start(bf16[2,256,256]{2,1,0:T(8,128)(2,1)} %constant.5.clone.order_ref) | copy-start | bytes 786436
  32.5 30.2 %collective-permute-start.3 = (bf16[4,4,32,128]{3,2,1,0:T(8,128)(2,1)S(1)}, bf16[4,4,32,128]{3,2,1,0:T(8,128)(2,1)S(1)}, u32[]{:S(2)}, u32[]{:S(2)}) collective-permute-start(bf16[4,4,32,128]{3,2,1,0:T(8,128)(2,1)S(1)} %pad_maximum_fusion.1), channel_id=1, source_target_pairs={{0,1},{1,0},{8,9},{9,8},{16,17},{17,16},{24,25},{25,24},{2,3},{3,2... | collective-permute-start | bytes 393224 | tf_op jit(solution)/shard_map/ppermute | solution.py:341
  34.1 28.6 %collective-permute-start.4 = (bf16[4,4,32,128]{3,2,1,0:T(8,128)(2,1)S(1)}, bf16[4,4,32,128]{3,2,1,0:T(8,128)(2,1)S(1)}, u32[]{:S(2)}, u32[]{:S(2)}) collective-permute-start(bf16[4,4,32,128]{3,2,1,0:T(8,128)(2,1)S(1)} %pad_maximum_fusion.2), channel_id=1, source_target_pairs={{0,8},{1,9},{8,0},{9,1},{16,24},{17,25},{24,16},{25,17},{2,10},{3,... | collective-permute-start | bytes 393224 | tf_op jit(solution)/shard_map/ppermute | solution.py:341
  34.2 32.2 %collective-permute-start.5 = (bf16[4,4,32,128]{3,2,1,0:T(8,128)(2,1)S(1)}, bf16[4,4,32,128]{3,2,1,0:T(8,128)(2,1)S(1)}, u32[]{:S(2)}, u32[]{:S(2)}) collective-permute-start(bf16[4,4,32,128]{3,2,1,0:T(8,128)(2,1)S(1)} %pad_maximum_fusion.3), channel_id=1, source_target_pairs={{0,9},{1,8},{8,1},{9,0},{16,25},{17,24},{24,17},{25,16},{2,11},{3,... | collective-permute-start | bytes 393224 | tf_op jit(solution)/shard_map/ppermute | solution.py:341
  35.0 31.5 %collective-permute-start.6 = (bf16[4,4,32,128]{3,2,1,0:T(8,128)(2,1)S(1)}, bf16[4,4,32,128]{3,2,1,0:T(8,128)(2,1)S(1)}, u32[]{:S(2)}, u32[]{:S(2)}) collective-permute-start(bf16[4,4,32,128]{3,2,1,0:T(8,128)(2,1)S(1)} %pad_maximum_fusion.4), channel_id=1, source_target_pairs={{0,16},{1,17},{8,24},{9,25},{16,0},{17,1},{24,8},{25,9},{2,18},{3,... | collective-permute-start | bytes 393224 | tf_op jit(solution)/shard_map/ppermute | solution.py:341
  36.6 36.7 %collective-permute-start.7 = (bf16[4,4,32,128]{3,2,1,0:T(8,128)(2,1)S(1)}, bf16[4,4,32,128]{3,2,1,0:T(8,128)(2,1)S(1)}, u32[]{:S(2)}, u32[]{:S(2)}) collective-permute-start(bf16[4,4,32,128]{3,2,1,0:T(8,128)(2,1)S(1)} %pad_maximum_fusion.5), channel_id=1, source_target_pairs={{0,17},{1,16},{8,25},{9,24},{16,1},{17,0},{24,9},{25,8},{2,19},{3,... | collective-permute-start | bytes 393224 | tf_op jit(solution)/shard_map/ppermute | solution.py:341
  62.7 16.1 %collective-permute-start.8 = (bf16[4,4,32,128]{3,2,1,0:T(8,128)(2,1)S(1)}, bf16[4,4,32,128]{3,2,1,0:T(8,128)(2,1)S(1)}, u32[]{:S(2)}, u32[]{:S(2)}) collective-permute-start(bf16[4,4,32,128]{3,2,1,0:T(8,128)(2,1)S(1)} %pad_maximum_fusion.6), channel_id=1, source_target_pairs={{0,24},{1,25},{8,16},{9,17},{16,8},{17,9},{24,0},{25,1},{2,26},{3,... | collective-permute-start | bytes 393224 | tf_op jit(solution)/shard_map/ppermute | solution.py:341
  62.7 16.1 %collective-permute-start.9 = (bf16[4,4,32,128]{3,2,1,0:T(8,128)(2,1)S(1)}, bf16[4,4,32,128]{3,2,1,0:T(8,128)(2,1)S(1)}, u32[]{:S(2)}, u32[]{:S(2)}) collective-permute-start(bf16[4,4,32,128]{3,2,1,0:T(8,128)(2,1)S(1)} %pad_maximum_fusion.7), channel_id=1, source_target_pairs={{0,25},{1,24},{8,17},{9,16},{16,9},{17,8},{24,1},{25,0},{2,27},{3,... | collective-permute-start | bytes 393224 | tf_op jit(solution)/shard_map/ppermute | solution.py:341
  79.7 1.0 copy-start

commit v8 on v7

--- a/solution.py
+++ b/solution.py
@@ -21,7 +21,7 @@
 BLOCK = 128
 EARLY = 1
 HEAD_FLOPS = 5 * 10**10
-GROUP = 4
+GROUP = 2
 STEP = 8
 PIECES = 2
 HEAD_VMEM = 32 << 20

time: 107 us -> 107 us (level)
  no operation moved by 1% of the time
where the time goes in v8:
time: 107 us; the launch traced here: 106 us
  waiting for transfers between devices  62.9 us (59%)
  Pallas kernels  20.9 us (20%)
  starting transfers between devices  17.5 us (16%)
  local copies, waits for them, and re-layouts  4.62 us (4%)
    ppermute x7, waiting for transfers between devices, swap(): return lax.ppermute(x, ('grp', 'near'), [(a, a ^ r) for a in range(near)])  40.4 us
    all_to_all x1, waiting for transfers between devices, local(): lax.all_to_all(late, ('grp', 'far', 'near'), split_axis=0, concat_axis=0,...  22.2 us
    pallas_call x2, Pallas kernels, channelise(): pl.pallas_call(functools.partial(filter_kernel, radix, rows, far, first,...  16.7 us
    all_to_all x1, starting transfers between devices, local(): lax.all_to_all(late, ('grp', 'far', 'near'), split_axis=0, concat_axis=0,...  6.07 us
    ppermute x7, starting transfers between devices, swap(): return lax.ppermute(x, ('grp', 'near'), [(a, a ^ r) for a in range(near)])  5.74 us
    ppermute x3, starting transfers between devices, cross(): return lax.ppermute(x, 'far', [(a, a ^ k) for a in range(far)])  5.68 us
    slice x4, local copies, waits for them, and re-layouts, local(): crossed[k][r]  3.62 us
    pallas_call x1, Pallas kernels, correlate(): pl.pallas_call(functools.partial(gram_kernel, radix_of(ch_dev), ch_dev, r...  3.36 us
  transfers between devices with their start and end apart: 11, of which 6 were waited for; matrix products, arithmetic and copies ran while one was open for 4% of the time, Pallas kernels for 11%

profile of v8, /device:TPU:0, one launch (start us, length us, event | category | flops | bytes accessed | tf_op | source)
XLA Modules:
  0.0 106.3 jit_solution(3783566860793700709)
XLA Ops:
  0.0 5.9 %shard_map.55 = (bf16[8,4,32,128]{3,2,1,0:T(8,128)(2,1)}, bf16[8,4,32,128]{3,2,1,0:T(8,128)(2,1)}, bf16[8,4,32,128]{3,2,1,0:T(8,128)(2,1)}, bf16[8,4,32,128]{3,2,1,0:T(8,128)(2,1)}) custom-call(s32[515,32,128]{2,1,0:T(8,128)} %bitcast.6, s32[4,1024]{1,0:T(4,128)} %taps_ref.3, bf16[2,6,4,64,256]{4,3,2,1,0:T(8,128)(2,1)} %constant.4.clone.table_ref), custom_call_target="tpu_custom_call" | custom-call | flops 1 | bytes 1 | tf_op jit(solution)/shard_map/pallas_call | solution.py:193
  5.9 3.1 %collective-permute-start = (bf16[8,4,32,128]{3,2,1,0:T(8,128)(2,1)}, bf16[8,4,32,128]{3,2,1,0:T(8,128)(2,1)}, u32[]{:S(2)}, u32[]{:S(2)}) collective-permute-start(bf16[8,4,32,128]{3,2,1,0:T(8,128)(2,1)} %get-tuple-element.13), channel_id=1, source_target_pairs={{0,2},{2,0},{4,6},{6,4},{1,3},{3,1},{5,7},{7,5},{8,10},{10,8},{12,... | collective-permute-start | bytes 786440 | tf_op jit(solution)/shard_map/ppermute | solution.py:338
  9.0 2.6 %collective-permute-start.1 = (bf16[8,4,32,128]{3,2,1,0:T(8,128)(2,1)}, bf16[8,4,32,128]{3,2,1,0:T(8,128)(2,1)}, u32[]{:S(2)}, u32[]{:S(2)}) collective-permute-start(bf16[8,4,32,128]{3,2,1,0:T(8,128)(2,1)} %get-tuple-element.14), channel_id=1, source_target_pairs={{0,4},{2,6},{4,0},{6,2},{1,5},{3,7},{5,1},{7,3},{8,12},{10,14},{12... | collective-permute-start | bytes 786440 | tf_op jit(solution)/shard_map/ppermute | solution.py:338
  11.6 0.0 collective-permute-start.2
  11.6 10.8 %shard_map.57 = bf16[4,4,2,3,4,32,128]{6,5,4,3,2,1,0:T(8,128)(2,1)} custom-call(s32[515,32,128]{2,1,0:T(8,128)} %bitcast.7, s32[4,1024]{1,0:T(4,128)} %taps_ref.3, bf16[2,6,4,64,256]{4,3,2,1,0:T(8,128)(2,1)} %constant.4.clone.table_ref), custom_call_target="tpu_custom_call" | custom-call | flops 1 | bytes 1 | tf_op jit(solution)/shard_map/pallas_call | solution.py:193
  22.4 6.1 %all-to-all-start = ((bf16[32,3,4,32,128]{4,3,2,1,0:T(8,128)(2,1)}), bf16[32,3,4,32,128]{4,3,2,1,0:T(8,128)(2,1)S(1)}, u32[]{:S(2)}, u32[]{:S(2)}) async-start(bf16[32,3,4,32,128]{4,3,2,1,0:T(8,128)(2,1)} %bitcast.8), calls=%async_computation | async-start | bytes 6291456 | tf_op jit(solution)/shard_map/all_to_all | solution.py:347
  28.5 0.0 copy-start.1
  28.5 0.9 fusion
  29.4 0.0 collective-permute-done
  29.4 0.9 fusion.1
  30.3 0.4 collective-permute-done.1
  30.7 0.9 fusion.2
  31.6 0.0 collective-permute-done.2
  31.6 0.9 fusion.3
  32.5 1.6 %collective-permute-start.3 = (bf16[4,4,32,128]{3,2,1,0:T(8,128)(2,1)S(1)}, bf16[4,4,32,128]{3,2,1,0:T(8,128)(2,1)S(1)}, u32[]{:S(2)}, u32[]{:S(2)}) collective-permute-start(bf16[4,4,32,128]{3,2,1,0:T(8,128)(2,1)S(1)} %pad_maximum_fusion.1), channel_id=1, source_target_pairs={{0,1},{1,0},{8,9},{9,8},{16,17},{17,16},{24,25},{25,24},{2,3},{3,2... | collective-permute-start | bytes 393224 | tf_op jit(solution)/shard_map/ppermute | solution.py:341
  34.1 0.1 collective-permute-start.4
  34.2 0.7 collective-permute-start.5
  35.0 1.6 %collective-permute-start.6 = (bf16[4,4,32,128]{3,2,1,0:T(8,128)(2,1)S(1)}, bf16[4,4,32,128]{3,2,1,0:T(8,128)(2,1)S(1)}, u32[]{:S(2)}, u32[]{:S(2)}) collective-permute-start(bf16[4,4,32,128]{3,2,1,0:T(8,128)(2,1)S(1)} %pad_maximum_fusion.4), channel_id=1, source_target_pairs={{0,16},{1,17},{8,24},{9,25},{16,0},{17,1},{24,8},{25,9},{2,18},{3,... | collective-permute-start | bytes 393224 | tf_op jit(solution)/shard_map/ppermute | solution.py:341
  36.6 1.5 %collective-permute-start.7 = (bf16[4,4,32,128]{3,2,1,0:T(8,128)(2,1)S(1)}, bf16[4,4,32,128]{3,2,1,0:T(8,128)(2,1)S(1)}, u32[]{:S(2)}, u32[]{:S(2)}) collective-permute-start(bf16[4,4,32,128]{3,2,1,0:T(8,128)(2,1)S(1)} %pad_maximum_fusion.5), channel_id=1, source_target_pairs={{0,17},{1,16},{8,25},{9,24},{16,1},{17,0},{24,9},{25,8},{2,19},{3,... | collective-permute-start | bytes 393224 | tf_op jit(solution)/shard_map/ppermute | solution.py:341
  38.1 24.6 %collective-permute-done.3.refs_1_ = bf16[4,4,32,128]{3,2,1,0:T(8,128)(2,1)S(1)} collective-permute-done((bf16[4,4,32,128]{3,2,1,0:T(8,128)(2,1)S(1)}, bf16[4,4,32,128]{3,2,1,0:T(8,128)(2,1)S(1)}, u32[]{:S(2)}, u32[]{:S(2)}) %collective-permute-start.3) | collective-permute-done | bytes 131104 | tf_op jit(solution)/shard_map/ppermute | solution.py:341
  62.7 0.0 collective-permute-start.8
  62.7 0.0 collective-permute-done.4.refs_2_
  62.7 0.3 collective-permute-start.9
  63.1 3.4 %collective-permute-done.5.refs_3_ = bf16[4,4,32,128]{3,2,1,0:T(8,128)(2,1)S(1)} collective-permute-done((bf16[4,4,32,128]{3,2,1,0:T(8,128)(2,1)S(1)}, bf16[4,4,32,128]{3,2,1,0:T(8,128)(2,1)S(1)}, u32[]{:S(2)}, u32[]{:S(2)}) %collective-permute-start.5) | collective-permute-done | bytes 131104 | tf_op jit(solution)/shard_map/ppermute | solution.py:341
  66.4 0.0 collective-permute-done.6.refs_4_
  66.4 6.8 %collective-permute-done.7.refs_5_ = bf16[4,4,32,128]{3,2,1,0:T(8,128)(2,1)S(1)} collective-permute-done((bf16[4,4,32,128]{3,2,1,0:T(8,128)(2,1)S(1)}, bf16[4,4,32,128]{3,2,1,0:T(8,128)(2,1)S(1)}, u32[]{:S(2)}, u32[]{:S(2)}) %collective-permute-start.7) | collective-permute-done | bytes 131104 | tf_op jit(solution)/shard_map/ppermute | solution.py:341
  73.2 5.6 %collective-permute-done.8.refs_6_ = bf16[4,4,32,128]{3,2,1,0:T(8,128)(2,1)S(1)} collective-permute-done((bf16[4,4,32,128]{3,2,1,0:T(8,128)(2,1)S(1)}, bf16[4,4,32,128]{3,2,1,0:T(8,128)(2,1)S(1)}, u32[]{:S(2)}, u32[]{:S(2)}) %collective-permute-start.8) | collective-permute-done | bytes 131104 | tf_op jit(solution)/shard_map/ppermute | solution.py:341
  78.8 0.0 collective-permute-done.9.refs_7_
  78.8 0.0 copy-done.1
  78.8 0.9 shard_map.56.early_ref
  79.7 0.0 copy-start
  79.7 1.0 copy-done
  80.7 22.2 %all-to-all-done.late_ref = bf16[32,3,4,32,128]{4,3,2,1,0:T(8,128)(2,1)S(1)} async-done(((bf16[32,3,4,32,128]{4,3,2,1,0:T(8,128)(2,1)}), bf16[32,3,4,32,128]{4,3,2,1,0:T(8,128)(2,1)S(1)}, u32[]{:S(2)}, u32[]{:S(2)}) %all-to-all-start) | async-done | bytes 3145760 | tf_op jit(solution)/shard_map/all_to_all | solution.py:347
  102.9 3.4 %shard_map.58 = f32[2,16,128,128]{3,2,1,0:T(8,128)} custom-call(bf16[2,256,256]{2,1,0:T(8,128)(2,1)S(1)} %copy-done.1, bf16[32,128,128]{2,1,0:T(8,128)(2,1)} %copy-done, bf16[32,3,4,32,128]{4,3,2,1,0:T(8,128)(2,1)S(1)} %all-to-all-done.late_ref), custom_call_target="tpu_custom_call" | custom-call | flops 1 | bytes 1 | tf_op jit(solution)/shard_map/pallas_call | solution.py:311
  (8 shorter events, 0.2 us)
Async XLA Ops:
  5.9 23.5 %collective-permute-start = (bf16[8,4,32,128]{3,2,1,0:T(8,128)(2,1)}, bf16[8,4,32,128]{3,2,1,0:T(8,128)(2,1)}, u32[]{:S(2)}, u32[]{:S(2)}) collective-permute-start(bf16[8,4,32,128]{3,2,1,0:T(8,128)(2,1)} %get-tuple-element.13), channel_id=1, source_target_pairs={{0,2},{2,0},{4,6},{6,4},{1,3},{3,1},{5,7},{7,5},{8,10},{10,8},{12,... | collective-permute-start | bytes 786440 | tf_op jit(solution)/shard_map/ppermute | solution.py:338
  9.0 21.7 %collective-permute-start.1 = (bf16[8,4,32,128]{3,2,1,0:T(8,128)(2,1)}, bf16[8,4,32,128]{3,2,1,0:T(8,128)(2,1)}, u32[]{:S(2)}, u32[]{:S(2)}) collective-permute-start(bf16[8,4,32,128]{3,2,1,0:T(8,128)(2,1)} %get-tuple-element.14), channel_id=1, source_target_pairs={{0,4},{2,6},{4,0},{6,2},{1,5},{3,7},{5,1},{7,3},{8,12},{10,14},{12... | collective-permute-start | bytes 786440 | tf_op jit(solution)/shard_map/ppermute | solution.py:338
  11.6 20.0 %collective-permute-start.2 = (bf16[8,4,32,128]{3,2,1,0:T(8,128)(2,1)}, bf16[8,4,32,128]{3,2,1,0:T(8,128)(2,1)}, u32[]{:S(2)}, u32[]{:S(2)}) collective-permute-start(bf16[8,4,32,128]{3,2,1,0:T(8,128)(2,1)} %get-tuple-element.15), channel_id=1, source_target_pairs={{0,6},{2,4},{4,2},{6,0},{1,7},{3,5},{5,3},{7,1},{8,14},{10,12},{12... | collective-permute-start | bytes 786440 | tf_op jit(solution)/shard_map/ppermute | solution.py:338
  22.4 80.5 %all-to-all-start = ((bf16[32,3,4,32,128]{4,3,2,1,0:T(8,128)(2,1)}), bf16[32,3,4,32,128]{4,3,2,1,0:T(8,128)(2,1)S(1)}, u32[]{:S(2)}, u32[]{:S(2)}) async-start(bf16[32,3,4,32,128]{4,3,2,1,0:T(8,128)(2,1)} %bitcast.8), calls=%async_computation | async-start | bytes 6291456 | tf_op jit(solution)/shard_map/all_to_all | solution.py:347
  28.5 50.4 %copy-start.1 = (bf16[2,256,256]{2,1,0:T(8,128)(2,1)S(1)}, bf16[2,256,256]{2,1,0:T(8,128)(2,1)}, u32[]{:S(2)}) copy-start(bf16[2,256,256]{2,1,0:T(8,128)(2,1)} %constant.5.clone.order_ref) | copy-start | bytes 786436
  32.5 30.2 %collective-permute-start.3 = (bf16[4,4,32,128]{3,2,1,0:T(8,128)(2,1)S(1)}, bf16[4,4,32,128]{3,2,1,0:T(8,128)(2,1)S(1)}, u32[]{:S(2)}, u32[]{:S(2)}) collective-permute-start(bf16[4,4,32,128]{3,2,1,0:T(8,128)(2,1)S(1)} %pad_maximum_fusion.1), channel_id=1, source_target_pairs={{0,1},{1,0},{8,9},{9,8},{16,17},{17,16},{24,25},{25,24},{2,3},{3,2... | collective-permute-start | bytes 393224 | tf_op jit(solution)/shard_map/ppermute | solution.py:341
  34.1 28.6 %collective-permute-start.4 = (bf16[4,4,32,128]{3,2,1,0:T(8,128)(2,1)S(1)}, bf16[4,4,32,128]{3,2,1,0:T(8,128)(2,1)S(1)}, u32[]{:S(2)}, u32[]{:S(2)}) collective-permute-start(bf16[4,4,32,128]{3,2,1,0:T(8,128)(2,1)S(1)} %pad_maximum_fusion.2), channel_id=1, source_target_pairs={{0,8},{1,9},{8,0},{9,1},{16,24},{17,25},{24,16},{25,17},{2,10},{3,... | collective-permute-start | bytes 393224 | tf_op jit(solution)/shard_map/ppermute | solution.py:341
  34.2 32.2 %collective-permute-start.5 = (bf16[4,4,32,128]{3,2,1,0:T(8,128)(2,1)S(1)}, bf16[4,4,32,128]{3,2,1,0:T(8,128)(2,1)S(1)}, u32[]{:S(2)}, u32[]{:S(2)}) collective-permute-start(bf16[4,4,32,128]{3,2,1,0:T(8,128)(2,1)S(1)} %pad_maximum_fusion.3), channel_id=1, source_target_pairs={{0,9},{1,8},{8,1},{9,0},{16,25},{17,24},{24,17},{25,16},{2,11},{3,... | collective-permute-start | bytes 393224 | tf_op jit(solution)/shard_map/ppermute | solution.py:341
  35.0 31.5 %collective-permute-start.6 = (bf16[4,4,32,128]{3,2,1,0:T(8,128)(2,1)S(1)}, bf16[4,4,32,128]{3,2,1,0:T(8,128)(2,1)S(1)}, u32[]{:S(2)}, u32[]{:S(2)}) collective-permute-start(bf16[4,4,32,128]{3,2,1,0:T(8,128)(2,1)S(1)} %pad_maximum_fusion.4), channel_id=1, source_target_pairs={{0,16},{1,17},{8,24},{9,25},{16,0},{17,1},{24,8},{25,9},{2,18},{3,... | collective-permute-start | bytes 393224 | tf_op jit(solution)/shard_map/ppermute | solution.py:341
  36.6 36.7 %collective-permute-start.7 = (bf16[4,4,32,128]{3,2,1,0:T(8,128)(2,1)S(1)}, bf16[4,4,32,128]{3,2,1,0:T(8,128)(2,1)S(1)}, u32[]{:S(2)}, u32[]{:S(2)}) collective-permute-start(bf16[4,4,32,128]{3,2,1,0:T(8,128)(2,1)S(1)} %pad_maximum_fusion.5), channel_id=1, source_target_pairs={{0,17},{1,16},{8,25},{9,24},{16,1},{17,0},{24,9},{25,8},{2,19},{3,... | collective-permute-start | bytes 393224 | tf_op jit(solution)/shard_map/ppermute | solution.py:341
  62.7 16.1 %collective-permute-start.8 = (bf16[4,4,32,128]{3,2,1,0:T(8,128)(2,1)S(1)}, bf16[4,4,32,128]{3,2,1,0:T(8,128)(2,1)S(1)}, u32[]{:S(2)}, u32[]{:S(2)}) collective-permute-start(bf16[4,4,32,128]{3,2,1,0:T(8,128)(2,1)S(1)} %pad_maximum_fusion.6), channel_id=1, source_target_pairs={{0,24},{1,25},{8,16},{9,17},{16,8},{17,9},{24,0},{25,1},{2,26},{3,... | collective-permute-start | bytes 393224 | tf_op jit(solution)/shard_map/ppermute | solution.py:341
  62.7 16.1 %collective-permute-start.9 = (bf16[4,4,32,128]{3,2,1,0:T(8,128)(2,1)S(1)}, bf16[4,4,32,128]{3,2,1,0:T(8,128)(2,1)S(1)}, u32[]{:S(2)}, u32[]{:S(2)}) collective-permute-start(bf16[4,4,32,128]{3,2,1,0:T(8,128)(2,1)S(1)} %pad_maximum_fusion.7), channel_id=1, source_target_pairs={{0,25},{1,24},{8,17},{9,16},{16,9},{17,8},{24,1},{25,0},{2,27},{3,... | collective-permute-start | bytes 393224 | tf_op jit(solution)/shard_map/ppermute | solution.py:341
  79.7 1.0 copy-start

commit v9 on v8

--- a/solution.py
+++ b/solution.py
@@ -22,7 +22,7 @@
 EARLY = 1
 HEAD_FLOPS = 5 * 10**10
 GROUP = 2
-STEP = 8
+STEP = 16
 PIECES = 2
 HEAD_VMEM = 32 << 20
 TAIL_VMEM = 32 << 20

time: 107 us -> 107 us (level)
    all_to_all x1, waiting for transfers between devices: 22.2 us -> 23.4 us  [local(): lax.all_to_all(late, ('grp', 'far', 'near'), split_axis=0, concat_axis=0,...]
where the time goes in v9:
time: 107 us
  waiting for transfers between devices  63.4 us (59%)
  Pallas kernels  20.7 us (19%)
  starting transfers between devices  17.9 us (17%)
  local copies, waits for them, and re-layouts  4.62 us (4%)
    ppermute x7, waiting for transfers between devices, swap(): return lax.ppermute(x, ('grp', 'near'), [(a, a ^ r) for a in range(near)])  39.5 us
    all_to_all x1, waiting for transfers between devices, local(): lax.all_to_all(late, ('grp', 'far', 'near'), split_axis=0, concat_axis=0,...  23.4 us
    pallas_call x2, Pallas kernels, channelise(): pl.pallas_call(functools.partial(filter_kernel, radix, rows, far, first,...  16.5 us
    ppermute x7, starting transfers between devices, swap(): return lax.ppermute(x, ('grp', 'near'), [(a, a ^ r) for a in range(near)])  6.17 us
    all_to_all x1, starting transfers between devices, local(): lax.all_to_all(late, ('grp', 'far', 'near'), split_axis=0, concat_axis=0,...  6.07 us
    ppermute x3, starting transfers between devices, cross(): return lax.ppermute(x, 'far', [(a, a ^ k) for a in range(far)])  5.68 us
    slice x4, local copies, waits for them, and re-layouts, local(): crossed[k][r]  3.62 us
    pallas_call x1, Pallas kernels, correlate(): pl.pallas_call(functools.partial(gram_kernel, radix_of(ch_dev), ch_dev, r...  3.37 us
  transfers between devices with their start and end apart: 11, of which 6 were waited for; matrix products, arithmetic and copies ran while one was open for 4% of the time, Pallas kernels for 11%

profile of v9, /device:TPU:0, one launch (start us, length us, event | category | flops | bytes accessed | tf_op | source)
XLA Modules:
  0.0 107.0 jit_solution(16976813471495941760)
XLA Ops:
  0.0 5.9 %shard_map.55 = (bf16[8,4,32,128]{3,2,1,0:T(8,128)(2,1)}, bf16[8,4,32,128]{3,2,1,0:T(8,128)(2,1)}, bf16[8,4,32,128]{3,2,1,0:T(8,128)(2,1)}, bf16[8,4,32,128]{3,2,1,0:T(8,128)(2,1)}) custom-call(s32[515,32,128]{2,1,0:T(8,128)} %bitcast.6, s32[4,1024]{1,0:T(4,128)} %taps_ref.3, bf16[2,6,4,64,256]{4,3,2,1,0:T(8,128)(2,1)} %constant.4.clone.table_ref), custom_call_target="tpu_custom_call" | custom-call | flops 1 | bytes 1 | tf_op jit(solution)/shard_map/pallas_call | solution.py:193
  5.9 3.1 %collective-permute-start = (bf16[8,4,32,128]{3,2,1,0:T(8,128)(2,1)}, bf16[8,4,32,128]{3,2,1,0:T(8,128)(2,1)}, u32[]{:S(2)}, u32[]{:S(2)}) collective-permute-start(bf16[8,4,32,128]{3,2,1,0:T(8,128)(2,1)} %get-tuple-element.13), channel_id=1, source_target_pairs={{0,2},{2,0},{4,6},{6,4},{1,3},{3,1},{5,7},{7,5},{8,10},{10,8},{12,... | collective-permute-start | bytes 786440 | tf_op jit(solution)/shard_map/ppermute | solution.py:338
  9.0 2.6 %collective-permute-start.1 = (bf16[8,4,32,128]{3,2,1,0:T(8,128)(2,1)}, bf16[8,4,32,128]{3,2,1,0:T(8,128)(2,1)}, u32[]{:S(2)}, u32[]{:S(2)}) collective-permute-start(bf16[8,4,32,128]{3,2,1,0:T(8,128)(2,1)} %get-tuple-element.14), channel_id=1, source_target_pairs={{0,4},{2,6},{4,0},{6,2},{1,5},{3,7},{5,1},{7,3},{8,12},{10,14},{12... | collective-permute-start | bytes 786440 | tf_op jit(solution)/shard_map/ppermute | solution.py:338
  11.6 0.0 collective-permute-start.2
  11.6 10.6 %shard_map.57 = bf16[4,4,2,3,4,32,128]{6,5,4,3,2,1,0:T(8,128)(2,1)} custom-call(s32[515,32,128]{2,1,0:T(8,128)} %bitcast.7, s32[4,1024]{1,0:T(4,128)} %taps_ref.3, bf16[2,6,4,64,256]{4,3,2,1,0:T(8,128)(2,1)} %constant.4.clone.table_ref), custom_call_target="tpu_custom_call" | custom-call | flops 1 | bytes 1 | tf_op jit(solution)/shard_map/pallas_call | solution.py:193
  22.2 6.1 %all-to-all-start = ((bf16[32,3,4,32,128]{4,3,2,1,0:T(8,128)(2,1)}), bf16[32,3,4,32,128]{4,3,2,1,0:T(8,128)(2,1)S(1)}, u32[]{:S(2)}, u32[]{:S(2)}) async-start(bf16[32,3,4,32,128]{4,3,2,1,0:T(8,128)(2,1)} %bitcast.8), calls=%async_computation | async-start | bytes 6291456 | tf_op jit(solution)/shard_map/all_to_all | solution.py:347
  28.3 0.0 copy-start.1
  28.3 0.9 fusion
  29.2 0.0 collective-permute-done
  29.2 0.9 fusion.1
  30.1 0.5 collective-permute-done.1
  30.7 0.9 fusion.2
  31.6 0.0 collective-permute-done.2
  31.6 0.9 fusion.3
  32.5 1.6 %collective-permute-start.3 = (bf16[4,4,32,128]{3,2,1,0:T(8,128)(2,1)S(1)}, bf16[4,4,32,128]{3,2,1,0:T(8,128)(2,1)S(1)}, u32[]{:S(2)}, u32[]{:S(2)}) collective-permute-start(bf16[4,4,32,128]{3,2,1,0:T(8,128)(2,1)S(1)} %pad_maximum_fusion.1), channel_id=1, source_target_pairs={{0,1},{1,0},{8,9},{9,8},{16,17},{17,16},{24,25},{25,24},{2,3},{3,2... | collective-permute-start | bytes 393224 | tf_op jit(solution)/shard_map/ppermute | solution.py:341
  34.1 0.1 collective-permute-start.4
  34.2 0.7 collective-permute-start.5
  34.9 1.6 %collective-permute-start.6 = (bf16[4,4,32,128]{3,2,1,0:T(8,128)(2,1)S(1)}, bf16[4,4,32,128]{3,2,1,0:T(8,128)(2,1)S(1)}, u32[]{:S(2)}, u32[]{:S(2)}) collective-permute-start(bf16[4,4,32,128]{3,2,1,0:T(8,128)(2,1)S(1)} %pad_maximum_fusion.4), channel_id=1, source_target_pairs={{0,16},{1,17},{8,24},{9,25},{16,0},{17,1},{24,8},{25,9},{2,18},{3,... | collective-permute-start | bytes 393224 | tf_op jit(solution)/shard_map/ppermute | solution.py:341
  36.5 1.5 %collective-permute-start.7 = (bf16[4,4,32,128]{3,2,1,0:T(8,128)(2,1)S(1)}, bf16[4,4,32,128]{3,2,1,0:T(8,128)(2,1)S(1)}, u32[]{:S(2)}, u32[]{:S(2)}) collective-permute-start(bf16[4,4,32,128]{3,2,1,0:T(8,128)(2,1)S(1)} %pad_maximum_fusion.5), channel_id=1, source_target_pairs={{0,17},{1,16},{8,25},{9,24},{16,1},{17,0},{24,9},{25,8},{2,19},{3,... | collective-permute-start | bytes 393224 | tf_op jit(solution)/shard_map/ppermute | solution.py:341
  38.1 23.5 %collective-permute-done.3.refs_1_ = bf16[4,4,32,128]{3,2,1,0:T(8,128)(2,1)S(1)} collective-permute-done((bf16[4,4,32,128]{3,2,1,0:T(8,128)(2,1)S(1)}, bf16[4,4,32,128]{3,2,1,0:T(8,128)(2,1)S(1)}, u32[]{:S(2)}, u32[]{:S(2)}) %collective-permute-start.3) | collective-permute-done | bytes 131104 | tf_op jit(solution)/shard_map/ppermute | solution.py:341
  61.5 0.2 collective-permute-start.8
  61.8 0.0 collective-permute-done.4.refs_2_
  61.8 0.5 collective-permute-start.9
  62.3 3.2 %collective-permute-done.5.refs_3_ = bf16[4,4,32,128]{3,2,1,0:T(8,128)(2,1)S(1)} collective-permute-done((bf16[4,4,32,128]{3,2,1,0:T(8,128)(2,1)S(1)}, bf16[4,4,32,128]{3,2,1,0:T(8,128)(2,1)S(1)}, u32[]{:S(2)}, u32[]{:S(2)}) %collective-permute-start.5) | collective-permute-done | bytes 131104 | tf_op jit(solution)/shard_map/ppermute | solution.py:341
  65.5 0.0 collective-permute-done.6.refs_4_
  65.5 7.2 %collective-permute-done.7.refs_5_ = bf16[4,4,32,128]{3,2,1,0:T(8,128)(2,1)S(1)} collective-permute-done((bf16[4,4,32,128]{3,2,1,0:T(8,128)(2,1)S(1)}, bf16[4,4,32,128]{3,2,1,0:T(8,128)(2,1)S(1)}, u32[]{:S(2)}, u32[]{:S(2)}) %collective-permute-start.7) | collective-permute-done | bytes 131104 | tf_op jit(solution)/shard_map/ppermute | solution.py:341
  72.7 5.7 %collective-permute-done.8.refs_6_ = bf16[4,4,32,128]{3,2,1,0:T(8,128)(2,1)S(1)} collective-permute-done((bf16[4,4,32,128]{3,2,1,0:T(8,128)(2,1)S(1)}, bf16[4,4,32,128]{3,2,1,0:T(8,128)(2,1)S(1)}, u32[]{:S(2)}, u32[]{:S(2)}) %collective-permute-start.8) | collective-permute-done | bytes 131104 | tf_op jit(solution)/shard_map/ppermute | solution.py:341
  78.4 0.0 collective-permute-done.9.refs_7_
  78.4 0.0 copy-done.1
  78.4 0.9 shard_map.56.early_ref
  79.2 0.0 copy-start
  79.2 1.0 copy-done
  80.2 23.4 %all-to-all-done.late_ref = bf16[32,3,4,32,128]{4,3,2,1,0:T(8,128)(2,1)S(1)} async-done(((bf16[32,3,4,32,128]{4,3,2,1,0:T(8,128)(2,1)}), bf16[32,3,4,32,128]{4,3,2,1,0:T(8,128)(2,1)S(1)}, u32[]{:S(2)}, u32[]{:S(2)}) %all-to-all-start) | async-done | bytes 3145760 | tf_op jit(solution)/shard_map/all_to_all | solution.py:347
  103.6 3.4 %shard_map.58 = f32[2,16,128,128]{3,2,1,0:T(8,128)} custom-call(bf16[2,256,256]{2,1,0:T(8,128)(2,1)S(1)} %copy-done.1, bf16[32,128,128]{2,1,0:T(8,128)(2,1)} %copy-done, bf16[32,3,4,32,128]{4,3,2,1,0:T(8,128)(2,1)S(1)} %all-to-all-done.late_ref), custom_call_target="tpu_custom_call" | custom-call | flops 1 | bytes 1 | tf_op jit(solution)/shard_map/pallas_call | solution.py:311
  (8 shorter events, 0.2 us)
Async XLA Ops:
  5.9 23.3 %collective-permute-start = (bf16[8,4,32,128]{3,2,1,0:T(8,128)(2,1)}, bf16[8,4,32,128]{3,2,1,0:T(8,128)(2,1)}, u32[]{:S(2)}, u32[]{:S(2)}) collective-permute-start(bf16[8,4,32,128]{3,2,1,0:T(8,128)(2,1)} %get-tuple-element.13), channel_id=1, source_target_pairs={{0,2},{2,0},{4,6},{6,4},{1,3},{3,1},{5,7},{7,5},{8,10},{10,8},{12,... | collective-permute-start | bytes 786440 | tf_op jit(solution)/shard_map/ppermute | solution.py:338
  9.0 21.7 %collective-permute-start.1 = (bf16[8,4,32,128]{3,2,1,0:T(8,128)(2,1)}, bf16[8,4,32,128]{3,2,1,0:T(8,128)(2,1)}, u32[]{:S(2)}, u32[]{:S(2)}) collective-permute-start(bf16[8,4,32,128]{3,2,1,0:T(8,128)(2,1)} %get-tuple-element.14), channel_id=1, source_target_pairs={{0,4},{2,6},{4,0},{6,2},{1,5},{3,7},{5,1},{7,3},{8,12},{10,14},{12... | collective-permute-start | bytes 786440 | tf_op jit(solution)/shard_map/ppermute | solution.py:338
  11.6 20.0 %collective-permute-start.2 = (bf16[8,4,32,128]{3,2,1,0:T(8,128)(2,1)}, bf16[8,4,32,128]{3,2,1,0:T(8,128)(2,1)}, u32[]{:S(2)}, u32[]{:S(2)}) collective-permute-start(bf16[8,4,32,128]{3,2,1,0:T(8,128)(2,1)} %get-tuple-element.15), channel_id=1, source_target_pairs={{0,6},{2,4},{4,2},{6,0},{1,7},{3,5},{5,3},{7,1},{8,14},{10,12},{12... | collective-permute-start | bytes 786440 | tf_op jit(solution)/shard_map/ppermute | solution.py:338
  22.2 81.4 %all-to-all-start = ((bf16[32,3,4,32,128]{4,3,2,1,0:T(8,128)(2,1)}), bf16[32,3,4,32,128]{4,3,2,1,0:T(8,128)(2,1)S(1)}, u32[]{:S(2)}, u32[]{:S(2)}) async-start(bf16[32,3,4,32,128]{4,3,2,1,0:T(8,128)(2,1)} %bitcast.8), calls=%async_computation | async-start | bytes 6291456 | tf_op jit(solution)/shard_map/all_to_all | solution.py:347
  28.3 50.1 %copy-start.1 = (bf16[2,256,256]{2,1,0:T(8,128)(2,1)S(1)}, bf16[2,256,256]{2,1,0:T(8,128)(2,1)}, u32[]{:S(2)}) copy-start(bf16[2,256,256]{2,1,0:T(8,128)(2,1)} %constant.5.clone.order_ref) | copy-start | bytes 786436
  32.5 29.0 %collective-permute-start.3 = (bf16[4,4,32,128]{3,2,1,0:T(8,128)(2,1)S(1)}, bf16[4,4,32,128]{3,2,1,0:T(8,128)(2,1)S(1)}, u32[]{:S(2)}, u32[]{:S(2)}) collective-permute-start(bf16[4,4,32,128]{3,2,1,0:T(8,128)(2,1)S(1)} %pad_maximum_fusion.1), channel_id=1, source_target_pairs={{0,1},{1,0},{8,9},{9,8},{16,17},{17,16},{24,25},{25,24},{2,3},{3,2... | collective-permute-start | bytes 393224 | tf_op jit(solution)/shard_map/ppermute | solution.py:341
  34.1 27.7 %collective-permute-start.4 = (bf16[4,4,32,128]{3,2,1,0:T(8,128)(2,1)S(1)}, bf16[4,4,32,128]{3,2,1,0:T(8,128)(2,1)S(1)}, u32[]{:S(2)}, u32[]{:S(2)}) collective-permute-start(bf16[4,4,32,128]{3,2,1,0:T(8,128)(2,1)S(1)} %pad_maximum_fusion.2), channel_id=1, source_target_pairs={{0,8},{1,9},{8,0},{9,1},{16,24},{17,25},{24,16},{25,17},{2,10},{3,... | collective-permute-start | bytes 393224 | tf_op jit(solution)/shard_map/ppermute | solution.py:341
  34.2 31.3 %collective-permute-start.5 = (bf16[4,4,32,128]{3,2,1,0:T(8,128)(2,1)S(1)}, bf16[4,4,32,128]{3,2,1,0:T(8,128)(2,1)S(1)}, u32[]{:S(2)}, u32[]{:S(2)}) collective-permute-start(bf16[4,4,32,128]{3,2,1,0:T(8,128)(2,1)S(1)} %pad_maximum_fusion.3), channel_id=1, source_target_pairs={{0,9},{1,8},{8,1},{9,0},{16,25},{17,24},{24,17},{25,16},{2,11},{3,... | collective-permute-start | bytes 393224 | tf_op jit(solution)/shard_map/ppermute | solution.py:341
  34.9 30.6 %collective-permute-start.6 = (bf16[4,4,32,128]{3,2,1,0:T(8,128)(2,1)S(1)}, bf16[4,4,32,128]{3,2,1,0:T(8,128)(2,1)S(1)}, u32[]{:S(2)}, u32[]{:S(2)}) collective-permute-start(bf16[4,4,32,128]{3,2,1,0:T(8,128)(2,1)S(1)} %pad_maximum_fusion.4), channel_id=1, source_target_pairs={{0,16},{1,17},{8,24},{9,25},{16,0},{17,1},{24,8},{25,9},{2,18},{3,... | collective-permute-start | bytes 393224 | tf_op jit(solution)/shard_map/ppermute | solution.py:341
  36.5 36.1 %collective-permute-start.7 = (bf16[4,4,32,128]{3,2,1,0:T(8,128)(2,1)S(1)}, bf16[4,4,32,128]{3,2,1,0:T(8,128)(2,1)S(1)}, u32[]{:S(2)}, u32[]{:S(2)}) collective-permute-start(bf16[4,4,32,128]{3,2,1,0:T(8,128)(2,1)S(1)} %pad_maximum_fusion.5), channel_id=1, source_target_pairs={{0,17},{1,16},{8,25},{9,24},{16,1},{17,0},{24,9},{25,8},{2,19},{3,... | collective-permute-start | bytes 393224 | tf_op jit(solution)/shard_map/ppermute | solution.py:341
  61.5 16.8 %collective-permute-start.8 = (bf16[4,4,32,128]{3,2,1,0:T(8,128)(2,1)S(1)}, bf16[4,4,32,128]{3,2,1,0:T(8,128)(2,1)S(1)}, u32[]{:S(2)}, u32[]{:S(2)}) collective-permute-start(bf16[4,4,32,128]{3,2,1,0:T(8,128)(2,1)S(1)} %pad_maximum_fusion.6), channel_id=1, source_target_pairs={{0,24},{1,25},{8,16},{9,17},{16,8},{17,9},{24,0},{25,1},{2,26},{3,... | collective-permute-start | bytes 393224 | tf_op jit(solution)/shard_map/ppermute | solution.py:341
  61.8 16.6 %collective-permute-start.9 = (bf16[4,4,32,128]{3,2,1,0:T(8,128)(2,1)S(1)}, bf16[4,4,32,128]{3,2,1,0:T(8,128)(2,1)S(1)}, u32[]{:S(2)}, u32[]{:S(2)}) collective-permute-start(bf16[4,4,32,128]{3,2,1,0:T(8,128)(2,1)S(1)} %pad_maximum_fusion.7), channel_id=1, source_target_pairs={{0,25},{1,24},{8,17},{9,16},{16,9},{17,8},{24,1},{25,0},{2,27},{3,... | collective-permute-start | bytes 393224 | tf_op jit(solution)/shard_map/ppermute | solution.py:341
  79.2 1.0 copy-start
